TPU v7x, 128 devices: a whole 4x4x4 slice. The times are simulated.
128 devices in a mesh: gx: 16 (over z, y), gy: 8 (over x, core).
Axes of the slice: x: 4, y: 4, z: 4, core: 2. Of those that a mesh axis runs over, the one named last changes fastest.
Arguments:
- thermal_grid: float32 [64, 128, 128], P('gx', 'gy'), may hold values from -6 to 6
- average_blend_fraction: float32 [64, 128, 128], P('gx', 'gy'), may hold values from 0.05 to 0.95
- normalized_blend_variance: float32 [64, 128, 128], P('gx', 'gy'), may hold values from 0.002 to 0.5
- small_volume_mass: float32 [64, 128, 128], P('gx', 'gy'), may hold values from 0.01 to 0.1
- bare_scalar_decay: float32 [64, 128, 128], P('gx', 'gy'), may hold values from 0.05 to 1
- parent_block: int32 [64, 128, 128], P('gx', 'gy'), may hold values from 0 to 511, as said below
- species_given_block: float32 [512, 16, 128], P(('gx', 'gy')), may hold values from -6 to 6
- block_position: int32 [512], replicated, may hold values from 0 to 511, each once
- face_partners: int32 [512, 6], replicated, may hold values from 0 to 511, as said below
- reaction_increments: int32 [512], replicated, may hold values from 0 to 15, as said below
- chemical_coupling: float32 [16, 16], replicated, may hold values from -1.5 to 1.5
- species_thermal_weight: float32 [16], replicated, may hold values from -1.5 to 1.5
Outputs:
- species_next: float32 [512, 16, 128], P(('gx', 'gy'))
- temperature_next: float32 [64, 128, 128], P('gx', 'gy')
Inputs may be any that keep to these rules, and one draw needn't show every extreme that they name: `parent_block`: each fine cell names the coarse cell under it after a shift of at most 2 fine cells along each dimension; every coarse cell is named. `face_partners`: A cell on the grid's border names itself in place of a missing neighbour; every coarse cell is named. `reaction_increments`: both ends are reached in every draw.
All inputs are finite; a program needn't handle non-finite values.
Results may differ from a plain program's by a relative error of at most 0.0003.
Values sent between devices are 32-bit elements; how exact they have to be, the bound alone decides.
No kernel may reach another device: no remote copies, remote signals or barrier semaphores. Data moves between devices by JAX's collectives and lax.ppermute only.
A program may use at most 128 MiB of HBM per device.

v0:
```python
import math

import jax
import jax.numpy as jnp
from jax import lax
from jax.sharding import Mesh
from jax.sharding import PartitionSpec as P

ETA = 128
STEPS = 2
GX_GY = ("gx_0", "gx_1", "gy_0", "gy_1")
GX = ("gx_0", "gx_1")
GY = ("gy_0", "gy_1")


coupling = 0.05
mixing_rate = 0.2
react_rate = 0.5
prior_weight = 1.0
prior_flux = 0.5
thermal_diffusion = 0.1
damping_contribution = 0.3


def extended(array, sides, width):
    edges = {}
    for axis, dim in sides:
        peers, length = (lax.axis_size(axis), array.shape[dim])
        up = [(i, (i + 1) % peers) for i in range(peers - 1)]
        last = lax.slice_in_dim(array, length - width, length, axis=dim)
        first = lax.slice_in_dim(array, 0, width, axis=dim)
        edges[dim] = (
            lax.ppermute(last, axis, up),
            lax.ppermute(first, axis, [(b, a) for a, b in up]),
        )
    done = []
    for _, dim in sides:
        low, high = edges[dim]
        around = [(width, width) if d in done else (0, 0) for d in range(array.ndim)]
        array = jnp.concatenate([jnp.pad(low, around), array, jnp.pad(high, around)], axis=dim)
        done.append(dim)
    return array


def in_blocks(array, dim, peers):
    shape = array.shape
    parts = array.reshape(*shape[:dim], peers, shape[dim] // peers, *shape[dim + 1 :])
    return jnp.moveaxis(parts, dim, 0)


def sent_and_summed(array, axis, dim):
    peers = lax.axis_size(axis)
    parts = lax.all_to_all(in_blocks(array, dim, peers), axis, 0, 0, tiled=True)
    return jnp.sum(parts, axis=0)


def sum_in_two_steps(array, axes, dim):
    far, near = axes
    own = sent_and_summed(in_blocks(array, dim, lax.axis_size(far)), near, dim + 1)
    return jnp.sum(lax.all_to_all(own, far, 0, 0, tiled=True), axis=0)


def copy_for_each(array, axis):
    copies = jnp.broadcast_to(array, (lax.axis_size(axis), *array.shape))
    return lax.all_to_all(copies, axis, split_axis=0, concat_axis=0, tiled=True)


def laid_out(parts, dim):
    shape = list(parts.shape[1:])
    shape[dim] *= parts.shape[0]
    return jnp.moveaxis(parts, 0, dim).reshape(shape)


def gathered_by_axis(array, axes, dim):
    far, near = axes
    first = copy_for_each(array, far)
    parts = jnp.swapaxes(copy_for_each(first, near), 0, 1)
    return laid_out(parts.reshape(-1, *array.shape), dim)


def beta_table(average_blend_fraction, normalized_blend_variance):
    points = (jnp.arange(ETA, dtype=jnp.float32) + 0.5) / ETA
    shape_sum = 1.0 / normalized_blend_variance - 1.0
    alpha = average_blend_fraction * shape_sum
    beta_b = (1.0 - average_blend_fraction) * shape_sum
    logits = (alpha - 1.0)[..., None] * jnp.log(points) + (beta_b - 1.0)[..., None] * jnp.log(
        1.0 - points
    )
    return jax.nn.softmax(logits, axis=-1)


def lap_mixture(field):
    bordered_grid = jnp.concatenate([field[..., :1], field, field[..., -1:]], axis=-1)
    return bordered_grid[..., 2:] - 2.0 * field + bordered_grid[..., :-2]


def coarse_advance(fluid_condition, nearby, scalar_decay_speed, counts, chemical_coupling, turns):
    fluid_condition = fluid_condition + coupling * jnp.sum(
        nearby - fluid_condition[:, None], axis=1
    )
    fraction = 1.0 / counts.astype(jnp.float32)

    def substep(index, current):
        source = jnp.einsum(
            "st,ctk->csk", chemical_coupling, jnp.tanh(current), precision=lax.Precision.HIGHEST
        )
        update = fraction[:, None, None] * (
            mixing_rate * scalar_decay_speed[:, None, :] * lap_mixture(current)
            + react_rate * source
        )
        return jnp.where((index < counts)[:, None, None], current + update, current)

    return lax.fori_loop(0, turns, substep, fluid_condition)


def cell_blocks(cells):
    width = math.gcd(cells, 512)
    return (cells // width, width)


def small_volume_accumulations(
    tabulated_values,
    small_volume_mass,
    bare_scalar_decay,
    thermal_grid,
    parent_block,
    block_numbers,
):
    points = tabulated_values.shape[-1]
    cells = parent_block.size
    nblocks, width = cell_blocks(cells)
    flat_table = tabulated_values.reshape(nblocks, width, points)
    flat_mass = small_volume_mass.reshape(nblocks, width, 1)
    flat_speed = (bare_scalar_decay * (1.0 + 0.5 * jnp.tanh(thermal_grid))).reshape(
        nblocks, width, 1
    )
    flat_parent = parent_block.reshape(nblocks, width)
    labels = jnp.arange(block_numbers, dtype=jnp.int32)

    def attach_block(total, pieces):
        table_piece, mass_piece, speed_piece, parent_piece = pieces
        weighted = mass_piece * table_piece
        values = jnp.concatenate([weighted, weighted * speed_piece], axis=-1)
        selector = (parent_piece[:, None] == labels[None, :]).astype(jnp.float32)
        added = lax.dot_general(
            selector,
            values,
            (((0,), (0,)), ((), ())),
            precision=lax.Precision.HIGHEST,
            preferred_element_type=jnp.float32,
        )
        return (total + added, None)

    start_total = jnp.zeros((block_numbers, 2 * points), jnp.float32)
    total, unused = lax.scan(
        attach_block, start_total, (flat_table, flat_mass, flat_speed, flat_parent)
    )
    return total.reshape(block_numbers, 2, points)


def coarse_to_fine(tabulated_values, blend_block_number, parent_block):
    points = tabulated_values.shape[-1]
    block_numbers = blend_block_number.shape[0]
    cells = parent_block.size
    nblocks, width = cell_blocks(cells)
    flat_table = tabulated_values.reshape(nblocks, width, points)
    flat_parent = parent_block.reshape(nblocks, width)
    labels = jnp.arange(block_numbers, dtype=jnp.int32)

    def one_block(pieces):
        table_piece, parent_piece = pieces
        selector = (parent_piece[:, None] == labels[None, :]).astype(jnp.float32)
        picked = jnp.dot(
            selector,
            blend_block_number,
            precision=lax.Precision.HIGHEST,
            preferred_element_type=jnp.float32,
        )
        return jnp.sum(table_piece * picked, axis=-1)

    return lax.map(one_block, (flat_table, flat_parent)).reshape(parent_block.shape)


def advance_small_fluid(thermal_grid, tabulated_values, blend_block_number, parent_block):
    bordered_grid = extended(thermal_grid, ((GX, 0), (GY, 1)), 1)
    small_grid_thermal = coarse_to_fine(tabulated_values, blend_block_number, parent_block)
    bordered_grid = jnp.pad(bordered_grid, ((0, 0), (0, 0), (1, 1)))
    nearby_blocks = bordered_grid[2:, 1:-1, 1:-1] + bordered_grid[:-2, 1:-1, 1:-1]
    nearby_blocks = nearby_blocks + bordered_grid[1:-1, 2:, 1:-1] + bordered_grid[1:-1, :-2, 1:-1]
    nearby_blocks = nearby_blocks + bordered_grid[1:-1, 1:-1, 2:] + bordered_grid[1:-1, 1:-1, :-2]
    return (
        thermal_grid
        + thermal_diffusion * (nearby_blocks - 6.0 * thermal_grid)
        + damping_contribution * (small_grid_thermal - thermal_grid)
    )


def shards(
    thermal_grid,
    average_blend_fraction,
    normalized_blend_variance,
    small_volume_mass,
    bare_scalar_decay,
    parent_block,
    species_given_block,
    block_position,
    face_partners,
    reaction_increments,
    chemical_coupling,
    species_thermal_weight,
):
    block_numbers = block_position.shape[0]
    owned = species_given_block.shape[0]
    device_index = lax.axis_index(GX) * lax.axis_size(GY) + lax.axis_index(GY)
    position_block_map = jnp.argsort(block_position)
    near_slot = block_position[face_partners[position_block_map]]
    counts = reaction_increments[position_block_map] + 1
    tabulated_values = beta_table(average_blend_fraction, normalized_blend_variance)
    local_condition = species_given_block
    near_own = lax.dynamic_slice_in_dim(near_slot, device_index * owned, owned, 0)
    counts_own = lax.dynamic_slice_in_dim(counts, device_index * owned, owned, 0)
    for turn in range(STEPS):
        local_aggregates = small_volume_accumulations(
            tabulated_values,
            small_volume_mass,
            bare_scalar_decay,
            thermal_grid,
            parent_block,
            block_numbers,
        )
        own_sums = sum_in_two_steps(
            local_aggregates[position_block_map], (("gx_0", "gx_1", "gy_0"), "gy_1"), 0
        )
        cchi_own = (own_sums[:, 1] + prior_flux) / (own_sums[:, 0] + prior_weight)
        state_all = lax.all_gather(local_condition, GX_GY, axis=0, tiled=True)
        local_condition = coarse_advance(
            local_condition,
            state_all[near_own],
            cchi_own,
            counts_own,
            chemical_coupling,
            jnp.max(counts_own),
        )
        theta_own = jnp.einsum(
            "s,csk->ck", species_thermal_weight, local_condition, precision=lax.Precision.HIGHEST
        )
        blend_position = gathered_by_axis(theta_own, (("gx_0", "gx_1", "gy_0"), "gy_1"), 0)
        thermal_grid = advance_small_fluid(
            thermal_grid, tabulated_values, blend_position[block_position], parent_block
        )
    return (local_condition, thermal_grid)


def solution(mesh):
    torus = Mesh(mesh.devices.reshape(4, 4, 4, 2), ("gx_0", "gx_1", "gy_0", "gy_1"))
    placed = (
        P(GX, GY, None),
        P(GX, GY, None),
        P(GX, GY, None),
        P(GX, GY, None),
        P(GX, GY, None),
        P(GX, GY, None),
        P(GX_GY, None, None),
        P(),
        P(),
        P(),
        P(),
        P(),
    )
    return jax.shard_map(
        shards,
        mesh=torus,
        in_specs=placed,
        out_specs=(P(GX_GY, None, None), P(GX, GY, None)),
        check_vma=False,
    )
```

profile of v0, /device:TPU:1, one launch (start us, length us, event | category | flops | bytes accessed | tf_op | source)
XLA Modules:
  0.0 365.9 jit_solution(11819357955965170304)
XLA Ops:
  8.6 4.0 %collective-permute-start.1 = (f32[1,16,128]{2,1,0:T(8,128)S(1)}, f32[1,16,128]{2,1,0:T(8,128)S(1)}, u32[]{:S(2)}, u32[]{:S(2)}) collective-permute-start(f32[1,16,128]{2,1,0:T(8,128)S(1)} %get-tuple-element.545), channel_id=1, source_target_pairs={{0,8},{8,16},{16,24},{24,32},{32,40},{40,48},{48,56},{56,64},{64,7... | collective-permute-start | bytes 24584 | tf_op jit(solution)/shard_map/ppermute | solution.py:33
  13.4 2.9 collective-permute-start.2
  17.6 3.0 collective-permute-start.3
  21.4 3.8 %fusion.42 = f32[4,16,128]{2,1,0:T(8,128)S(1)} fusion(f32[128]{0:T(128)S(1)} %get-tuple-element.550, f32[4,16,128]{2,1,0:T(8,128)S(1)} %get-tuple-element.537, f32[128]{0:T(128)S(1)} %get-tuple-element.551, f32[4,16,128]{2,1,0:T(8,128)S(1)} %get-tuple-element.536), kind=kLoop, calls=%fused_computation.80 | loop fusion | flops 4186112 | bytes 99328 | tf_op jit(solution)/shard_map/reduce_max | solution.py:89
  25.2 5.2 %exponential_reduce_fusion = f32[4,16,128]{2,1,0:T(8,128)S(1)} fusion(f32[4,16,128]{2,1,0:T(8,128)S(1)} %fusion.42, f32[128]{0:T(128)S(1)} %get-tuple-element.550, f32[4,16,128]{2,1,0:T(8,128)S(1)} %get-tuple-element.537, f32[128]{0:T(128)S(1)} %get-tuple-element.551, f32[4,16,128]{2,1,0:T(8,128)S(1)} %get-tuple-element.536), kind=kLoop, calls=%fused_computation.77 | loop fusion | flops 5234688 | bytes 132096 | tf_op jit(solution)/shard_map/reduce_sum | solution.py:89
  32.0 4.4 %sort.17 = (s32[512]{0:T(512)}, s32[512]{0:T(512)S(1)}) sort(s32[512]{0:T(512)} %param.31, s32[512]{0:T(512)S(1)} %iota.29), dimensions={0}, to_apply=%region_0.0 | sort | flops 4608 | bytes 8192 | tf_op jit(solution)/shard_map/jit(argsort)/sort | solution.py:215
  37.7 3.5 gather_fusion.3
  41.3 6.4 %exponential_divide_fusion = f32[16,512,128]{2,1,0:T(8,128)} fusion(f32[16,512]{1,0:T(8,128)S(1)} %div.46, f32[16,512]{1,0:T(8,128)S(1)} %sub.81, f32[128]{0:T(128)S(1)} %get-tuple-element.550, f32[16,512]{1,0:T(8,128)S(1)} %mul.222, f32[128]{0:T(128)S(1)} %get-tuple-element.551, f32[16,512]{1,0:T(8,128)S(1)} %mul.217), kind=kLoop, calls=%fused_computation.78 | loop fusion | flops 5242880 | bytes 4326400 | tf_op jit(solution)/shard_map/div | solution.py:89
  47.7 19.6 %gather_fusion.1 = s32[3072]{0:T(1024)S(1)} fusion(s32[512]{0:T(512)S(1)} %copy-done.1, s32[3072]{0:T(1024)S(1)} %broadcast_clamp_fusion), kind=kCustom, calls=%fused_computation.1 | custom fusion | bytes 36864 | tf_op jit(solution)/shard_map/gather | solution.py:216
  67.7 49.6 %while.68 = (s32[]{:T(128)}, f32[512,256]{1,0:T(8,128)S(1)}, s32[16,512]{1,0:T(8,128)S(1)}, f32[16,512,1]{1,2,0:T(1,128)}, f32[16,512,128]{2,1,0:T(8,128)}, /*index=5*/f32[16,512,1]{1,2,0:T(1,128)S(1)}, s32[]{:T(128)}, s32[]{:T(128)}) while((s32[]{:T(128)}, f32[512,256]{1,0:T(8,128)S(1)}, s32[16,512]{1,0:T(8,128)S(1)}, ...), condition=%wide.region_6.7_spmd.clone, body=%wide.region_5.6_spmd.clone.sunk | while | flops 806092800 | bytes 2377843 | solution.py:155
  117.6 2.1 gather_fusion.4
  120.1 3.8 %all_to_all.40 = f32[2,64,4,2,128]{4,3,2,1,0:T(2,128)S(1)} all-to-all(f32[2,64,4,2,128]{4,3,2,1,0:T(2,128)S(1)} %copy.65), channel_id=1, replica_groups=mesh['gx_0'=4,'gx_1'=4,'gy_0'=4,'gy_1'=2] {'gy_1'}, dimensions={0} | all-to-all | bytes 1048576 | tf_op jit(solution)/shard_map/all_to_all | solution.py:53
  125.1 11.8 %all-to-all-start.1 = ((f32[64,4,2,128]{3,2,1,0:T(2,128)}), f32[64,4,2,128]{3,2,1,0:T(2,128)S(1)}, u32[]{:S(2)}, u32[]{:S(2)}) async-start(f32[64,4,2,128]{3,2,1,0:T(2,128)} %reduce_sum.83), calls=%async_computation.1 | async-start | bytes 524288 | tf_op jit(solution)/shard_map/all_to_all | solution.py:60
  137.1 5.4 %copy.68 = f32[16,512,128]{1,2,0:T(8,128)} copy(f32[16,512,128]{2,1,0:T(8,128)} %get-tuple-element.940) | data formatting | bytes 8388608
  143.2 3.7 %all-to-all-done.1 = f32[64,4,2,128]{3,2,1,0:T(2,128)S(1)} async-done(((f32[64,4,2,128]{3,2,1,0:T(2,128)}), f32[64,4,2,128]{3,2,1,0:T(2,128)S(1)}, u32[]{:S(2)}, u32[]{:S(2)}) %all-to-all-start.1) | async-done | bytes 262176 | tf_op jit(solution)/shard_map/all_to_all | solution.py:60
  147.1 2.7 gather_fusion.2
  149.9 7.0 %while.64 = (s32[]{:T(128)}, f32[4,16,128]{2,1,0:T(8,128)S(1)}, s32[]{:T(128)}, s32[4]{0:T(128)S(1)}, f32[4]{0:T(128)S(1)}, /*index=5*/f32[4,128]{1,0:T(4,128)S(1)}, f32[16,16]{1,0:T(8,128)S(1)}, s32[]{:T(128)}) while((s32[]{:T(128)}, f32[4,16,128]{2,1,0:T(8,128)S(1)}, s32[]{:T(128)}, s32[4]{0:T(128)S(1)}, f32[4]{0:T(128)S(1)}, ...), condition=%wide.region_10.11_spmd, body=%wide.region_9.10_spmd.sunk | while | flops 1663494 | bytes 139913 | solution.py:113
  157.8 11.9 %all-to-all-start.2 = ((f32[64,4,128]{2,1,0:T(4,128)}), f32[64,4,128]{2,1,0:T(4,128)S(1)}, u32[]{:S(2)}, u32[]{:S(2)}) async-start(f32[64,4,128]{2,1,0:T(4,128)} %broadcast_in_dim.45), calls=%async_computation.2 | async-start | bytes 262144 | tf_op jit(solution)/shard_map/all_to_all | solution.py:65
  170.4 8.0 %all-to-all-done.2 = f32[64,4,128]{2,1,0:T(4,128)S(1)} async-done(((f32[64,4,128]{2,1,0:T(4,128)}), f32[64,4,128]{2,1,0:T(4,128)S(1)}, u32[]{:S(2)}, u32[]{:S(2)}) %all-to-all-start.2) | async-done | bytes 131104 | tf_op jit(solution)/shard_map/all_to_all | solution.py:65
  178.5 6.7 %all_to_all.41 = f32[2,64,4,128]{3,2,1,0:T(4,128)S(1)} all-to-all(f32[2,64,4,128]{3,2,1,0:T(4,128)S(1)} %broadcast_in_dim.46), channel_id=1, replica_groups=mesh['gx_0'=4,'gx_1'=4,'gy_0'=4,'gy_1'=2] {'gy_1'}, dimensions={0} | all-to-all | bytes 524288 | tf_op jit(solution)/shard_map/all_to_all | solution.py:65
  186.3 30.0 %while.66 = (s32[]{:T(128)}, f32[16,512]{1,0:T(8,128)S(1)}, f32[16,512,128]{1,2,0:T(8,128)}, s32[16,512]{1,0:T(8,128)S(1)}, f32[512,128]{1,0:T(8,128)S(1)}, /*index=5*/s32[]{:T(128)}, s32[]{:T(128)}) while((s32[]{:T(128)}, f32[16,512]{1,0:T(8,128)S(1)}, f32[16,512,128]{1,2,0:T(8,128)}, s32[16,512]{1,0:T(8,128)S(1)}, ...), condition=%wide.region_14.15_spmd.clone, body=%wide.region_12.14_spmd.clone.sunk | while | flops 403045888 | bytes 536673 | solution.py:181
  186.4 1.8 fusion.99
  188.2 1.8 fusion.99
  190.1 1.8 fusion.99
  193.8 1.8 fusion.99
  197.6 1.8 fusion.99
  201.3 1.8 fusion.99
  205.1 1.8 fusion.99
  206.9 1.8 fusion.99
  208.8 1.8 fusion.99
  210.7 1.8 fusion.99
  212.6 1.8 fusion.99
  214.5 1.8 fusion.99
  216.4 49.6 %while.69 = (s32[]{:T(128)}, f32[512,256]{1,0:T(8,128)S(1)}, s32[16,512]{1,0:T(8,128)S(1)}, f32[16,512,1]{1,2,0:T(1,128)}, f32[16,512,128]{2,1,0:T(8,128)}, /*index=5*/f32[16,512,1]{1,2,0:T(1,128)S(1)}, s32[]{:T(128)}, s32[]{:T(128)}) while((s32[]{:T(128)}, f32[512,256]{1,0:T(8,128)S(1)}, s32[16,512]{1,0:T(8,128)S(1)}, ...), condition=%wide.region_16.17_spmd.clone, body=%wide.region_15.16_spmd.clone.sunk | while | flops 806092800 | bytes 2377843 | solution.py:155
  266.3 2.1 gather_fusion.7
  268.9 4.1 %all_to_all.42 = f32[2,64,4,2,128]{4,3,2,1,0:T(2,128)S(1)} all-to-all(f32[2,64,4,2,128]{4,3,2,1,0:T(2,128)S(1)} %copy.71), channel_id=1, replica_groups=mesh['gx_0'=4,'gx_1'=4,'gy_0'=4,'gy_1'=2] {'gy_1'}, dimensions={0} | all-to-all | bytes 1048576 | tf_op jit(solution)/shard_map/all_to_all | solution.py:53
  274.1 4.6 %all-to-all-start.5 = ((f32[64,4,2,128]{3,2,1,0:T(2,128)}), f32[64,4,2,128]{3,2,1,0:T(2,128)S(1)}, u32[]{:S(2)}, u32[]{:S(2)}) async-start(f32[64,4,2,128]{3,2,1,0:T(2,128)} %reduce_sum.86), calls=%async_computation.5 | async-start | bytes 524288 | tf_op jit(solution)/shard_map/all_to_all | solution.py:60
  280.0 4.0 %collective-permute-start.5 = (f32[1,16,128]{2,1,0:T(8,128)S(1)}, f32[1,16,128]{2,1,0:T(8,128)S(1)}, u32[]{:S(2)}, u32[]{:S(2)}) collective-permute-start(f32[1,16,128]{2,1,0:T(8,128)S(1)} %get-tuple-element.538), channel_id=1, source_target_pairs={{0,8},{8,16},{16,24},{24,32},{32,40},{40,48},{48,56},{56,64},{64,7... | collective-permute-start | bytes 24584 | tf_op jit(solution)/shard_map/ppermute | solution.py:33
  284.0 4.7 %all-to-all-done.5 = f32[64,4,2,128]{3,2,1,0:T(2,128)S(1)} async-done(((f32[64,4,2,128]{3,2,1,0:T(2,128)}), f32[64,4,2,128]{3,2,1,0:T(2,128)S(1)}, u32[]{:S(2)}, u32[]{:S(2)}) %all-to-all-start.5) | async-done | bytes 262176 | tf_op jit(solution)/shard_map/all_to_all | solution.py:60
  288.9 2.7 gather_fusion.5
  291.7 7.0 %while.65 = (s32[]{:T(128)}, f32[4,16,128]{2,1,0:T(8,128)S(1)}, s32[]{:T(128)}, s32[4]{0:T(128)S(1)}, f32[4]{0:T(128)S(1)}, /*index=5*/f32[4,128]{1,0:T(4,128)S(1)}, f32[16,16]{1,0:T(8,128)S(1)}, s32[]{:T(128)}) while((s32[]{:T(128)}, f32[4,16,128]{2,1,0:T(8,128)S(1)}, s32[]{:T(128)}, s32[4]{0:T(128)S(1)}, f32[4]{0:T(128)S(1)}, ...), condition=%wide.region_20.21_spmd, body=%wide.region_19.20_spmd.sunk | while | flops 1663494 | bytes 139913 | solution.py:113
  299.6 12.1 %all-to-all-start.6 = ((f32[64,4,128]{2,1,0:T(4,128)}), f32[64,4,128]{2,1,0:T(4,128)S(1)}, u32[]{:S(2)}, u32[]{:S(2)}) async-start(f32[64,4,128]{2,1,0:T(4,128)} %broadcast_in_dim.51), calls=%async_computation.6 | async-start | bytes 262144 | tf_op jit(solution)/shard_map/all_to_all | solution.py:65
  311.8 3.9 %collective-permute-start.6 = (f32[4,1,128]{2,1,0:T(1,128)S(1)}, f32[4,1,128]{2,1,0:T(1,128)S(1)}, u32[]{:S(2)}, u32[]{:S(2)}) collective-permute-start(f32[4,1,128]{2,1,0:T(1,128)S(1)} %get-tuple-element.541), channel_id=1, source_target_pairs={{1,0},{2,1},{3,2},{4,3},{5,4},{6,5},{7,6},{9,8},{10,9},{11,10},{12... | collective-permute-start | bytes 6152 | tf_op jit(solution)/shard_map/ppermute | solution.py:34
  315.7 3.1 collective-permute-start.7
  320.6 6.7 %all_to_all.43 = f32[2,64,4,128]{3,2,1,0:T(4,128)S(1)} all-to-all(f32[2,64,4,128]{3,2,1,0:T(4,128)S(1)} %broadcast_in_dim.52), channel_id=1, replica_groups=mesh['gx_0'=4,'gx_1'=4,'gy_0'=4,'gy_1'=2] {'gy_1'}, dimensions={0} | all-to-all | bytes 524288 | tf_op jit(solution)/shard_map/all_to_all | solution.py:65
  328.4 29.9 %while.67 = (s32[]{:T(128)}, f32[16,512]{1,0:T(8,128)S(1)}, f32[16,512,128]{1,2,0:T(8,128)}, s32[16,512]{1,0:T(8,128)S(1)}, f32[512,128]{1,0:T(8,128)S(1)}, /*index=5*/s32[]{:T(128)}, s32[]{:T(128)}) while((s32[]{:T(128)}, f32[16,512]{1,0:T(8,128)S(1)}, f32[16,512,128]{1,2,0:T(8,128)}, s32[16,512]{1,0:T(8,128)S(1)}, ...), condition=%wide.region_23.24_spmd.clone, body=%wide.region_21.23_spmd.clone.sunk | while | flops 403045888 | bytes 536673 | solution.py:181
  328.4 1.8 fusion.101
  332.2 1.8 fusion.101
  (389 shorter events, 156.4 us)
Async XLA Ops:
  7.2 30.6 %copy-start = (s32[512]{0:T(512)S(1)}, s32[512]{0:T(512)}, u32[]{:S(2)}) copy-start(s32[512]{0:T(512)} %param.33) | copy-start | bytes 6148
  7.2 139.9 %all-gather.3.cloned.1.call-start = ((), (), s32[]{:S(2)}) async-start(), calls=%async_computation.8 | async-start | bytes 4227072 | tf_op jit(solution)/shard_map/all_gather | solution.py:235
  8.6 59.0 %collective-permute-start.1 = (f32[1,16,128]{2,1,0:T(8,128)S(1)}, f32[1,16,128]{2,1,0:T(8,128)S(1)}, u32[]{:S(2)}, u32[]{:S(2)}) collective-permute-start(f32[1,16,128]{2,1,0:T(8,128)S(1)} %get-tuple-element.545), channel_id=1, source_target_pairs={{0,8},{8,16},{16,24},{24,32},{32,40},{40,48},{48,56},{56,64},{64,7... | collective-permute-start | bytes 24584 | tf_op jit(solution)/shard_map/ppermute | solution.py:33
  13.4 129.8 %collective-permute-start.2 = (f32[4,1,128]{2,1,0:T(1,128)S(1)}, f32[4,1,128]{2,1,0:T(1,128)S(1)}, u32[]{:S(2)}, u32[]{:S(2)}) collective-permute-start(f32[4,1,128]{2,1,0:T(1,128)S(1)} %get-tuple-element.543), channel_id=1, source_target_pairs={{1,0},{2,1},{3,2},{4,3},{5,4},{6,5},{7,6},{9,8},{10,9},{11,10},{12... | collective-permute-start | bytes 6152 | tf_op jit(solution)/shard_map/ppermute | solution.py:34
  16.2 153.5 %collective-permute-start = (f32[1,16,128]{2,1,0:T(8,128)S(1)}, f32[1,16,128]{2,1,0:T(8,128)S(1)}, u32[]{:S(2)}, u32[]{:S(2)}) collective-permute-start(f32[1,16,128]{2,1,0:T(8,128)S(1)} %get-tuple-element.544), channel_id=1, source_target_pairs={{8,0},{16,8},{24,16},{32,24},{40,32},{48,40},{56,48},{64,56},{72,6... | collective-permute-start | bytes 24584 | tf_op jit(solution)/shard_map/ppermute | solution.py:34
  17.6 125.7 %collective-permute-start.3 = (f32[4,1,128]{2,1,0:T(1,128)S(1)}, f32[4,1,128]{2,1,0:T(1,128)S(1)}, u32[]{:S(2)}, u32[]{:S(2)}) collective-permute-start(f32[4,1,128]{2,1,0:T(1,128)S(1)} %get-tuple-element.542), channel_id=1, source_target_pairs={{0,1},{1,2},{2,3},{3,4},{4,5},{5,6},{6,7},{8,9},{9,10},{10,11},{11... | collective-permute-start | bytes 6152 | tf_op jit(solution)/shard_map/ppermute | solution.py:33
  37.5 10.2 %copy-start.1 = (s32[512]{0:T(512)S(1)}, s32[512]{0:T(512)}, u32[]{:S(2)}) copy-start(s32[512]{0:T(512)} %param.31) | copy-start | bytes 6148
  47.7 19.9 %copy-start.9 = (s32[4,16,128]{2,1,0:T(8,128)S(1)}, s32[4,16,128]{2,1,0:T(8,128)}, u32[]{:S(2)}) copy-start(s32[4,16,128]{2,1,0:T(8,128)} %param.29) | copy-start | bytes 98308
  47.7 19.9 %copy-start.7 = (f32[4,16,128]{2,1,0:T(8,128)S(1)}, f32[4,16,128]{2,1,0:T(8,128)}, u32[]{:S(2)}) copy-start(f32[4,16,128]{2,1,0:T(8,128)} %param.24) | copy-start | bytes 98308
  47.7 19.9 %copy-start.8 = (f32[4,16,128]{2,1,0:T(8,128)S(1)}, f32[4,16,128]{2,1,0:T(8,128)}, u32[]{:S(2)}) copy-start(f32[4,16,128]{2,1,0:T(8,128)} %param.28) | copy-start | bytes 98308
  125.1 21.8 %all-to-all-start.1 = ((f32[64,4,2,128]{3,2,1,0:T(2,128)}), f32[64,4,2,128]{3,2,1,0:T(2,128)S(1)}, u32[]{:S(2)}, u32[]{:S(2)}) async-start(f32[64,4,2,128]{3,2,1,0:T(2,128)} %reduce_sum.83), calls=%async_computation.1 | async-start | bytes 524288 | tf_op jit(solution)/shard_map/all_to_all | solution.py:60
  137.1 12.7 %copy-start.6 = (f32[4,16,128]{2,1,0:T(8,128)S(1)}, f32[4,16,128]{2,1,0:T(8,128)}, u32[]{:S(2)}) copy-start(f32[4,16,128]{2,1,0:T(8,128)} %param.30) | copy-start | bytes 98308
  137.1 12.8 %copy-start.5 = (f32[16,16]{1,0:T(8,128)S(1)}, f32[16,16]{1,0:T(8,128)}, u32[]{:S(2)}) copy-start(f32[16,16]{1,0:T(8,128)} %param.34) | copy-start | bytes 3076
  137.1 19.8 %copy-start.10 = (f32[16]{0:T(128)S(1)}, f32[16]{0:T(128)}, u32[]{:S(2)}) copy-start(f32[16]{0:T(128)} %param.35) | copy-start | bytes 196
  156.9 13.0 %copy-start.2 = (f32[4,16,128]{2,1,0:T(8,128)}, f32[4,16,128]{2,1,0:T(8,128)S(1)}, u32[]{:S(2)}) copy-start(f32[4,16,128]{2,1,0:T(8,128)S(1)} %get-tuple-element.219) | copy-start | bytes 98308
  157.8 20.7 %all-to-all-start.2 = ((f32[64,4,128]{2,1,0:T(4,128)}), f32[64,4,128]{2,1,0:T(4,128)S(1)}, u32[]{:S(2)}, u32[]{:S(2)}) async-start(f32[64,4,128]{2,1,0:T(4,128)} %broadcast_in_dim.45), calls=%async_computation.2 | async-start | bytes 262144 | tf_op jit(solution)/shard_map/all_to_all | solution.py:65
  169.7 119.2 %all-gather.5.cloned.1.call-start = ((), (), s32[]{:S(2)}) async-start(), calls=%async_computation.9 | async-start | bytes 4227072 | tf_op jit(solution)/shard_map/all_gather | solution.py:235
  266.0 25.7 %copy-start.3 = (f32[4,16,128]{2,1,0:T(8,128)S(1)}, f32[4,16,128]{2,1,0:T(8,128)}, u32[]{:S(2)}) copy-start(f32[4,16,128]{2,1,0:T(8,128)} %copy-done.2) | copy-start | bytes 98308
  274.1 14.7 %all-to-all-start.5 = ((f32[64,4,2,128]{3,2,1,0:T(2,128)}), f32[64,4,2,128]{3,2,1,0:T(2,128)S(1)}, u32[]{:S(2)}, u32[]{:S(2)}) async-start(f32[64,4,2,128]{3,2,1,0:T(2,128)} %reduce_sum.86), calls=%async_computation.5 | async-start | bytes 524288 | tf_op jit(solution)/shard_map/all_to_all | solution.py:60
  278.7 40.8 %collective-permute-start.4 = (f32[1,16,128]{2,1,0:T(8,128)S(1)}, f32[1,16,128]{2,1,0:T(8,128)S(1)}, u32[]{:S(2)}, u32[]{:S(2)}) collective-permute-start(f32[1,16,128]{2,1,0:T(8,128)S(1)} %get-tuple-element.539), channel_id=1, source_target_pairs={{8,0},{16,8},{24,16},{32,24},{40,32},{48,40},{56,48},{64,56},{72,6... | collective-permute-start | bytes 24584 | tf_op jit(solution)/shard_map/ppermute | solution.py:34
  280.0 39.5 %collective-permute-start.5 = (f32[1,16,128]{2,1,0:T(8,128)S(1)}, f32[1,16,128]{2,1,0:T(8,128)S(1)}, u32[]{:S(2)}, u32[]{:S(2)}) collective-permute-start(f32[1,16,128]{2,1,0:T(8,128)S(1)} %get-tuple-element.538), channel_id=1, source_target_pairs={{0,8},{8,16},{16,24},{24,32},{32,40},{40,48},{48,56},{56,64},{64,7... | collective-permute-start | bytes 24584 | tf_op jit(solution)/shard_map/ppermute | solution.py:33
  298.8 60.3 %copy-start.4 = (f32[4,16,128]{2,1,0:T(8,128)}, f32[4,16,128]{2,1,0:T(8,128)S(1)}, u32[]{:S(2)}) copy-start(f32[4,16,128]{2,1,0:T(8,128)S(1)} %get-tuple-element.215) | copy-start | bytes 98308
  299.6 20.9 %all-to-all-start.6 = ((f32[64,4,128]{2,1,0:T(4,128)}), f32[64,4,128]{2,1,0:T(4,128)S(1)}, u32[]{:S(2)}, u32[]{:S(2)}) async-start(f32[64,4,128]{2,1,0:T(4,128)} %broadcast_in_dim.51), calls=%async_computation.6 | async-start | bytes 262144 | tf_op jit(solution)/shard_map/all_to_all | solution.py:65
  311.8 7.0 %collective-permute-start.6 = (f32[4,1,128]{2,1,0:T(1,128)S(1)}, f32[4,1,128]{2,1,0:T(1,128)S(1)}, u32[]{:S(2)}, u32[]{:S(2)}) collective-permute-start(f32[4,1,128]{2,1,0:T(1,128)S(1)} %get-tuple-element.541), channel_id=1, source_target_pairs={{1,0},{2,1},{3,2},{4,3},{5,4},{6,5},{7,6},{9,8},{10,9},{11,10},{12... | collective-permute-start | bytes 6152 | tf_op jit(solution)/shard_map/ppermute | solution.py:34
  315.7 3.8 %collective-permute-start.7 = (f32[4,1,128]{2,1,0:T(1,128)S(1)}, f32[4,1,128]{2,1,0:T(1,128)S(1)}, u32[]{:S(2)}, u32[]{:S(2)}) collective-permute-start(f32[4,1,128]{2,1,0:T(1,128)S(1)} %get-tuple-element.540), channel_id=1, source_target_pairs={{0,1},{1,2},{2,3},{3,4},{4,5},{5,6},{6,7},{8,9},{9,10},{10,11},{11... | collective-permute-start | bytes 6152 | tf_op jit(solution)/shard_map/ppermute | solution.py:33
Sparse Core Ops, SparseCore 0:
  11.1 71.7 all-gather.2
  174.2 69.4 all-gather.4
where the time goes:
time: 370 us; the launch traced here: 366 us
  matrix products  97.8 us (26%)
  local copies, waits for them, and re-layouts  73 us (20%)
  starting transfers between devices  64 us (17%)
  other arithmetic  62.9 us (17%)
  blocking collectives  21.3 us (6%)
  waiting for transfers between devices  19.3 us (5%)
  between operations  14.8 us (4%)
  loops' own time  12.8 us (3%)
    dot_general x32, matrix products, one_block(): jnp.dot(selector, blend_block_number, precision=lax.Precision.HIGHEST, pr...  56.5 us
    dot_general x32, matrix products, attach_block(): lax.dot_general(selector, values, (((0,), (0,)), ((), ())), precision=lax...  38.6 us
    mul x32, other arithmetic, attach_block(): values = jnp.concatenate([weighted, weighted * speed_piece], axis=-1)  36.8 us
    all_to_all x2, starting transfers between devices, copy_for_each(): return lax.all_to_all(copies, axis, split_axis=0, concat_axis=0, tiled=True)  24 us
    dynamic_slice x96, local copies, waits for them, and re-layouts, small_volume_accumulations(): lax.scan(attach_block, start_total, (flat_table, flat_mass, flat_speed, f...  22.8 us
    gather x3, local copies, waits for them, and re-layouts, shards(): near_slot = block_position[face_partners[position_block_map]]  20.8 us
    all_to_all x2, starting transfers between devices, sum_in_two_steps(): return jnp.sum(lax.all_to_all(own, far, 0, 0, tiled=True), axis=0)  16.4 us
    ppermute x4, starting transfers between devices, extended(): lax.ppermute(last, axis, up)  14.1 us
  transfers between devices with their start and end apart: 14, of which 5 were waited for; matrix products, arithmetic and copies ran while one was open for 55% of the time, Pallas kernels for 0%

commit v1 on v0

v1 whole, which is shorter than its diff:
```python
import jax
import jax.numpy as jnp
from jax import lax
from jax.experimental import pallas as pl
from jax.experimental.pallas import tpu as pltpu
from jax.sharding import PartitionSpec as P

DEV = 128
OWN = 4
SLOTS = 512
SPEC = 16
ETA = 128
ROWS = 64
SUBMAX = 16
LABELS = 48
GROUPS = 8
WIDE = 1024
FIRST = 9
LATER = 5

coupling = 0.05
mixing_rate = 0.2
react_rate = 0.5
prior_weight = 1.0
prior_flux = 0.5
thermal_diffusion = 0.1
damping_contribution = 0.3

f32 = jnp.float32
bf16 = jnp.bfloat16
NN = ((1,), (0,))
NT = ((1,), (1,))
TN = ((0,), (0,))


def dot(a, b, dims):
    return lax.dot_general(a, b, (dims, ((), ())), preferred_element_type=f32)


def iota(shape, dim):
    return lax.broadcasted_iota(jnp.int32, shape, dim)


def halves(x):
    high = x.astype(bf16)
    return high, (x - high.astype(f32)).astype(bf16)


def thirds(x):
    high = x.astype(bf16)
    rest = x - high.astype(f32)
    mid = rest.astype(bf16)
    return high, mid, (rest - mid.astype(f32)).astype(bf16)


def hot(mask):
    return jnp.where(mask, 1.0, 0.0).astype(bf16)


def rows_of(ref, group):
    return ref[pl.ds(pl.multiple_of(group * 8, 8), 8), :]


def put_rows(ref, group, rows):
    ref[pl.ds(pl.multiple_of(group * 8, 8), 8), :] = jnp.concatenate(rows, axis=0)


def to_slots(rs, sums):
    high, mid, low = thirds(sums)
    return dot(rs, high, NN) + dot(rs, mid, NN) + dot(rs, low, NN)


def prep_kernel(
    t_ref, av_ref, var_ref, mass_ref, bare_ref, par_ref, bp_ref, fp_ref,
    e_ref, mw_ref, rinv_ref, lab_ref, rs_ref, m_ref, sums_ref,
    pres, le, l1e, a1, b1, chi, arms, acc,
):
    for block in range(4):
        ids = iota((128, 128), 0) + block * 128

        def seen(group, found):
            rows = rows_of(par_ref, group)
            for q in range(8):
                found = jnp.where(rows[q : q + 1] == ids, 1.0, found)
            return found

        found = lax.fori_loop(0, GROUPS, seen, jnp.zeros((128, 128), f32))
        pres[block * 128 : (block + 1) * 128, :] = found.astype(bf16)
    named = dot(pres[...], jnp.ones((128, 128), bf16), NN) > 0.5
    before = hot(iota((SLOTS, SLOTS), 1) < iota((SLOTS, SLOTS), 0))
    rank = dot(before, hot(named), NN)
    sel = hot(named & (rank == iota((SLOTS, 128), 1).astype(f32)))
    cell = iota((SLOTS, 128), 0) + 1
    upper = dot(sel, (cell >> 4).astype(f32).astype(bf16), TN)
    lower = dot(sel, (cell & 15).astype(f32).astype(bf16), TN)
    label = (upper * 16.0 + lower).astype(jnp.int32) - 1
    lab = label[:LABELS]
    lab_ref[...] = lab

    place = iota((SLOTS, SLOTS), 0)
    place = (place & 127) * OWN + (place >> 7)
    pt = hot(bp_ref[...] == place)
    rs = dot(pt, sel, NN).astype(bf16)[:, :LABELS]
    rs_ref[...] = rs
    other = iota((SLOTS, SLOTS), 1)
    adjacent = jnp.zeros((SLOTS, SLOTS), f32)
    for j in range(6):
        adjacent = adjacent + jnp.where(fp_ref[:, j : j + 1] == other, 1.0, 0.0)
    half = dot(pt, adjacent.astype(bf16), NN).astype(bf16)
    m_ref[...] = dot(half, pt, NT).astype(bf16)

    point = (iota((ETA, 128), 0).astype(f32) + 0.5) / ETA
    le[...] = jnp.log(point)
    l1e[...] = jnp.log(1.0 - point)
    shape_sum = 1.0 / var_ref[...] - 1.0
    a1[...] = av_ref[...] * shape_sum - 1.0
    b1[...] = (1.0 - av_ref[...]) * shape_sum - 1.0
    chi[...] = bare_ref[...] * (1.0 + 0.5 * jnp.tanh(t_ref[...]))
    acc[...] = jnp.zeros_like(acc)

    def tables(group, carry):
        a_rows, b_rows = rows_of(a1, group), rows_of(b1, group)
        chi_rows, mass_rows, par_rows = rows_of(chi, group), rows_of(mass_ref, group), rows_of(par_ref, group)
        inverse, mass_over = [], []
        for q in range(8):
            at = slice(q * 128, (q + 1) * 128)
            logits = a_rows[q : q + 1] * le[...] + b_rows[q : q + 1] * l1e[...]
            table = jnp.exp(logits - jnp.max(logits, axis=0, keepdims=True))
            r = 1.0 / jnp.sum(table, axis=0, keepdims=True)
            high, low = halves(table)
            e_ref[group, 0:128, at] = high
            e_ref[group, 128:256, at] = low
            w = mass_rows[q : q + 1] * r
            n = w * chi_rows[q : q + 1]
            inverse.append(r)
            mass_over.append(w)
            mine = lab == par_rows[q : q + 1]
            for k, part in enumerate((*halves(w), *halves(n))):
                arms[k * LABELS : (k + 1) * LABELS, at] = jnp.where(mine, part.astype(f32), 0.0).astype(bf16)
        put_rows(rinv_ref, group, inverse)
        put_rows(mw_ref, group, mass_over)
        acc[...] += dot(arms[...], e_ref[group], NT)
        return carry

    lax.fori_loop(0, GROUPS, tables, 0)
    both = acc[:, :128] + acc[:, 128:]
    w48 = both[0:48] + both[48:96]
    n48 = both[96:144] + both[144:192]
    sums_ref[...] = to_slots(rs, jnp.concatenate([w48, n48], axis=1))


def neighbour_sums(part, m):
    lane = iota((128, 128), 1)
    stacked = jnp.concatenate([jnp.where(lane >> 4 == t, part, 0.0) for t in range(OWN)], axis=0)
    high, low = halves(stacked)
    both = dot(m, jnp.concatenate([high, low], axis=1), NN)
    total = both[:, :128] + both[:, 128:]
    for shift in (64, 32, 16):
        total = total + pltpu.roll(total, shift, 1)
    out = jnp.zeros((128, 128), f32)
    for t in range(OWN):
        out = jnp.where(lane >> 4 == t, total[t * 128 : (t + 1) * 128], out)
    return out


def edges_by_z(t_ref, edge):
    edge[...] = jnp.zeros_like(edge)
    edge[64:80, :] = t_ref[0:16, :]
    edge[80:96, :] = t_ref[48:64, :]
    for x in range(4):
        edge[96 + x : 97 + x, :] = t_ref[16 * x : 16 * x + 1, :]
        edge[100 + x : 101 + x, :] = t_ref[16 * x + 15 : 16 * x + 16, :]
    return edge[...].T


def first_pack_kernel(got_ref, m_ref, sums_ref, t_ref, out_ref, edge):
    misc = neighbour_sums(got_ref[...], m_ref[...]) + edges_by_z(t_ref, edge)
    for t in range(OWN):
        out_ref[pl.ds(t, 128, stride=FIRST), :] = sums_ref[t * 128 : (t + 1) * 128, 0:128]
        out_ref[pl.ds(OWN + t, 128, stride=FIRST), :] = sums_ref[t * 128 : (t + 1) * 128, 128:256]
    out_ref[pl.ds(2 * OWN, 128, stride=FIRST), :] = misc


def passed_on(misc):
    lane, row = iota((128, 128), 1), iota((128, 128), 0)
    gx, gy = row >> 3, row & 7
    out = jnp.where((lane >= 64) & (lane < 80) & (gx < 15), pltpu.roll(misc, 120, 0), 0.0)
    out = jnp.where((lane >= 80) & (lane < 96) & (gx > 0), pltpu.roll(misc, 8, 0), out)
    out = jnp.where((lane >= 96) & (lane < 100) & (gy < 7), pltpu.roll(misc, 127, 0), out)
    return jnp.where((lane >= 100) & (lane < 104) & (gy > 0), pltpu.roll(misc, 1, 0), out)


def advance(state_ref, misc, cchi, dev, bp_ref, ri_ref, c_ref, sw_ref, cols, out_ref, last):
    for s in range(SPEC):
        cols[s] = jnp.broadcast_to(c_ref[:, s : s + 1], (SPEC, ETA))
    mine = bp_ref[...] == dev * OWN + (iota((ROWS, SLOTS), 0) >> 4)
    count = jnp.sum(jnp.where(mine, ri_ref[...] + 1, 0).astype(f32), axis=1, keepdims=True)
    count = jnp.broadcast_to(count, (ROWS, ETA))
    fraction = 1.0 / count
    mixing = fraction * mixing_rate * jnp.concatenate(
        [jnp.broadcast_to(cchi[t], (SPEC, ETA)) for t in range(OWN)], axis=0
    )
    reacting = fraction * react_rate
    near = misc.T[:ROWS]
    state = state_ref[...]
    state = state + coupling * (near - 6.0 * state)
    lane = iota((ROWS, ETA), 1)

    def substep(index, current):
        speed = jnp.tanh(current)
        source = []
        for t in range(OWN):
            parts = [speed[t * SPEC + s : t * SPEC + s + 1] * cols[s] for s in range(SPEC)]
            while len(parts) > 1:
                parts = [a + b for a, b in zip(parts[::2], parts[1::2])]
            source.append(parts[0])
        source = jnp.concatenate(source, axis=0)
        left = jnp.where(lane == 0, current, pltpu.roll(current, 1, 1))
        right = jnp.where(lane == ETA - 1, current, pltpu.roll(current, ETA - 1, 1))
        update = mixing * (right - 2.0 * current + left) + reacting * source
        return jnp.where(index.astype(f32) < count, current + update, current)

    state = lax.fori_loop(0, SUBMAX, substep, state)
    state_ref_out, pay = out_ref
    state_ref_out[...] = state
    weight = jnp.sum(
        jnp.where(iota((SPEC, SPEC), 0) == iota((SPEC, SPEC), 1), sw_ref[...], 0.0), axis=1, keepdims=True
    )
    for t in range(OWN):
        theta = jnp.sum(weight * state[t * SPEC : (t + 1) * SPEC], axis=0, keepdims=True)
        pay[pl.ds(t, 128, stride=LATER), :] = jnp.broadcast_to(theta, (128, ETA))
    out = passed_on(misc)
    if not last:
        out = out + jnp.concatenate([state, jnp.zeros((128 - ROWS, ETA), f32)], axis=0).T
    pay[pl.ds(OWN, 128, stride=LATER), :] = out


def total_of(got_ref, row, stride):
    return jnp.sum(got_ref[pl.ds(row, 128, stride=stride), :], axis=0, keepdims=True)


def first_advance_kernel(
    dev_ref, got_ref, state_ref, bp_ref, ri_ref, c_ref, sw_ref, state_out, weight_out, pay, cols
):
    cchi = []
    for t in range(OWN):
        w = total_of(got_ref, t, FIRST)
        n = total_of(got_ref, OWN + t, FIRST)
        weight_out[t : t + 1, :] = w
        cchi.append((n + prior_flux) / (w + prior_weight))
    misc = got_ref[pl.ds(2 * OWN, 128, stride=FIRST), :]
    advance(state_ref, misc, cchi, dev_ref[0], bp_ref, ri_ref, c_ref, sw_ref, cols, (state_out, pay), False)


def later_advance_kernel(
    dev_ref, got_ref, state_ref, weight_ref, bp_ref, ri_ref, c_ref, sw_ref, state_out, pay, cols
):
    cchi = []
    for t in range(OWN):
        n = total_of(got_ref, t, LATER)
        cchi.append((n + prior_flux) / (weight_ref[t : t + 1, :] + prior_weight))
    misc = got_ref[pl.ds(OWN, 128, stride=LATER), :]
    advance(state_ref, misc, cchi, dev_ref[0], bp_ref, ri_ref, c_ref, sw_ref, cols, (state_out, pay), True)


def fine_update(got_ref, misc, t_ref, e_ref, rinv_ref, lab_ref, rs_ref, par_ref, tfine, grid):
    theta = jnp.concatenate([got_ref[pl.ds(t, 128, stride=LATER), :] for t in range(OWN)], axis=0)
    picked = dot(rs_ref[...], jnp.concatenate(halves(theta), axis=1), TN).astype(bf16)
    high, low = picked[:, :128], picked[:, 128:]
    rows = jnp.concatenate(
        [jnp.concatenate([high, high], axis=1), jnp.concatenate([low, low], axis=1)], axis=0
    )
    lab = lab_ref[...]

    def weigh(group, carry):
        means = dot(rows, e_ref[group], NN)
        means = means[:LABELS] + means[LABELS:]
        par_rows, inverse = rows_of(par_ref, group), rows_of(rinv_ref, group)
        out = []
        for q in range(8):
            mine = lab == par_rows[q : q + 1]
            out.append(jnp.sum(jnp.where(mine, means[:, q * 128 : (q + 1) * 128], 0.0), axis=0, keepdims=True))
        put_rows(tfine, group, [jnp.concatenate(out, axis=0) * inverse])
        return carry

    lax.fori_loop(0, GROUPS, weigh, 0)
    beside = misc.T
    t = t_ref[...]
    grid[1:5, 8:24, :] = t.reshape(4, 16, 128)
    grid[5, 8:24, :] = beside[64:80]
    grid[0, 8:24, :] = beside[80:96]
    for x in range(4):
        grid[1 + x, 24:25, :] = beside[96 + x : 97 + x]
        grid[1 + x, 7:8, :] = beside[100 + x : 101 + x]
    around = grid[2:6, 8:24, :] + grid[0:4, 8:24, :]
    around = around + grid[1:5, 9:25, :] + grid[1:5, 7:23, :]
    around = around.reshape(ROWS, 128)
    lane = iota((ROWS, 128), 1)
    around = around + jnp.where(lane == 127, 0.0, pltpu.roll(t, 127, 1))
    around = around + jnp.where(lane == 0, 0.0, pltpu.roll(t, 1, 1))
    return t + thermal_diffusion * (around - 6.0 * t) + damping_contribution * (tfine[...] - t)


def middle_kernel(
    got_ref, t_ref, e_ref, rinv_ref, mw_ref, lab_ref, rs_ref, m_ref, par_ref, bare_ref,
    t_out, pay, tfine, grid, flux, arms, acc, edge,
):
    misc = got_ref[pl.ds(OWN, 128, stride=LATER), :]
    t = fine_update(got_ref, misc, t_ref, e_ref, rinv_ref, lab_ref, rs_ref, par_ref, tfine, grid)
    t_out[...] = t
    flux[...] = mw_ref[...] * (bare_ref[...] * (1.0 + 0.5 * jnp.tanh(t)))
    acc[...] = jnp.zeros_like(acc)
    lab = lab_ref[...]

    def gather(group, carry):
        flux_rows, par_rows = rows_of(flux, group), rows_of(par_ref, group)
        for q in range(8):
            mine = lab == par_rows[q : q + 1]
            for k, part in enumerate(halves(flux_rows[q : q + 1])):
                arms[k * LABELS : (k + 1) * LABELS, q * 128 : (q + 1) * 128] = jnp.where(
                    mine, part.astype(f32), 0.0
                ).astype(bf16)
        acc[...] += dot(arms[...], e_ref[group], NT)
        return carry

    lax.fori_loop(0, GROUPS, gather, 0)
    both = acc[:, :128] + acc[:, 128:]
    sums = to_slots(rs_ref[...], both[0:48] + both[48:96])
    for k in range(OWN):
        pay[pl.ds(k, 128, stride=LATER), :] = sums[k * 128 : (k + 1) * 128]
    out = neighbour_sums(misc, m_ref[...]) + edges_by_z(t_out, edge)
    pay[pl.ds(OWN, 128, stride=LATER), :] = out


def final_kernel(got_ref, t_ref, e_ref, rinv_ref, lab_ref, rs_ref, par_ref, t_out, tfine, grid):
    misc = got_ref[pl.ds(OWN, 128, stride=LATER), :]
    t_out[...] = fine_update(got_ref, misc, t_ref, e_ref, rinv_ref, lab_ref, rs_ref, par_ref, tfine, grid)


def call(kernel, outs, scratch, *operands, scalars=0):
    vmem, smem = pl.BlockSpec(memory_space=pltpu.VMEM), pl.BlockSpec(memory_space=pltpu.SMEM)
    return pl.pallas_call(
        kernel,
        out_shape=[jax.ShapeDtypeStruct(*o) for o in outs],
        in_specs=[smem] * scalars + [vmem] * (len(operands) - scalars),
        out_specs=[vmem] * len(outs),
        scratch_shapes=[pltpu.VMEM(*s) for s in scratch],
    )(*operands)


def exchange(array):
    rows = array.shape[0] // DEV
    sent = array.reshape(DEV, 1, rows * 128)
    return lax.all_to_all(sent, ("gx", "gy"), 0, 0, tiled=True).reshape(array.shape)


def shards(thermal, average, variance, mass, bare, parent, species, position, partners, increments, chem, weight):
    dev = (lax.axis_index("gx") * 8 + lax.axis_index("gy")).astype(jnp.int32).reshape(1)
    fine = [a.reshape(ROWS, 128) for a in (thermal, average, variance, mass, bare, parent)]
    t0, av, var, mass, bare, par = fine
    state = species.reshape(ROWS, ETA)
    bp, ri, sw = position.reshape(1, SLOTS), increments.reshape(1, SLOTS), weight.reshape(1, SPEC)
    cells = ((ROWS, 128), f32)
    square = ((128, 128), f32)
    pay = ((DEV * LATER, 128), f32)

    states = exchange(jnp.pad(state.T, ((0, 0), (0, 128 - ROWS))))
    table, mw, rinv, lab, rs, m, sums = call(
        prep_kernel,
        [((GROUPS, 256, WIDE), bf16), cells, cells, ((LABELS, 128), jnp.int32), ((SLOTS, LABELS), bf16),
         ((SLOTS, SLOTS), bf16), ((SLOTS, 256), f32)],
        [((SLOTS, 128), bf16), square, square, cells, cells, cells, ((4 * LABELS, WIDE), bf16), ((4 * LABELS, 256), f32)],
        t0, av, var, mass, bare, par, bp, partners,
    )
    (sent,) = call(first_pack_kernel, [((DEV * FIRST, 128), f32)], [square], states, m, sums, t0)
    got = exchange(sent)
    cols = ((SPEC, SPEC, ETA), f32)
    state, own_weight, sent = call(
        first_advance_kernel, [((ROWS, ETA), f32), ((8, 128), f32), pay], [cols],
        dev, got, state, bp, ri, chem, sw, scalars=1,
    )
    got = exchange(sent)
    grid = ((6, 32, 128), f32)
    t1, sent = call(
        middle_kernel, [cells, pay],
        [cells, grid, cells, ((2 * LABELS, WIDE), bf16), ((2 * LABELS, 256), f32), square],
        got, t0, table, rinv, mw, lab, rs, m, par, bare,
    )
    got = exchange(sent)
    state, sent = call(
        later_advance_kernel, [((ROWS, ETA), f32), pay], [cols],
        dev, got, state, own_weight, bp, ri, chem, sw, scalars=1,
    )
    got = exchange(sent)
    (t2,) = call(final_kernel, [cells], [cells, grid], got, t1, table, rinv, lab, rs, par)
    return state.reshape(species.shape), t2.reshape(thermal.shape)


def solution(mesh):
    fine = P("gx", "gy", None)
    slots = P(("gx", "gy"), None, None)
    return jax.shard_map(
        shards,
        mesh=mesh,
        in_specs=(fine,) * 6 + (slots,) + (P(),) * 5,
        out_specs=(slots, fine),
        check_vma=False,
    )
```

time: 370 us -> 127 us (0.34); the launches traced: 366 us -> 127 us
  matrix products: 97.8 us -> 0 us
  local copies, waits for them, and re-layouts: 73 us -> 4.48 us
  other arithmetic: 62.9 us -> 0 us
  starting transfers between devices: 64 us -> 21.2 us
  Pallas kernels: 0 us -> 35.1 us
  blocking collectives: 21.3 us -> 51.1 us
  between operations: 14.8 us -> 0.66 us
  loops' own time: 12.8 us -> 0 us
  waiting for transfers between devices: 19.3 us -> 14.3 us
    dot_general x80 -> x0, matrix products: 97.8 us -> none  [the longest x32 56.5 us: one_block(): jnp.dot(selector, blend_block_number, precision=lax.Precision.HIGHEST, pr...]
    mul x47 -> x0, other arithmetic: 36.9 us -> none  [the longest x32 36.8 us: attach_block(): values = jnp.concatenate([weighted, weighted * speed_piece], axis=-1)]
    gather x12 -> x0, local copies, waits for them, and re-layouts: 36.1 us -> none  [the longest x3 20.8 us: shards(): near_slot = block_position[face_partners[position_block_map]]]
    pallas_call x0 -> x6, Pallas kernels: none -> 35.1 us  [call(): pl.pallas_call(kernel, out_shape=[jax.ShapeDtypeStruct(*o) for o in outs]...]
    all_to_all x4 -> x3, blocking collectives: 21.3 us -> 51.1 us  [exchange(): lax.all_to_all(sent, ('gx', 'gy'), 0, 0, tiled=True).reshape(array.shape)]
    ppermute x8 -> x0, starting transfers between devices: 23.5 us -> none  [the longest x4 14.1 us: extended(): lax.ppermute(last, axis, up)]
    dynamic_slice x96 -> x0, local copies, waits for them, and re-layouts: 22.8 us -> none  [small_volume_accumulations(): lax.scan(attach_block, start_total, (flat_table, flat_mass, flat_speed, f...]
    all_to_all x4 -> x2, starting transfers between devices: 40.5 us -> 21.2 us  [exchange(): lax.all_to_all(sent, ('gx', 'gy'), 0, 0, tiled=True).reshape(array.shape)]
  transfers between devices with their start and end apart: 14 -> 2, of which waited for: 5 -> 1; matrix products, arithmetic and copies ran while one was open for 55% -> 1% of each run, Pallas kernels for 0% -> 9%
where the time goes in v1:
time: 127 us
  blocking collectives  51.1 us (40%)
  Pallas kernels  35.1 us (28%)
  starting transfers between devices  21.2 us (17%)
  waiting for transfers between devices  14.3 us (11%)
  local copies, waits for them, and re-layouts  4.48 us (4%)
    all_to_all x3, blocking collectives, exchange(): lax.all_to_all(sent, ('gx', 'gy'), 0, 0, tiled=True).reshape(array.shape)  51.1 us
    pallas_call x6, Pallas kernels, call(): pl.pallas_call(kernel, out_shape=[jax.ShapeDtypeStruct(*o) for o in outs]...  35.1 us
    all_to_all x2, starting transfers between devices, exchange(): lax.all_to_all(sent, ('gx', 'gy'), 0, 0, tiled=True).reshape(array.shape)  21.2 us
    all_to_all x2, waiting for transfers between devices, exchange(): lax.all_to_all(sent, ('gx', 'gy'), 0, 0, tiled=True).reshape(array.shape)  14.3 us
    unnamed x5, local copies, waits for them, and re-layouts  2.99 us
  transfers between devices with their start and end apart: 2, of which 1 were waited for; matrix products, arithmetic and copies ran while one was open for 1% of the time, Pallas kernels for 9%

profile of v1, /device:TPU:1, one launch (start us, length us, event | category | flops | bytes accessed | tf_op | source)
XLA Modules:
  0.0 126.9 jit_solution(7349075408754383793)
XLA Ops:
  0.6 0.8 pad_bitcast_fusion
  1.4 0.7 copy.16
  2.1 11.5 %all-to-all-start = ((f32[128,1,128]{2,1,0:T(1,128)}), f32[128,1,128]{2,1,0:T(1,128)S(1)}, u32[]{:S(2)}, u32[]{:S(2)}) async-start(f32[128,1,128]{2,1,0:T(1,128)} %copy.16), calls=%async_computation | async-start | bytes 131072 | tf_op jit(solution)/shard_map/all_to_all | solution.py:354
  13.6 1.6 %copy.17.fp_ref = s32[512,6]{1,0:T(8,128)} copy(s32[512,6]{0,1:T(8,128)} %param.20) | data formatting | bytes 24576 | tf_op args[8]
  15.2 11.7 %shard_map.131 = (bf16[8,256,1024]{2,1,0:T(8,128)(2,1)}, f32[64,128]{1,0:T(8,128)}, f32[64,128]{1,0:T(8,128)}, s32[48,128]{1,0:T(8,128)}, bf16[512,48]{1,0:T(8,1...) custom-call(f32[64,128]{1,0:T(8,128)} %bitcast.37, f32[64,128]{1,0:T(8,128)} %bitcast.46, f32[64,128]{1,0:T(8,128)} %bitcast.47, ...), custom_call_target="tpu_custom_call" | custom-call | tf_op jit(solution)/shard_map/pallas_call | solution.py:342
  26.8 0.0 all-to-all-done
  26.8 0.0 copy-start.1
  26.8 0.6 copy-done.1
  27.5 2.6 %shard_map.132 = f32[1152,128]{1,0:T(8,128)} custom-call(f32[128,128]{1,0:T(8,128)} %bitcast.40, bf16[512,512]{1,0:T(8,128)(2,1)} %get-tuple-element.16.m_ref, f32[512,256]{1,0:T(8,128)} %get-tuple-element.17.sums_ref, f32[64,128]{1,0:T(8,128)} %bitcast.38), custom_call_target="tpu_custom_call" | custom-call | tf_op jit(solution)/shard_map/pallas_call | solution.py:342
  30.0 9.8 %all-to-all-start.1 = ((f32[128,1,1152]{2,1,0:T(1,128)}), f32[128,1,1152]{2,1,0:T(1,128)S(1)}, u32[]{:S(2)}, u32[]{:S(2)}) async-start(f32[128,1,1152]{2,1,0:T(1,128)} %bitcast.27), calls=%async_computation.1 | async-start | bytes 1179648 | tf_op jit(solution)/shard_map/all_to_all | solution.py:354
  39.8 14.3 %all-to-all-done.1 = f32[128,1,1152]{2,1,0:T(1,128)S(1)} async-done(((f32[128,1,1152]{2,1,0:T(1,128)}), f32[128,1,1152]{2,1,0:T(1,128)S(1)}, u32[]{:S(2)}, u32[]{:S(2)}) %all-to-all-start.1) | async-done | bytes 589856 | tf_op jit(solution)/shard_map/all_to_all | solution.py:354
  54.1 0.0 copy-start
  54.1 0.8 copy-done
  54.9 3.6 %shard_map.133 = (f32[64,128]{1,0:T(8,128)}, f32[8,128]{1,0:T(8,128)}, f32[640,128]{1,0:T(8,128)}) custom-call(s32[1]{0:T(128)} %bitcast.dev_ref, f32[1152,128]{1,0:T(8,128)} %bitcast.26, f32[64,128]{1,0:T(8,128)} %bitcast.44, s32[1,512]{1,0:T(1,128)} %bitcast.50, s32[1,512]{1,0:T(1,128)} %bitcast.52, f32[16,16]{1,0:T(8,128)} %c_ref.3, f32[1,16]{1,0:T(1,128)} %bitcast.54), custom_call_target="tpu_custom_call" | custom-call | tf_op jit(solution)/shard_map/pallas_call | solution.py:342
  58.6 17.2 %all_to_all.25 = f32[128,1,640]{2,1,0:T(1,128)} all-to-all(f32[128,1,640]{2,1,0:T(1,128)} %bitcast.33), channel_id=1, replica_groups=mesh['gx'=16,'gy'=8] {'gx','gy'}, dimensions={0} | all-to-all | bytes 655360 | tf_op jit(solution)/shard_map/all_to_all | solution.py:354
  75.8 8.5 %shard_map.134 = (f32[64,128]{1,0:T(8,128)}, f32[640,128]{1,0:T(8,128)}) custom-call(f32[640,128]{1,0:T(8,128)} %bitcast.30, f32[64,128]{1,0:T(8,128)} %bitcast.39, bf16[8,256,1024]{2,1,0:T(8,128)(2,1)} %get-tuple-element.19.e_ref, f32[64,128]{1,0:T(8,128)} %get-tuple-element.20.rinv_ref, f32[64,128]{1,0:T(8,128)} %get-tuple-element.21.mw_ref, ...), custom_call_target="tpu_custom_call" | custom-call | tf_op jit(solution)/shard_map/pallas_call | solution.py:342
  84.3 16.9 %all_to_all.26 = f32[128,1,640]{2,1,0:T(1,128)} all-to-all(f32[128,1,640]{2,1,0:T(1,128)} %bitcast.32), channel_id=1, replica_groups=mesh['gx'=16,'gy'=8] {'gx','gy'}, dimensions={0} | all-to-all | bytes 655360 | tf_op jit(solution)/shard_map/all_to_all | solution.py:354
  101.2 3.5 %shard_map.135 = (f32[64,128]{1,0:T(8,128)}, f32[640,128]{1,0:T(8,128)}) custom-call(s32[1]{0:T(128)} %bitcast.dev_ref, f32[640,128]{1,0:T(8,128)} %bitcast.29, f32[64,128]{1,0:T(8,128)} %get-tuple-element.25.state_ref, f32[8,128]{1,0:T(8,128)} %get-tuple-element.26.weight_ref, s32[1,512]{1,0:T(1,128)} %bitcast.51, s32[1,512]{1,0:T(1,128)} %bitcast.53, ...), custom_call_target="tpu_custom_call" | custom-call | tf_op jit(solution)/shard_map/pallas_call | solution.py:342
  104.7 16.9 %all_to_all.27 = f32[128,1,640]{2,1,0:T(1,128)} all-to-all(f32[128,1,640]{2,1,0:T(1,128)} %bitcast.31), channel_id=1, replica_groups=mesh['gx'=16,'gy'=8] {'gx','gy'}, dimensions={0} | all-to-all | bytes 655360 | tf_op jit(solution)/shard_map/all_to_all | solution.py:354
  121.7 5.2 %shard_map.136 = f32[64,128]{1,0:T(8,128)} custom-call(f32[640,128]{1,0:T(8,128)} %bitcast.28, f32[64,128]{1,0:T(8,128)} %get-tuple-element.29.t_ref, bf16[8,256,1024]{2,1,0:T(8,128)(2,1)} %get-tuple-element.19.e_ref, f32[64,128]{1,0:T(8,128)} %get-tuple-element.20.rinv_ref, s32[48,128]{1,0:T(8,128)} %get-tuple-element.22.lab_ref, ...), custom_call_target="tpu_custom_call" | custom-call | tf_op jit(solution)/shard_map/pallas_call | solution.py:342
Async XLA Ops:
  2.1 24.7 %all-to-all-start = ((f32[128,1,128]{2,1,0:T(1,128)}), f32[128,1,128]{2,1,0:T(1,128)S(1)}, u32[]{:S(2)}, u32[]{:S(2)}) async-start(f32[128,1,128]{2,1,0:T(1,128)} %copy.16), calls=%async_computation | async-start | bytes 131072 | tf_op jit(solution)/shard_map/all_to_all | solution.py:354
  26.8 0.6 copy-start.1
  30.0 24.1 %all-to-all-start.1 = ((f32[128,1,1152]{2,1,0:T(1,128)}), f32[128,1,1152]{2,1,0:T(1,128)S(1)}, u32[]{:S(2)}, u32[]{:S(2)}) async-start(f32[128,1,1152]{2,1,0:T(1,128)} %bitcast.27), calls=%async_computation.1 | async-start | bytes 1179648 | tf_op jit(solution)/shard_map/all_to_all | solution.py:354
  54.1 0.8 copy-start

commit v2 on v1

--- a/solution.py
+++ b/solution.py
@@ -71,10 +71,23 @@
 
 
 def prep_kernel(
-    t_ref, av_ref, var_ref, mass_ref, bare_ref, par_ref, bp_ref, fp_ref,
-    e_ref, mw_ref, rinv_ref, lab_ref, rs_ref, m_ref, sums_ref,
-    pres, le, l1e, a1, b1, chi, arms, acc,
+    dev_ref, t_ref, av_ref, var_ref, mass_ref, bare_ref, par_ref, bp_ref, fp_ref, ri_ref, c_ref, sw_ref,
+    e_out, mb_ref, rinv_ref, lab_ref, rs_ref, m_ref, sums_ref, edge_ref, count_ref, cols, weight_ref,
+    pres, le, l1e, a1, b1, chi, arms, acc, e_ref, edge, sems,
 ):
+    edge_ref[...] = edges_by_z(t_ref, edge)
+    for s in range(SPEC):
+        cols[s] = jnp.broadcast_to(c_ref[:, s : s + 1], (SPEC, ETA))
+    weight_ref[...] = jnp.broadcast_to(
+        jnp.sum(
+            jnp.where(iota((SPEC, SPEC), 0) == iota((SPEC, SPEC), 1), sw_ref[...], 0.0), axis=1, keepdims=True
+        ),
+        (SPEC, ETA),
+    )
+    own = bp_ref[...] == dev_ref[0] * OWN + (iota((ROWS, SLOTS), 0) >> 4)
+    count = jnp.sum(jnp.where(own, ri_ref[...] + 1, 0).astype(f32), axis=1, keepdims=True)
+    count_ref[...] = jnp.broadcast_to(count, (ROWS, ETA))
+
     for block in range(4):
         ids = iota((128, 128), 0) + block * 128
 
@@ -102,11 +115,11 @@
     pt = hot(bp_ref[...] == place)
     rs = dot(pt, sel, NN).astype(bf16)[:, :LABELS]
     rs_ref[...] = rs
-    other = iota((SLOTS, SLOTS), 1)
+    other = iota((SLOTS, SLOTS), 0)
     adjacent = jnp.zeros((SLOTS, SLOTS), f32)
     for j in range(6):
-        adjacent = adjacent + jnp.where(fp_ref[:, j : j + 1] == other, 1.0, 0.0)
-    half = dot(pt, adjacent.astype(bf16), NN).astype(bf16)
+        adjacent = adjacent + jnp.where(fp_ref[j : j + 1, :] == other, 1.0, 0.0)
+    half = dot(pt, adjacent.astype(bf16), NT).astype(bf16)
     m_ref[...] = dot(half, pt, NT).astype(bf16)
 
     point = (iota((ETA, 128), 0).astype(f32) + 0.5) / ETA
@@ -138,7 +151,8 @@
             for k, part in enumerate((*halves(w), *halves(n))):
                 arms[k * LABELS : (k + 1) * LABELS, at] = jnp.where(mine, part.astype(f32), 0.0).astype(bf16)
         put_rows(rinv_ref, group, inverse)
-        put_rows(mw_ref, group, mass_over)
+        put_rows(mb_ref, group, [jnp.concatenate(mass_over, axis=0) * rows_of(bare_ref, group)])
+        pltpu.make_async_copy(e_ref.at[group], e_out.at[group], sems.at[group]).start()
         acc[...] += dot(arms[...], e_ref[group], NT)
         return carry
 
@@ -147,6 +161,8 @@
     w48 = both[0:48] + both[48:96]
     n48 = both[96:144] + both[144:192]
     sums_ref[...] = to_slots(rs, jnp.concatenate([w48, n48], axis=1))
+    for group in range(GROUPS):
+        pltpu.make_async_copy(e_ref.at[group], e_out.at[group], sems.at[group]).wait()
 
 
 def neighbour_sums(part, m):
@@ -173,8 +189,12 @@
     return edge[...].T
 
 
-def first_pack_kernel(got_ref, m_ref, sums_ref, t_ref, out_ref, edge):
-    misc = neighbour_sums(got_ref[...], m_ref[...]) + edges_by_z(t_ref, edge)
+def split_kernel(state_ref, out_ref):
+    out_ref[...] = jnp.concatenate([state_ref[...], jnp.zeros((128 - ROWS, ETA), f32)], axis=0).T
+
+
+def first_pack_kernel(got_ref, m_ref, sums_ref, edge_ref, out_ref):
+    misc = neighbour_sums(got_ref[...], m_ref[...]) + edge_ref[...]
     for t in range(OWN):
         out_ref[pl.ds(t, 128, stride=FIRST), :] = sums_ref[t * 128 : (t + 1) * 128, 0:128]
         out_ref[pl.ds(OWN + t, 128, stride=FIRST), :] = sums_ref[t * 128 : (t + 1) * 128, 128:256]
@@ -190,12 +210,8 @@
     return jnp.where((lane >= 100) & (lane < 104) & (gy > 0), pltpu.roll(misc, 1, 0), out)
 
 
-def advance(state_ref, misc, cchi, dev, bp_ref, ri_ref, c_ref, sw_ref, cols, out_ref, last):
-    for s in range(SPEC):
-        cols[s] = jnp.broadcast_to(c_ref[:, s : s + 1], (SPEC, ETA))
-    mine = bp_ref[...] == dev * OWN + (iota((ROWS, SLOTS), 0) >> 4)
-    count = jnp.sum(jnp.where(mine, ri_ref[...] + 1, 0).astype(f32), axis=1, keepdims=True)
-    count = jnp.broadcast_to(count, (ROWS, ETA))
+def advance(state_ref, misc, cchi, count_ref, cols, weight_ref, out_ref, last):
+    count = count_ref[...]
     fraction = 1.0 / count
     mixing = fraction * mixing_rate * jnp.concatenate(
         [jnp.broadcast_to(cchi[t], (SPEC, ETA)) for t in range(OWN)], axis=0
@@ -223,9 +239,7 @@
     state = lax.fori_loop(0, SUBMAX, substep, state)
     state_ref_out, pay = out_ref
     state_ref_out[...] = state
-    weight = jnp.sum(
-        jnp.where(iota((SPEC, SPEC), 0) == iota((SPEC, SPEC), 1), sw_ref[...], 0.0), axis=1, keepdims=True
-    )
+    weight = weight_ref[...]
     for t in range(OWN):
         theta = jnp.sum(weight * state[t * SPEC : (t + 1) * SPEC], axis=0, keepdims=True)
         pay[pl.ds(t, 128, stride=LATER), :] = jnp.broadcast_to(theta, (128, ETA))
@@ -240,7 +254,7 @@
 
 
 def first_advance_kernel(
-    dev_ref, got_ref, state_ref, bp_ref, ri_ref, c_ref, sw_ref, state_out, weight_out, pay, cols
+    got_ref, state_ref, count_ref, cols, weight_ref, state_out, weight_out, pay
 ):
     cchi = []
     for t in range(OWN):
@@ -249,18 +263,18 @@
         weight_out[t : t + 1, :] = w
         cchi.append((n + prior_flux) / (w + prior_weight))
     misc = got_ref[pl.ds(2 * OWN, 128, stride=FIRST), :]
-    advance(state_ref, misc, cchi, dev_ref[0], bp_ref, ri_ref, c_ref, sw_ref, cols, (state_out, pay), False)
+    advance(state_ref, misc, cchi, count_ref, cols, weight_ref, (state_out, pay), False)
 
 
 def later_advance_kernel(
-    dev_ref, got_ref, state_ref, weight_ref, bp_ref, ri_ref, c_ref, sw_ref, state_out, pay, cols
+    got_ref, state_ref, mass_ref, count_ref, cols, weight_ref, state_out, pay
 ):
     cchi = []
     for t in range(OWN):
         n = total_of(got_ref, t, LATER)
-        cchi.append((n + prior_flux) / (weight_ref[t : t + 1, :] + prior_weight))
+        cchi.append((n + prior_flux) / (mass_ref[t : t + 1, :] + prior_weight))
     misc = got_ref[pl.ds(OWN, 128, stride=LATER), :]
-    advance(state_ref, misc, cchi, dev_ref[0], bp_ref, ri_ref, c_ref, sw_ref, cols, (state_out, pay), True)
+    advance(state_ref, misc, cchi, count_ref, cols, weight_ref, (state_out, pay), True)
 
 
 def fine_update(got_ref, misc, t_ref, e_ref, rinv_ref, lab_ref, rs_ref, par_ref, tfine, grid):
@@ -302,13 +316,13 @@
 
 
 def middle_kernel(
-    got_ref, t_ref, e_ref, rinv_ref, mw_ref, lab_ref, rs_ref, m_ref, par_ref, bare_ref,
+    got_ref, t_ref, e_ref, rinv_ref, mb_ref, lab_ref, rs_ref, m_ref, par_ref,
     t_out, pay, tfine, grid, flux, arms, acc, edge,
 ):
     misc = got_ref[pl.ds(OWN, 128, stride=LATER), :]
     t = fine_update(got_ref, misc, t_ref, e_ref, rinv_ref, lab_ref, rs_ref, par_ref, tfine, grid)
     t_out[...] = t
-    flux[...] = mw_ref[...] * (bare_ref[...] * (1.0 + 0.5 * jnp.tanh(t)))
+    flux[...] = mb_ref[...] * (1.0 + 0.5 * jnp.tanh(t))
     acc[...] = jnp.zeros_like(acc)
     lab = lab_ref[...]
 
@@ -337,14 +351,16 @@
     t_out[...] = fine_update(got_ref, misc, t_ref, e_ref, rinv_ref, lab_ref, rs_ref, par_ref, tfine, grid)
 
 
-def call(kernel, outs, scratch, *operands, scalars=0):
+def call(kernel, outs, scratch, *operands, scalars=0, results=(), streamed=()):
     vmem, smem = pl.BlockSpec(memory_space=pltpu.VMEM), pl.BlockSpec(memory_space=pltpu.SMEM)
+    away = set(results) | set(streamed)
     return pl.pallas_call(
         kernel,
-        out_shape=[jax.ShapeDtypeStruct(*o) for o in outs],
+        out_shape=[pltpu.HBM(*o) if i in away else pltpu.VMEM(*o) for i, o in enumerate(outs)],
         in_specs=[smem] * scalars + [vmem] * (len(operands) - scalars),
-        out_specs=[vmem] * len(outs),
-        scratch_shapes=[pltpu.VMEM(*s) for s in scratch],
+        out_specs=[pl.BlockSpec(memory_space=pl.ANY) if i in streamed else vmem for i in range(len(outs))],
+        scratch_shapes=[pltpu.VMEM(*s) if isinstance(s, tuple) else s for s in scratch],
+        compiler_params=pltpu.CompilerParams(vmem_limit_bytes=24 << 20),
     )(*operands)
 
 
@@ -352,6 +368,10 @@
     rows = array.shape[0] // DEV
     sent = array.reshape(DEV, 1, rows * 128)
     return lax.all_to_all(sent, ("gx", "gy"), 0, 0, tiled=True).reshape(array.shape)
+
+
+def from_hbm(*arrays):
+    return [pltpu.with_memory_space_constraint(a, pltpu.HBM) for a in arrays]
 
 
 def shards(thermal, average, variance, mass, bare, parent, species, position, partners, increments, chem, weight):
@@ -364,35 +384,35 @@
     square = ((128, 128), f32)
     pay = ((DEV * LATER, 128), f32)
 
-    states = exchange(jnp.pad(state.T, ((0, 0), (0, 128 - ROWS))))
-    table, mw, rinv, lab, rs, m, sums = call(
+    states = exchange(call(split_kernel, [square], [], *from_hbm(state))[0])
+    table, mb, rinv, lab, rs, m, sums, edges, count, cols, sw = call(
         prep_kernel,
         [((GROUPS, 256, WIDE), bf16), cells, cells, ((LABELS, 128), jnp.int32), ((SLOTS, LABELS), bf16),
-         ((SLOTS, SLOTS), bf16), ((SLOTS, 256), f32)],
-        [((SLOTS, 128), bf16), square, square, cells, cells, cells, ((4 * LABELS, WIDE), bf16), ((4 * LABELS, 256), f32)],
-        t0, av, var, mass, bare, par, bp, partners,
-    )
-    (sent,) = call(first_pack_kernel, [((DEV * FIRST, 128), f32)], [square], states, m, sums, t0)
+         ((SLOTS, SLOTS), bf16), ((SLOTS, 256), f32), square, cells, ((SPEC, SPEC, ETA), f32), ((SPEC, ETA), f32)],
+        [((SLOTS, 128), bf16), square, square, cells, cells, cells, ((4 * LABELS, WIDE), bf16),
+         ((4 * LABELS, 256), f32), ((GROUPS, 256, WIDE), bf16), square, pltpu.SemaphoreType.DMA((GROUPS,))],
+        dev, *from_hbm(t0, av, var, mass, bare, par, bp, partners.T, ri, chem, sw), scalars=1, streamed=(0,),
+    )
+    (sent,) = call(first_pack_kernel, [((DEV * FIRST, 128), f32)], [], states, m, sums, edges)
     got = exchange(sent)
-    cols = ((SPEC, SPEC, ETA), f32)
     state, own_weight, sent = call(
-        first_advance_kernel, [((ROWS, ETA), f32), ((8, 128), f32), pay], [cols],
-        dev, got, state, bp, ri, chem, sw, scalars=1,
+        first_advance_kernel, [((ROWS, ETA), f32), ((8, 128), f32), pay], [],
+        got, *from_hbm(state), count, cols, sw,
     )
     got = exchange(sent)
     grid = ((6, 32, 128), f32)
     t1, sent = call(
         middle_kernel, [cells, pay],
         [cells, grid, cells, ((2 * LABELS, WIDE), bf16), ((2 * LABELS, 256), f32), square],
-        got, t0, table, rinv, mw, lab, rs, m, par, bare,
+        got, t0, table, rinv, mb, lab, rs, m, par,
     )
     got = exchange(sent)
     state, sent = call(
-        later_advance_kernel, [((ROWS, ETA), f32), pay], [cols],
-        dev, got, state, own_weight, bp, ri, chem, sw, scalars=1,
+        later_advance_kernel, [((ROWS, ETA), f32), pay], [],
+        got, state, own_weight, count, cols, sw, results=(0,),
     )
     got = exchange(sent)
-    (t2,) = call(final_kernel, [cells], [cells, grid], got, t1, table, rinv, lab, rs, par)
+    (t2,) = call(final_kernel, [cells], [cells, grid], got, t1, table, rinv, lab, rs, par, results=(0,))
     return state.reshape(species.shape), t2.reshape(thermal.shape)
 
 

time: 127 us -> 109 us (0.86)
  blocking collectives: 51.1 us -> 72 us
  waiting for transfers between devices: 14.3 us -> 0.01 us
  Pallas kernels: 35.1 us -> 24.7 us
  starting transfers between devices: 21.2 us -> 11.5 us
  local copies, waits for them, and re-layouts: 4.48 us -> 0.02 us
    all_to_all x3 -> x4, blocking collectives: 51.1 us -> 72 us  [exchange(): lax.all_to_all(sent, ('gx', 'gy'), 0, 0, tiled=True).reshape(array.shape)]
    all_to_all x2 -> x1, waiting for transfers between devices: 14.3 us -> 0.01 us  [exchange(): lax.all_to_all(sent, ('gx', 'gy'), 0, 0, tiled=True).reshape(array.shape)]
    pallas_call x6 -> x7, Pallas kernels: 35.1 us -> 24.7 us  [call(): pl.pallas_call(kernel, out_shape=[pltpu.HBM(*o) if i in away else pltpu.V...]
    all_to_all x2 -> x1, starting transfers between devices: 21.2 us -> 11.5 us  [exchange(): lax.all_to_all(sent, ('gx', 'gy'), 0, 0, tiled=True).reshape(array.shape)]
    unnamed x5 -> x6, local copies, waits for them, and re-layouts: 2.99 us -> 0.02 us
    reshape x2 -> x0, local copies, waits for them, and re-layouts: 1.49 us -> none  [exchange(): sent = array.reshape(DEV, 1, rows * 128)]
  transfers between devices with their start and end apart: 2 -> 1, of which waited for: 1 -> 0; matrix products, arithmetic and copies ran while one was open for 1% -> 0% of each run, Pallas kernels for 9% -> 9%
where the time goes in v2:
time: 109 us
  blocking collectives  72 us (66%)
  Pallas kernels  24.7 us (23%)
  starting transfers between devices  11.5 us (11%)
    all_to_all x4, blocking collectives, exchange(): lax.all_to_all(sent, ('gx', 'gy'), 0, 0, tiled=True).reshape(array.shape)  72 us
    pallas_call x7, Pallas kernels, call(): pl.pallas_call(kernel, out_shape=[pltpu.HBM(*o) if i in away else pltpu.V...  24.7 us
    all_to_all x1, starting transfers between devices, exchange(): lax.all_to_all(sent, ('gx', 'gy'), 0, 0, tiled=True).reshape(array.shape)  11.5 us
  transfers between devices with their start and end apart: 1, of which 0 were waited for; matrix products, arithmetic and copies ran while one was open for 0% of the time, Pallas kernels for 9%

profile of v2, /device:TPU:1, one launch (start us, length us, event | category | flops | bytes accessed | tf_op | source)
XLA Modules:
  0.0 108.9 jit_solution(5479308845998222152)
XLA Ops:
  0.6 0.0 copy-start.1
  0.6 0.0 copy-start.2
  0.7 1.5 %shard_map.131 = f32[128,128]{1,0:T(8,128)} custom-call(f32[64,128]{1,0:T(8,128)} %bitcast.40), custom_call_target="tpu_custom_call" | custom-call | tf_op jit(solution)/shard_map/pallas_call | solution.py:357
  2.1 11.5 %all-to-all-start = ((f32[128,1,128]{2,1,0:T(1,128)}), f32[128,1,128]{2,1,0:T(1,128)S(1)}, u32[]{:S(2)}, u32[]{:S(2)}) async-start(f32[128,1,128]{2,1,0:T(1,128)} %bitcast.2), calls=%async_computation | async-start | bytes 131072 | tf_op jit(solution)/shard_map/all_to_all | solution.py:370
  13.6 10.0 %shard_map.132 = (bf16[8,256,1024]{2,1,0:T(8,128)(2,1)}, f32[64,128]{1,0:T(8,128)S(1)}, f32[64,128]{1,0:T(8,128)S(1)}, s32[48,128]{1,0:T(8,128)S(1)}, bf16[512,4...) custom-call(s32[1]{0:T(128)} %bitcast.4.dev_ref, ...), custom_call_target="tpu_custom_call" | custom-call | tf_op jit(solution)/shard_map/pallas_call | solution.py:357
  23.7 0.0 all-to-all-done
  23.7 0.0 copy-start
  23.7 0.5 shard_map.133
  24.2 23.9 %all_to_all.25 = f32[128,1,1152]{2,1,0:T(1,128)S(1)} all-to-all(f32[128,1,1152]{2,1,0:T(1,128)S(1)} %bitcast.26), channel_id=1, replica_groups=mesh['gx'=16,'gy'=8] {'gx','gy'}, dimensions={0} | all-to-all | bytes 1179648 | tf_op jit(solution)/shard_map/all_to_all | solution.py:370
  48.1 2.4 %shard_map.134 = (f32[64,128]{1,0:T(8,128)S(1)}, f32[8,128]{1,0:T(8,128)S(1)}, f32[640,128]{1,0:T(8,128)S(1)}) custom-call(f32[1152,128]{1,0:T(8,128)S(1)} %bitcast.27, f32[64,128]{1,0:T(8,128)} %bitcast.41, f32[64,128]{1,0:T(8,128)S(1)} %get-tuple-element.23.count_ref, f32[16,16,128]{2,1,0:T(8,128)S(1)} %get-tuple-element.24.cols, ...), custom_call_target="tpu_custom_call" | custom-call | tf_op jit(solution)/shard_map/pallas_call | solution.py:357
  50.5 16.2 %all_to_all.26 = f32[128,1,640]{2,1,0:T(1,128)S(1)} all-to-all(f32[128,1,640]{2,1,0:T(1,128)S(1)} %bitcast.33), channel_id=1, replica_groups=mesh['gx'=16,'gy'=8] {'gx','gy'}, dimensions={0} | all-to-all | bytes 655360 | tf_op jit(solution)/shard_map/all_to_all | solution.py:370
  66.7 0.0 copy-done.1
  66.7 0.0 copy-done.2
  66.7 0.0 copy-done
  66.7 5.3 %shard_map.135 = (f32[64,128]{1,0:T(8,128)S(1)}, f32[640,128]{1,0:T(8,128)S(1)}) custom-call(f32[640,128]{1,0:T(8,128)S(1)} %bitcast.30, f32[64,128]{1,0:T(8,128)S(1)} %bitcast.39, bf16[8,256,1024]{2,1,0:T(8,128)(2,1)S(1)} %copy-done, f32[64,128]{1,0:T(8,128)S(1)} %get-tuple-element.28.rinv_ref, f32[64,128]{1,0:T(8,128)S(1)} %get-tuple-element.29.mb_ref, ...), custom_call_target="tpu_custom_call" | custom-call | tf_op jit(solution)/shard_map/pallas_call | solution.py:357
  72.0 16.0 %all_to_all.27 = f32[128,1,640]{2,1,0:T(1,128)S(1)} all-to-all(f32[128,1,640]{2,1,0:T(1,128)S(1)} %bitcast.32), channel_id=1, replica_groups=mesh['gx'=16,'gy'=8] {'gx','gy'}, dimensions={0} | all-to-all | bytes 655360 | tf_op jit(solution)/shard_map/all_to_all | solution.py:370
  87.9 2.2 %shard_map.136 = (f32[64,128]{1,0:T(8,128)}, f32[640,128]{1,0:T(8,128)S(1)}) custom-call(f32[640,128]{1,0:T(8,128)S(1)} %bitcast.29, f32[64,128]{1,0:T(8,128)S(1)} %get-tuple-element.33.state_ref, f32[8,128]{1,0:T(8,128)S(1)} %get-tuple-element.34.mass_ref, f32[64,128]{1,0:T(8,128)S(1)} %get-tuple-element.23.count_ref, ...), custom_call_target="tpu_custom_call" | custom-call | tf_op jit(solution)/shard_map/pallas_call | solution.py:357
  90.1 16.0 %all_to_all.28 = f32[128,1,640]{2,1,0:T(1,128)S(1)} all-to-all(f32[128,1,640]{2,1,0:T(1,128)S(1)} %bitcast.31), channel_id=1, replica_groups=mesh['gx'=16,'gy'=8] {'gx','gy'}, dimensions={0} | all-to-all | bytes 655360 | tf_op jit(solution)/shard_map/all_to_all | solution.py:370
  106.1 2.8 %shard_map.137 = f32[64,128]{1,0:T(8,128)} custom-call(f32[640,128]{1,0:T(8,128)S(1)} %bitcast.28, f32[64,128]{1,0:T(8,128)S(1)} %get-tuple-element.37.t_ref, bf16[8,256,1024]{2,1,0:T(8,128)(2,1)S(1)} %copy-done, f32[64,128]{1,0:T(8,128)S(1)} %get-tuple-element.28.rinv_ref, s32[48,128]{1,0:T(8,128)S(1)} %get-tuple-element.30.lab_ref, ...), custom_call_target="tpu_custom_call" | custom-call | tf_op jit(solution)/shard_map/pallas_call | solution.py:357
Async XLA Ops:
  0.6 66.0 %copy-start.1 = (s32[4,16,128]{2,1,0:T(8,128)S(1)}, s32[4,16,128]{2,1,0:T(8,128)}, u32[]{:S(2)}) copy-start(s32[4,16,128]{2,1,0:T(8,128)} %param.17) | copy-start | bytes 98308
  0.6 66.0 %copy-start.2 = (f32[4,16,128]{2,1,0:T(8,128)S(1)}, f32[4,16,128]{2,1,0:T(8,128)}, u32[]{:S(2)}) copy-start(f32[4,16,128]{2,1,0:T(8,128)} %param.12) | copy-start | bytes 98308
  2.1 21.5 %all-to-all-start = ((f32[128,1,128]{2,1,0:T(1,128)}), f32[128,1,128]{2,1,0:T(1,128)S(1)}, u32[]{:S(2)}, u32[]{:S(2)}) async-start(f32[128,1,128]{2,1,0:T(1,128)} %bitcast.2), calls=%async_computation | async-start | bytes 131072 | tf_op jit(solution)/shard_map/all_to_all | solution.py:370
  23.7 43.0 %copy-start = (bf16[8,256,1024]{2,1,0:T(8,128)(2,1)S(1)}, bf16[8,256,1024]{2,1,0:T(8,128)(2,1)}, u32[]{:S(2)}) copy-start(bf16[8,256,1024]{2,1,0:T(8,128)(2,1)} %get-tuple-element.27.e_ref) | copy-start | bytes 12582916

commit v3 on v2

--- a/solution.py
+++ b/solution.py
@@ -17,6 +17,8 @@
 WIDE = 1024
 FIRST = 9
 LATER = 5
+UNROLL = 4
+LOG2E = 1.4426950408889634
 
 coupling = 0.05
 mixing_rate = 0.2
@@ -57,6 +59,10 @@
     return jnp.where(mask, 1.0, 0.0).astype(bf16)
 
 
+def marked(mask):
+    return jnp.where(mask, jnp.ones((), bf16), jnp.zeros((), bf16))
+
+
 def rows_of(ref, group):
     return ref[pl.ds(pl.multiple_of(group * 8, 8), 8), :]
 
@@ -72,8 +78,8 @@
 
 def prep_kernel(
     dev_ref, t_ref, av_ref, var_ref, mass_ref, bare_ref, par_ref, bp_ref, fp_ref, ri_ref, c_ref, sw_ref,
-    e_out, mb_ref, rinv_ref, lab_ref, rs_ref, m_ref, sums_ref, edge_ref, count_ref, cols, weight_ref,
-    pres, le, l1e, a1, b1, chi, arms, acc, e_ref, edge, sems,
+    e_out, mb_ref, rinv_ref, lab_ref, rs_ref, m_ref, sums_ref, edge_ref, count_ref, cols, weight_ref, who_ref,
+    le, l1e, a1, b1, chi, arms, acc, e_ref, edge, sems,
 ):
     edge_ref[...] = edges_by_z(t_ref, edge)
     for s in range(SPEC):
@@ -88,43 +94,58 @@
     count = jnp.sum(jnp.where(own, ri_ref[...] + 1, 0).astype(f32), axis=1, keepdims=True)
     count_ref[...] = jnp.broadcast_to(count, (ROWS, ETA))
 
-    for block in range(4):
-        ids = iota((128, 128), 0) + block * 128
-
-        def seen(group, found):
-            rows = rows_of(par_ref, group)
-            for q in range(8):
-                found = jnp.where(rows[q : q + 1] == ids, 1.0, found)
-            return found
-
-        found = lax.fori_loop(0, GROUPS, seen, jnp.zeros((128, 128), f32))
-        pres[block * 128 : (block + 1) * 128, :] = found.astype(bf16)
-    named = dot(pres[...], jnp.ones((128, 128), bf16), NN) > 0.5
-    before = hot(iota((SLOTS, SLOTS), 1) < iota((SLOTS, SLOTS), 0))
-    rank = dot(before, hot(named), NN)
-    sel = hot(named & (rank == iota((SLOTS, 128), 1).astype(f32)))
+    named = jnp.zeros((32, 16), f32)
+    for group in range(GROUPS):
+        rows = par_ref[group * 8 : (group + 1) * 8, :]
+        tall, short = rows >> 4, rows & 15
+        tall = jnp.concatenate([hot(tall[q : q + 1] == iota((32, 128), 0)) for q in range(8)], axis=1)
+        short = jnp.concatenate([hot(short[q : q + 1] == iota((16, 128), 0)) for q in range(8)], axis=1)
+        named = named + dot(tall, short, NT)
+    named = hot(named > 0.5)
+    within = dot(named, hot(iota((16, 16), 0) < iota((16, 16), 1)), NN)
+    ahead = dot(hot(iota((32, 32), 1) < iota((32, 32), 0)), named, NN).astype(bf16)
+    ahead = dot(ahead, jnp.ones((16, 16), bf16), NN)
+    order = jnp.where(named > 0, within + ahead + 1.0, 0.0).astype(bf16)
+    spread = dot(hot(iota((SLOTS, 32), 0) >> 4 == iota((SLOTS, 32), 1)), order, NN)
+    spread = jnp.where(iota((SLOTS, 16), 0) & 15 == iota((SLOTS, 16), 1), spread, 0.0).astype(bf16)
+    order = dot(spread, jnp.ones((16, 128), bf16), NN)
+    sel = hot(order == (iota((SLOTS, 128), 1) + 1).astype(f32))
     cell = iota((SLOTS, 128), 0) + 1
-    upper = dot(sel, (cell >> 4).astype(f32).astype(bf16), TN)
-    lower = dot(sel, (cell & 15).astype(f32).astype(bf16), TN)
-    label = (upper * 16.0 + lower).astype(jnp.int32) - 1
-    lab = label[:LABELS]
+    label = dot(
+        sel,
+        jnp.concatenate([(cell >> 4).astype(f32).astype(bf16), (cell & 15).astype(f32).astype(bf16)], axis=1),
+        TN,
+    )
+    lab = ((label[:, :128] * 16.0 + label[:, 128:]).astype(jnp.int32) - 1)[:LABELS]
     lab_ref[...] = lab
 
-    place = iota((SLOTS, SLOTS), 0)
-    place = (place & 127) * OWN + (place >> 7)
-    pt = hot(bp_ref[...] == place)
+    bp = bp_ref[...]
+    device = iota((128, SLOTS), 0).astype(f32).astype(bf16)
+    pt = jnp.concatenate(
+        [
+            marked(jnp.where(bp & 3 == t, bp >> 2, -1).astype(f32).astype(bf16) == device)
+            for t in range(OWN)
+        ],
+        axis=0,
+    )
     rs = dot(pt, sel, NN).astype(bf16)[:, :LABELS]
     rs_ref[...] = rs
-    other = iota((SLOTS, SLOTS), 0)
-    adjacent = jnp.zeros((SLOTS, SLOTS), f32)
-    for j in range(6):
-        adjacent = adjacent + jnp.where(fp_ref[j : j + 1, :] == other, 1.0, 0.0)
-    half = dot(pt, adjacent.astype(bf16), NT).astype(bf16)
+    other = iota((256, SLOTS), 0).astype(f32).astype(bf16)
+    near = fp_ref[...]
+    adjacent = []
+    for half in range(2):
+        part = near - 256 * half
+        part = jnp.where((part >= 0) & (part < 256), part, -1).astype(f32)
+        total = jnp.zeros((256, SLOTS), bf16)
+        for j in range(6):
+            total = total + marked(part[j : j + 1].astype(bf16) == other)
+        adjacent.append(total)
+    half = dot(pt, jnp.concatenate(adjacent, axis=0), NT).astype(bf16)
     m_ref[...] = dot(half, pt, NT).astype(bf16)
 
     point = (iota((ETA, 128), 0).astype(f32) + 0.5) / ETA
-    le[...] = jnp.log(point)
-    l1e[...] = jnp.log(1.0 - point)
+    le[...] = jnp.log(point) * LOG2E
+    l1e[...] = jnp.log(1.0 - point) * LOG2E
     shape_sum = 1.0 / var_ref[...] - 1.0
     a1[...] = av_ref[...] * shape_sum - 1.0
     b1[...] = (1.0 - av_ref[...]) * shape_sum - 1.0
@@ -138,7 +159,7 @@
         for q in range(8):
             at = slice(q * 128, (q + 1) * 128)
             logits = a_rows[q : q + 1] * le[...] + b_rows[q : q + 1] * l1e[...]
-            table = jnp.exp(logits - jnp.max(logits, axis=0, keepdims=True))
+            table = jnp.exp2(logits - jnp.max(logits, axis=0, keepdims=True))
             r = 1.0 / jnp.sum(table, axis=0, keepdims=True)
             high, low = halves(table)
             e_ref[group, 0:128, at] = high
@@ -147,17 +168,18 @@
             n = w * chi_rows[q : q + 1]
             inverse.append(r)
             mass_over.append(w)
-            mine = lab == par_rows[q : q + 1]
+            mine = hot(lab == par_rows[q : q + 1])
+            who_ref[group, :, at] = mine
             for k, part in enumerate((*halves(w), *halves(n))):
-                arms[k * LABELS : (k + 1) * LABELS, at] = jnp.where(mine, part.astype(f32), 0.0).astype(bf16)
+                arms[k * LABELS : (k + 1) * LABELS, at] = mine * part
         put_rows(rinv_ref, group, inverse)
         put_rows(mb_ref, group, [jnp.concatenate(mass_over, axis=0) * rows_of(bare_ref, group)])
         pltpu.make_async_copy(e_ref.at[group], e_out.at[group], sems.at[group]).start()
-        acc[...] += dot(arms[...], e_ref[group], NT)
+        acc[...] += dot(arms[...], e_ref[group, 0:128], NT)
         return carry
 
-    lax.fori_loop(0, GROUPS, tables, 0)
-    both = acc[:, :128] + acc[:, 128:]
+    lax.fori_loop(0, GROUPS, tables, 0, unroll=UNROLL)
+    both = acc[...]
     w48 = both[0:48] + both[48:96]
     n48 = both[96:144] + both[144:192]
     sums_ref[...] = to_slots(rs, jnp.concatenate([w48, n48], axis=1))
@@ -297,7 +319,7 @@
         put_rows(tfine, group, [jnp.concatenate(out, axis=0) * inverse])
         return carry
 
-    lax.fori_loop(0, GROUPS, weigh, 0)
+    lax.fori_loop(0, GROUPS, weigh, 0, unroll=UNROLL)
     beside = misc.T
     t = t_ref[...]
     grid[1:5, 8:24, :] = t.reshape(4, 16, 128)
@@ -316,7 +338,7 @@
 
 
 def middle_kernel(
-    got_ref, t_ref, e_ref, rinv_ref, mb_ref, lab_ref, rs_ref, m_ref, par_ref,
+    got_ref, t_ref, e_ref, rinv_ref, mb_ref, lab_ref, rs_ref, m_ref, par_ref, who_ref,
     t_out, pay, tfine, grid, flux, arms, acc, edge,
 ):
     misc = got_ref[pl.ds(OWN, 128, stride=LATER), :]
@@ -324,21 +346,18 @@
     t_out[...] = t
     flux[...] = mb_ref[...] * (1.0 + 0.5 * jnp.tanh(t))
     acc[...] = jnp.zeros_like(acc)
-    lab = lab_ref[...]
 
     def gather(group, carry):
-        flux_rows, par_rows = rows_of(flux, group), rows_of(par_ref, group)
+        flux_rows = rows_of(flux, group)
         for q in range(8):
-            mine = lab == par_rows[q : q + 1]
+            at = slice(q * 128, (q + 1) * 128)
             for k, part in enumerate(halves(flux_rows[q : q + 1])):
-                arms[k * LABELS : (k + 1) * LABELS, q * 128 : (q + 1) * 128] = jnp.where(
-                    mine, part.astype(f32), 0.0
-                ).astype(bf16)
-        acc[...] += dot(arms[...], e_ref[group], NT)
+                arms[k * LABELS : (k + 1) * LABELS, at] = who_ref[group, :, at] * part
+        acc[...] += dot(arms[...], e_ref[group, 0:128], NT)
         return carry
 
-    lax.fori_loop(0, GROUPS, gather, 0)
-    both = acc[:, :128] + acc[:, 128:]
+    lax.fori_loop(0, GROUPS, gather, 0, unroll=UNROLL)
+    both = acc[...]
     sums = to_slots(rs_ref[...], both[0:48] + both[48:96])
     for k in range(OWN):
         pay[pl.ds(k, 128, stride=LATER), :] = sums[k * 128 : (k + 1) * 128]
@@ -385,12 +404,13 @@
     pay = ((DEV * LATER, 128), f32)
 
     states = exchange(call(split_kernel, [square], [], *from_hbm(state))[0])
-    table, mb, rinv, lab, rs, m, sums, edges, count, cols, sw = call(
+    table, mb, rinv, lab, rs, m, sums, edges, count, cols, sw, who = call(
         prep_kernel,
         [((GROUPS, 256, WIDE), bf16), cells, cells, ((LABELS, 128), jnp.int32), ((SLOTS, LABELS), bf16),
-         ((SLOTS, SLOTS), bf16), ((SLOTS, 256), f32), square, cells, ((SPEC, SPEC, ETA), f32), ((SPEC, ETA), f32)],
-        [((SLOTS, 128), bf16), square, square, cells, cells, cells, ((4 * LABELS, WIDE), bf16),
-         ((4 * LABELS, 256), f32), ((GROUPS, 256, WIDE), bf16), square, pltpu.SemaphoreType.DMA((GROUPS,))],
+         ((SLOTS, SLOTS), bf16), ((SLOTS, 256), f32), square, cells, ((SPEC, SPEC, ETA), f32), ((SPEC, ETA), f32),
+         ((GROUPS, LABELS, WIDE), bf16)],
+        [square, square, cells, cells, cells, ((4 * LABELS, WIDE), bf16),
+         ((4 * LABELS, 128), f32), ((GROUPS, 256, WIDE), bf16), square, pltpu.SemaphoreType.DMA((GROUPS,))],
         dev, *from_hbm(t0, av, var, mass, bare, par, bp, partners.T, ri, chem, sw), scalars=1, streamed=(0,),
     )
     (sent,) = call(first_pack_kernel, [((DEV * FIRST, 128), f32)], [], states, m, sums, edges)
@@ -403,8 +423,8 @@
     grid = ((6, 32, 128), f32)
     t1, sent = call(
         middle_kernel, [cells, pay],
-        [cells, grid, cells, ((2 * LABELS, WIDE), bf16), ((2 * LABELS, 256), f32), square],
-        got, t0, table, rinv, mb, lab, rs, m, par,
+        [cells, grid, cells, ((2 * LABELS, WIDE), bf16), ((2 * LABELS, 128), f32), square],
+        got, t0, table, rinv, mb, lab, rs, m, par, who,
     )
     got = exchange(sent)
     state, sent = call(

time: 109 us -> 104 us (0.954)
  Pallas kernels: 24.7 us -> 19.1 us
  waiting for transfers between devices: 0.01 us -> 2.03 us
  blocking collectives: 72 us -> 70 us
    pallas_call x7, Pallas kernels: 24.7 us -> 19.1 us  [call(): pl.pallas_call(kernel, out_shape=[pltpu.HBM(*o) if i in away else pltpu.V...]
    all_to_all x1, waiting for transfers between devices: 0.01 us -> 2.03 us  [exchange(): lax.all_to_all(sent, ('gx', 'gy'), 0, 0, tiled=True).reshape(array.shape)]
    all_to_all x4, blocking collectives: 72 us -> 70 us  [exchange(): lax.all_to_all(sent, ('gx', 'gy'), 0, 0, tiled=True).reshape(array.shape)]
  transfers between devices with their start and end apart: 1 -> 1, of which waited for: 0 -> 1; matrix products, arithmetic and copies ran while one was open for 0% -> 0% of each run, Pallas kernels for 9% -> 7%
where the time goes in v3:
time: 104 us; the launch traced here: 103 us
  blocking collectives  70 us (67%)
  Pallas kernels  19.1 us (18%)
  starting transfers between devices  11.5 us (11%)
  waiting for transfers between devices  2.03 us (2%)
    all_to_all x4, blocking collectives, exchange(): lax.all_to_all(sent, ('gx', 'gy'), 0, 0, tiled=True).reshape(array.shape)  70 us
    pallas_call x7, Pallas kernels, call(): pl.pallas_call(kernel, out_shape=[pltpu.HBM(*o) if i in away else pltpu.V...  19.1 us
    all_to_all x1, starting transfers between devices, exchange(): lax.all_to_all(sent, ('gx', 'gy'), 0, 0, tiled=True).reshape(array.shape)  11.5 us
  transfers between devices with their start and end apart: 1, of which 1 were waited for; matrix products, arithmetic and copies ran while one was open for 0% of the time, Pallas kernels for 7%

profile of v3, /device:TPU:1, one launch (start us, length us, event | category | flops | bytes accessed | tf_op | source)
XLA Modules:
  0.0 103.3 jit_solution(3742545783521493861)
XLA Ops:
  0.6 0.0 copy-start.1
  0.6 0.0 copy-start.2
  0.7 1.5 %shard_map.131 = f32[128,128]{1,0:T(8,128)} custom-call(f32[64,128]{1,0:T(8,128)} %bitcast.40), custom_call_target="tpu_custom_call" | custom-call | tf_op jit(solution)/shard_map/pallas_call | solution.py:376
  2.1 11.5 %all-to-all-start = ((f32[128,1,128]{2,1,0:T(1,128)}), f32[128,1,128]{2,1,0:T(1,128)S(1)}, u32[]{:S(2)}, u32[]{:S(2)}) async-start(f32[128,1,128]{2,1,0:T(1,128)} %bitcast.2), calls=%async_computation | async-start | bytes 131072 | tf_op jit(solution)/shard_map/all_to_all | solution.py:389
  13.6 7.6 %shard_map.132 = (bf16[8,256,1024]{2,1,0:T(8,128)(2,1)}, f32[64,128]{1,0:T(8,128)S(1)}, f32[64,128]{1,0:T(8,128)S(1)}, s32[48,128]{1,0:T(8,128)S(1)}, bf16[512,4...) custom-call(s32[1]{0:T(128)} %bitcast.4.dev_ref, ...), custom_call_target="tpu_custom_call" | custom-call | tf_op jit(solution)/shard_map/pallas_call | solution.py:376
  21.2 2.0 %all-to-all-done = f32[128,1,128]{2,1,0:T(1,128)S(1)} async-done(((f32[128,1,128]{2,1,0:T(1,128)}), f32[128,1,128]{2,1,0:T(1,128)S(1)}, u32[]{:S(2)}, u32[]{:S(2)}) %all-to-all-start) | async-done | bytes 65568 | tf_op jit(solution)/shard_map/all_to_all | solution.py:389
  23.2 0.0 copy-start
  23.2 0.5 shard_map.133
  23.8 21.9 %all_to_all.25 = f32[128,1,1152]{2,1,0:T(1,128)S(1)} all-to-all(f32[128,1,1152]{2,1,0:T(1,128)S(1)} %bitcast.26), channel_id=1, replica_groups=mesh['gx'=16,'gy'=8] {'gx','gy'}, dimensions={0} | all-to-all | bytes 1179648 | tf_op jit(solution)/shard_map/all_to_all | solution.py:389
  45.6 2.4 %shard_map.134 = (f32[64,128]{1,0:T(8,128)S(1)}, f32[8,128]{1,0:T(8,128)S(1)}, f32[640,128]{1,0:T(8,128)S(1)}) custom-call(f32[1152,128]{1,0:T(8,128)S(1)} %bitcast.27, f32[64,128]{1,0:T(8,128)} %bitcast.41, f32[64,128]{1,0:T(8,128)S(1)} %get-tuple-element.24.count_ref, f32[16,16,128]{2,1,0:T(8,128)S(1)} %get-tuple-element.25.cols, ...), custom_call_target="tpu_custom_call" | custom-call | tf_op jit(solution)/shard_map/pallas_call | solution.py:376
  48.0 16.2 %all_to_all.26 = f32[128,1,640]{2,1,0:T(1,128)S(1)} all-to-all(f32[128,1,640]{2,1,0:T(1,128)S(1)} %bitcast.33), channel_id=1, replica_groups=mesh['gx'=16,'gy'=8] {'gx','gy'}, dimensions={0} | all-to-all | bytes 655360 | tf_op jit(solution)/shard_map/all_to_all | solution.py:389
  64.2 0.0 copy-done.1
  64.2 0.0 copy-done.2
  64.2 0.0 copy-done
  64.2 3.1 %shard_map.135 = (f32[64,128]{1,0:T(8,128)S(1)}, f32[640,128]{1,0:T(8,128)S(1)}) custom-call(f32[640,128]{1,0:T(8,128)S(1)} %bitcast.28, f32[64,128]{1,0:T(8,128)S(1)} %bitcast.39, bf16[8,256,1024]{2,1,0:T(8,128)(2,1)S(1)} %copy-done, f32[64,128]{1,0:T(8,128)S(1)} %get-tuple-element.29.rinv_ref, f32[64,128]{1,0:T(8,128)S(1)} %get-tuple-element.30.mb_ref, ...), custom_call_target="tpu_custom_call" | custom-call | tf_op jit(solution)/shard_map/pallas_call | solution.py:376
  67.3 16.0 %all_to_all.27 = f32[128,1,640]{2,1,0:T(1,128)S(1)} all-to-all(f32[128,1,640]{2,1,0:T(1,128)S(1)} %bitcast.32), channel_id=1, replica_groups=mesh['gx'=16,'gy'=8] {'gx','gy'}, dimensions={0} | all-to-all | bytes 655360 | tf_op jit(solution)/shard_map/all_to_all | solution.py:389
  83.3 2.2 %shard_map.136 = (f32[64,128]{1,0:T(8,128)}, f32[640,128]{1,0:T(8,128)S(1)}) custom-call(f32[640,128]{1,0:T(8,128)S(1)} %bitcast.30, f32[64,128]{1,0:T(8,128)S(1)} %get-tuple-element.35.state_ref, f32[8,128]{1,0:T(8,128)S(1)} %get-tuple-element.36.mass_ref, f32[64,128]{1,0:T(8,128)S(1)} %get-tuple-element.24.count_ref, ...), custom_call_target="tpu_custom_call" | custom-call | tf_op jit(solution)/shard_map/pallas_call | solution.py:376
  85.5 16.0 %all_to_all.28 = f32[128,1,640]{2,1,0:T(1,128)S(1)} all-to-all(f32[128,1,640]{2,1,0:T(1,128)S(1)} %bitcast.31), channel_id=1, replica_groups=mesh['gx'=16,'gy'=8] {'gx','gy'}, dimensions={0} | all-to-all | bytes 655360 | tf_op jit(solution)/shard_map/all_to_all | solution.py:389
  101.4 1.9 %shard_map.137 = f32[64,128]{1,0:T(8,128)} custom-call(f32[640,128]{1,0:T(8,128)S(1)} %bitcast.29, f32[64,128]{1,0:T(8,128)S(1)} %get-tuple-element.39.t_ref, bf16[8,256,1024]{2,1,0:T(8,128)(2,1)S(1)} %copy-done, f32[64,128]{1,0:T(8,128)S(1)} %get-tuple-element.29.rinv_ref, s32[48,128]{1,0:T(8,128)S(1)} %get-tuple-element.31.lab_ref, ...), custom_call_target="tpu_custom_call" | custom-call | tf_op jit(solution)/shard_map/pallas_call | solution.py:376
Async XLA Ops:
  0.6 63.6 %copy-start.1 = (s32[4,16,128]{2,1,0:T(8,128)S(1)}, s32[4,16,128]{2,1,0:T(8,128)}, u32[]{:S(2)}) copy-start(s32[4,16,128]{2,1,0:T(8,128)} %param.17) | copy-start | bytes 98308
  0.6 63.6 %copy-start.2 = (f32[4,16,128]{2,1,0:T(8,128)S(1)}, f32[4,16,128]{2,1,0:T(8,128)}, u32[]{:S(2)}) copy-start(f32[4,16,128]{2,1,0:T(8,128)} %param.12) | copy-start | bytes 98308
  2.1 21.1 %all-to-all-start = ((f32[128,1,128]{2,1,0:T(1,128)}), f32[128,1,128]{2,1,0:T(1,128)S(1)}, u32[]{:S(2)}, u32[]{:S(2)}) async-start(f32[128,1,128]{2,1,0:T(1,128)} %bitcast.2), calls=%async_computation | async-start | bytes 131072 | tf_op jit(solution)/shard_map/all_to_all | solution.py:389
  23.2 41.0 %copy-start = (bf16[8,256,1024]{2,1,0:T(8,128)(2,1)S(1)}, bf16[8,256,1024]{2,1,0:T(8,128)(2,1)}, u32[]{:S(2)}) copy-start(bf16[8,256,1024]{2,1,0:T(8,128)(2,1)} %get-tuple-element.28.e_ref) | copy-start | bytes 12582916

commit v4 on v3

--- a/solution.py
+++ b/solution.py
@@ -17,7 +17,7 @@
 WIDE = 1024
 FIRST = 9
 LATER = 5
-UNROLL = 4
+UNROLL = 8
 LOG2E = 1.4426950408889634
 
 coupling = 0.05
@@ -211,12 +211,8 @@
     return edge[...].T
 
 
-def split_kernel(state_ref, out_ref):
-    out_ref[...] = jnp.concatenate([state_ref[...], jnp.zeros((128 - ROWS, ETA), f32)], axis=0).T
-
-
 def first_pack_kernel(got_ref, m_ref, sums_ref, edge_ref, out_ref):
-    misc = neighbour_sums(got_ref[...], m_ref[...]) + edge_ref[...]
+    misc = neighbour_sums(jnp.concatenate([got_ref[...], jnp.zeros((128, 128 - ROWS), f32)], axis=1), m_ref[...]) + edge_ref[...]
     for t in range(OWN):
         out_ref[pl.ds(t, 128, stride=FIRST), :] = sums_ref[t * 128 : (t + 1) * 128, 0:128]
         out_ref[pl.ds(OWN + t, 128, stride=FIRST), :] = sums_ref[t * 128 : (t + 1) * 128, 128:256]
@@ -403,7 +399,7 @@
     square = ((128, 128), f32)
     pay = ((DEV * LATER, 128), f32)
 
-    states = exchange(call(split_kernel, [square], [], *from_hbm(state))[0])
+    states = lax.all_to_all(state.T.reshape(DEV, 1, ROWS), ("gx", "gy"), 0, 0, tiled=True).reshape(DEV, ROWS)
     table, mb, rinv, lab, rs, m, sums, edges, count, cols, sw, who = call(
         prep_kernel,
         [((GROUPS, 256, WIDE), bf16), cells, cells, ((LABELS, 128), jnp.int32), ((SLOTS, LABELS), bf16),

time: 104 us -> 102 us (0.981)
  Pallas kernels: 19.1 us -> 16.3 us
  local copies, waits for them, and re-layouts: 0.02 us -> 1.5 us
    pallas_call x7 -> x6, Pallas kernels: 19.1 us -> 16.3 us  [call(): pl.pallas_call(kernel, out_shape=[pltpu.HBM(*o) if i in away else pltpu.V...]
    reshape x0 -> x1, local copies, waits for them, and re-layouts: none -> 1.48 us  [shards(): state.T.reshape(DEV, 1, ROWS)]
where the time goes in v4:
time: 102 us
  blocking collectives  69.2 us (68%)
  Pallas kernels  16.3 us (16%)
  starting transfers between devices  11.5 us (11%)
  waiting for transfers between devices  2.85 us (3%)
  local copies, waits for them, and re-layouts  1.5 us (1%)
    all_to_all x4, blocking collectives, exchange(): lax.all_to_all(sent, ('gx', 'gy'), 0, 0, tiled=True).reshape(array.shape)  69.2 us
    pallas_call x6, Pallas kernels, call(): pl.pallas_call(kernel, out_shape=[pltpu.HBM(*o) if i in away else pltpu.V...  16.3 us
    all_to_all x1, starting transfers between devices, shards(): lax.all_to_all(state.T.reshape(DEV, 1, ROWS), ('gx', 'gy'), 0, 0, tiled=T...  11.5 us
    all_to_all x1, waiting for transfers between devices, shards(): lax.all_to_all(state.T.reshape(DEV, 1, ROWS), ('gx', 'gy'), 0, 0, tiled=T...  2.85 us
  transfers between devices with their start and end apart: 1, of which 1 were waited for; matrix products, arithmetic and copies ran while one was open for 0% of the time, Pallas kernels for 7%

profile of v4, /device:TPU:1, one launch (start us, length us, event | category | flops | bytes accessed | tf_op | source)
XLA Modules:
  0.0 102.0 jit_solution(12890759129709819214)
XLA Ops:
  0.6 0.0 copy-start.1
  0.6 0.0 copy-start.2
  0.7 1.5 %copy.15 = f32[128,1,64]{2,1,0:T(1,128)} copy(f32[128,1,64]{0,2,1:T(8,128)} %bitcast.41) | data formatting | bytes 65536 | tf_op jit(solution)/shard_map/reshape | solution.py:402
  2.1 11.5 %all-to-all-start = ((f32[128,1,64]{2,1,0:T(1,128)}), f32[128,1,64]{2,1,0:T(1,128)S(1)}, u32[]{:S(2)}, u32[]{:S(2)}) async-start(f32[128,1,64]{2,1,0:T(1,128)} %copy.15), calls=%async_computation | async-start | bytes 131072 | tf_op jit(solution)/shard_map/all_to_all | solution.py:402
  13.6 6.7 %shard_map.131 = (bf16[8,256,1024]{2,1,0:T(8,128)(2,1)}, f32[64,128]{1,0:T(8,128)S(1)}, f32[64,128]{1,0:T(8,128)S(1)}, s32[48,128]{1,0:T(8,128)S(1)}, bf16[512,4...) custom-call(s32[1]{0:T(128)} %bitcast.4.dev_ref, ...), custom_call_target="tpu_custom_call" | custom-call | tf_op jit(solution)/shard_map/pallas_call | solution.py:372
  20.4 2.8 %all-to-all-done = f32[128,1,64]{2,1,0:T(1,128)S(1)} async-done(((f32[128,1,64]{2,1,0:T(1,128)}), f32[128,1,64]{2,1,0:T(1,128)S(1)}, u32[]{:S(2)}, u32[]{:S(2)}) %all-to-all-start) | async-done | bytes 32800 | tf_op jit(solution)/shard_map/all_to_all | solution.py:402
  23.2 0.0 copy-start
  23.2 0.5 shard_map.132
  23.8 21.1 %all_to_all.25 = f32[128,1,1152]{2,1,0:T(1,128)S(1)} all-to-all(f32[128,1,1152]{2,1,0:T(1,128)S(1)} %bitcast.27), channel_id=1, replica_groups=mesh['gx'=16,'gy'=8] {'gx','gy'}, dimensions={0} | all-to-all | bytes 1179648 | tf_op jit(solution)/shard_map/all_to_all | solution.py:385
  44.8 2.4 %shard_map.133 = (f32[64,128]{1,0:T(8,128)S(1)}, f32[8,128]{1,0:T(8,128)S(1)}, f32[640,128]{1,0:T(8,128)S(1)}) custom-call(f32[1152,128]{1,0:T(8,128)S(1)} %bitcast.28, f32[64,128]{1,0:T(8,128)} %bitcast.42, f32[64,128]{1,0:T(8,128)S(1)} %get-tuple-element.24.count_ref, f32[16,16,128]{2,1,0:T(8,128)S(1)} %get-tuple-element.25.cols, ...), custom_call_target="tpu_custom_call" | custom-call | tf_op jit(solution)/shard_map/pallas_call | solution.py:372
  47.2 16.2 %all_to_all.26 = f32[128,1,640]{2,1,0:T(1,128)S(1)} all-to-all(f32[128,1,640]{2,1,0:T(1,128)S(1)} %bitcast.34), channel_id=1, replica_groups=mesh['gx'=16,'gy'=8] {'gx','gy'}, dimensions={0} | all-to-all | bytes 655360 | tf_op jit(solution)/shard_map/all_to_all | solution.py:385
  63.4 0.0 copy-done.1
  63.4 0.0 copy-done.2
  63.4 0.0 copy-done
  63.4 2.9 %shard_map.134 = (f32[64,128]{1,0:T(8,128)S(1)}, f32[640,128]{1,0:T(8,128)S(1)}) custom-call(f32[640,128]{1,0:T(8,128)S(1)} %bitcast.29, f32[64,128]{1,0:T(8,128)S(1)} %bitcast.40, bf16[8,256,1024]{2,1,0:T(8,128)(2,1)S(1)} %copy-done, f32[64,128]{1,0:T(8,128)S(1)} %get-tuple-element.29.rinv_ref, f32[64,128]{1,0:T(8,128)S(1)} %get-tuple-element.30.mb_ref, ...), custom_call_target="tpu_custom_call" | custom-call | tf_op jit(solution)/shard_map/pallas_call | solution.py:372
  66.3 16.0 %all_to_all.27 = f32[128,1,640]{2,1,0:T(1,128)S(1)} all-to-all(f32[128,1,640]{2,1,0:T(1,128)S(1)} %bitcast.33), channel_id=1, replica_groups=mesh['gx'=16,'gy'=8] {'gx','gy'}, dimensions={0} | all-to-all | bytes 655360 | tf_op jit(solution)/shard_map/all_to_all | solution.py:385
  82.2 2.2 %shard_map.135 = (f32[64,128]{1,0:T(8,128)}, f32[640,128]{1,0:T(8,128)S(1)}) custom-call(f32[640,128]{1,0:T(8,128)S(1)} %bitcast.31, f32[64,128]{1,0:T(8,128)S(1)} %get-tuple-element.35.state_ref, f32[8,128]{1,0:T(8,128)S(1)} %get-tuple-element.36.mass_ref, f32[64,128]{1,0:T(8,128)S(1)} %get-tuple-element.24.count_ref, ...), custom_call_target="tpu_custom_call" | custom-call | tf_op jit(solution)/shard_map/pallas_call | solution.py:372
  84.4 16.0 %all_to_all.28 = f32[128,1,640]{2,1,0:T(1,128)S(1)} all-to-all(f32[128,1,640]{2,1,0:T(1,128)S(1)} %bitcast.32), channel_id=1, replica_groups=mesh['gx'=16,'gy'=8] {'gx','gy'}, dimensions={0} | all-to-all | bytes 655360 | tf_op jit(solution)/shard_map/all_to_all | solution.py:385
  100.4 1.7 %shard_map.136 = f32[64,128]{1,0:T(8,128)} custom-call(f32[640,128]{1,0:T(8,128)S(1)} %bitcast.30, f32[64,128]{1,0:T(8,128)S(1)} %get-tuple-element.39.t_ref, bf16[8,256,1024]{2,1,0:T(8,128)(2,1)S(1)} %copy-done, f32[64,128]{1,0:T(8,128)S(1)} %get-tuple-element.29.rinv_ref, s32[48,128]{1,0:T(8,128)S(1)} %get-tuple-element.31.lab_ref, ...), custom_call_target="tpu_custom_call" | custom-call | tf_op jit(solution)/shard_map/pallas_call | solution.py:372
Async XLA Ops:
  0.6 62.8 %copy-start.1 = (s32[4,16,128]{2,1,0:T(8,128)S(1)}, s32[4,16,128]{2,1,0:T(8,128)}, u32[]{:S(2)}) copy-start(s32[4,16,128]{2,1,0:T(8,128)} %param.17) | copy-start | bytes 98308
  0.6 62.8 %copy-start.2 = (f32[4,16,128]{2,1,0:T(8,128)S(1)}, f32[4,16,128]{2,1,0:T(8,128)}, u32[]{:S(2)}) copy-start(f32[4,16,128]{2,1,0:T(8,128)} %param.12) | copy-start | bytes 98308
  2.1 21.1 %all-to-all-start = ((f32[128,1,64]{2,1,0:T(1,128)}), f32[128,1,64]{2,1,0:T(1,128)S(1)}, u32[]{:S(2)}, u32[]{:S(2)}) async-start(f32[128,1,64]{2,1,0:T(1,128)} %copy.15), calls=%async_computation | async-start | bytes 131072 | tf_op jit(solution)/shard_map/all_to_all | solution.py:402
  23.2 40.2 %copy-start = (bf16[8,256,1024]{2,1,0:T(8,128)(2,1)S(1)}, bf16[8,256,1024]{2,1,0:T(8,128)(2,1)}, u32[]{:S(2)}) copy-start(bf16[8,256,1024]{2,1,0:T(8,128)(2,1)} %get-tuple-element.28.e_ref) | copy-start | bytes 12582916

commit v5 on v4

--- a/solution.py
+++ b/solution.py
@@ -18,6 +18,7 @@
 FIRST = 9
 LATER = 5
 UNROLL = 8
+SUBROLL = 4
 LOG2E = 1.4426950408889634
 
 coupling = 0.05
@@ -48,13 +49,6 @@
     return high, (x - high.astype(f32)).astype(bf16)
 
 
-def thirds(x):
-    high = x.astype(bf16)
-    rest = x - high.astype(f32)
-    mid = rest.astype(bf16)
-    return high, mid, (rest - mid.astype(f32)).astype(bf16)
-
-
 def hot(mask):
     return jnp.where(mask, 1.0, 0.0).astype(bf16)
 
@@ -63,6 +57,10 @@
     return jnp.where(mask, jnp.ones((), bf16), jnp.zeros((), bf16))
 
 
+def together(ref, group, count):
+    return jnp.concatenate([ref[group * 8 + q, 0:count, :] for q in range(8)], axis=1)
+
+
 def rows_of(ref, group):
     return ref[pl.ds(pl.multiple_of(group * 8, 8), 8), :]
 
@@ -72,14 +70,14 @@
 
 
 def to_slots(rs, sums):
-    high, mid, low = thirds(sums)
-    return dot(rs, high, NN) + dot(rs, mid, NN) + dot(rs, low, NN)
+    both = dot(rs, jnp.concatenate(halves(sums), axis=1), NN)
+    return both[:, : sums.shape[1]] + both[:, sums.shape[1] :]
 
 
 def prep_kernel(
     dev_ref, t_ref, av_ref, var_ref, mass_ref, bare_ref, par_ref, bp_ref, fp_ref, ri_ref, c_ref, sw_ref,
     e_out, mb_ref, rinv_ref, lab_ref, rs_ref, m_ref, sums_ref, edge_ref, count_ref, cols, weight_ref, who_ref,
-    le, l1e, a1, b1, chi, arms, acc, e_ref, edge, sems,
+    le, l1e, a1, b1, chi, acc, e_ref, edge, sems,
 ):
     edge_ref[...] = edges_by_z(t_ref, edge)
     for s in range(SPEC):
@@ -155,27 +153,25 @@
     def tables(group, carry):
         a_rows, b_rows = rows_of(a1, group), rows_of(b1, group)
         chi_rows, mass_rows, par_rows = rows_of(chi, group), rows_of(mass_ref, group), rows_of(par_ref, group)
-        inverse, mass_over = [], []
+        inverse, mass_over, arms = [], [], []
         for q in range(8):
-            at = slice(q * 128, (q + 1) * 128)
             logits = a_rows[q : q + 1] * le[...] + b_rows[q : q + 1] * l1e[...]
             table = jnp.exp2(logits - jnp.max(logits, axis=0, keepdims=True))
             r = 1.0 / jnp.sum(table, axis=0, keepdims=True)
             high, low = halves(table)
-            e_ref[group, 0:128, at] = high
-            e_ref[group, 128:256, at] = low
+            e_ref[group * 8 + q, 0:128, :] = high
+            e_ref[group * 8 + q, 128:256, :] = low
             w = mass_rows[q : q + 1] * r
             n = w * chi_rows[q : q + 1]
             inverse.append(r)
             mass_over.append(w)
             mine = hot(lab == par_rows[q : q + 1])
-            who_ref[group, :, at] = mine
-            for k, part in enumerate((*halves(w), *halves(n))):
-                arms[k * LABELS : (k + 1) * LABELS, at] = mine * part
+            who_ref[group * 8 + q] = mine
+            arms.append(jnp.concatenate([mine * part for part in (*halves(w), *halves(n))], axis=0))
         put_rows(rinv_ref, group, inverse)
         put_rows(mb_ref, group, [jnp.concatenate(mass_over, axis=0) * rows_of(bare_ref, group)])
-        pltpu.make_async_copy(e_ref.at[group], e_out.at[group], sems.at[group]).start()
-        acc[...] += dot(arms[...], e_ref[group, 0:128], NT)
+        pltpu.make_async_copy(e_ref.at[pl.ds(group * 8, 8)], e_out.at[pl.ds(group * 8, 8)], sems.at[group]).start()
+        acc[...] += dot(jnp.concatenate(arms, axis=1), together(e_ref, group, 128), NT)
         return carry
 
     lax.fori_loop(0, GROUPS, tables, 0, unroll=UNROLL)
@@ -184,7 +180,7 @@
     n48 = both[96:144] + both[144:192]
     sums_ref[...] = to_slots(rs, jnp.concatenate([w48, n48], axis=1))
     for group in range(GROUPS):
-        pltpu.make_async_copy(e_ref.at[group], e_out.at[group], sems.at[group]).wait()
+        pltpu.make_async_copy(e_ref.at[pl.ds(group * 8, 8)], e_out.at[pl.ds(group * 8, 8)], sems.at[group]).wait()
 
 
 def neighbour_sums(part, m):
@@ -228,7 +224,7 @@
     return jnp.where((lane >= 100) & (lane < 104) & (gy > 0), pltpu.roll(misc, 1, 0), out)
 
 
-def advance(state_ref, misc, cchi, count_ref, cols, weight_ref, out_ref, last):
+def advance(state_ref, misc, cchi, count_ref, cols, weight_ref, speed_ref, out_ref, last):
     count = count_ref[...]
     fraction = 1.0 / count
     mixing = fraction * mixing_rate * jnp.concatenate(
@@ -238,23 +234,30 @@
     near = misc.T[:ROWS]
     state = state_ref[...]
     state = state + coupling * (near - 6.0 * state)
-    lane = iota((ROWS, ETA), 1)
-
-    def substep(index, current):
-        speed = jnp.tanh(current)
-        source = []
+    lane = iota((8, ETA), 1)
+    pieces = [slice(p * 8, (p + 1) * 8) for p in range(8)]
+
+    def substep(index, states):
+        for p, current in enumerate(states):
+            speed_ref[pieces[p]] = jnp.tanh(current)
+        out = list(states)
         for t in range(OWN):
-            parts = [speed[t * SPEC + s : t * SPEC + s + 1] * cols[s] for s in range(SPEC)]
-            while len(parts) > 1:
-                parts = [a + b for a, b in zip(parts[::2], parts[1::2])]
-            source.append(parts[0])
-        source = jnp.concatenate(source, axis=0)
-        left = jnp.where(lane == 0, current, pltpu.roll(current, 1, 1))
-        right = jnp.where(lane == ETA - 1, current, pltpu.roll(current, ETA - 1, 1))
-        update = mixing * (right - 2.0 * current + left) + reacting * source
-        return jnp.where(index.astype(f32) < count, current + update, current)
-
-    state = lax.fori_loop(0, SUBMAX, substep, state)
+            speed = [speed_ref[pl.ds(t * SPEC + s, 8, stride=0), :] for s in range(SPEC)]
+            for half in range(2):
+                p = 2 * t + half
+                current = states[p]
+                parts = [speed[s] * cols[s, half * 8 : half * 8 + 8] for s in range(SPEC)]
+                while len(parts) > 1:
+                    parts = [a + b for a, b in zip(parts[::2], parts[1::2])]
+                left = jnp.where(lane == 0, current, pltpu.roll(current, 1, 1))
+                right = jnp.where(lane == ETA - 1, current, pltpu.roll(current, ETA - 1, 1))
+                update = mixing[pieces[p]] * (right - 2.0 * current + left) + reacting[pieces[p]] * parts[0]
+                out[p] = jnp.where(index.astype(f32) < count[pieces[p]], current + update, current)
+        return tuple(out)
+
+    state = jnp.concatenate(
+        lax.fori_loop(0, SUBMAX, substep, tuple(state[p] for p in pieces), unroll=SUBROLL), axis=0
+    )
     state_ref_out, pay = out_ref
     state_ref_out[...] = state
     weight = weight_ref[...]
@@ -272,7 +275,7 @@
 
 
 def first_advance_kernel(
-    got_ref, state_ref, count_ref, cols, weight_ref, state_out, weight_out, pay
+    got_ref, state_ref, count_ref, cols, weight_ref, state_out, weight_out, pay, speed_ref
 ):
     cchi = []
     for t in range(OWN):
@@ -281,18 +284,18 @@
         weight_out[t : t + 1, :] = w
         cchi.append((n + prior_flux) / (w + prior_weight))
     misc = got_ref[pl.ds(2 * OWN, 128, stride=FIRST), :]
-    advance(state_ref, misc, cchi, count_ref, cols, weight_ref, (state_out, pay), False)
+    advance(state_ref, misc, cchi, count_ref, cols, weight_ref, speed_ref, (state_out, pay), False)
 
 
 def later_advance_kernel(
-    got_ref, state_ref, mass_ref, count_ref, cols, weight_ref, state_out, pay
+    got_ref, state_ref, mass_ref, count_ref, cols, weight_ref, state_out, pay, speed_ref
 ):
     cchi = []
     for t in range(OWN):
         n = total_of(got_ref, t, LATER)
         cchi.append((n + prior_flux) / (mass_ref[t : t + 1, :] + prior_weight))
     misc = got_ref[pl.ds(OWN, 128, stride=LATER), :]
-    advance(state_ref, misc, cchi, count_ref, cols, weight_ref, (state_out, pay), True)
+    advance(state_ref, misc, cchi, count_ref, cols, weight_ref, speed_ref, (state_out, pay), True)
 
 
 def fine_update(got_ref, misc, t_ref, e_ref, rinv_ref, lab_ref, rs_ref, par_ref, tfine, grid):
@@ -305,7 +308,7 @@
     lab = lab_ref[...]
 
     def weigh(group, carry):
-        means = dot(rows, e_ref[group], NN)
+        means = dot(rows, together(e_ref, group, 256), NN)
         means = means[:LABELS] + means[LABELS:]
         par_rows, inverse = rows_of(par_ref, group), rows_of(rinv_ref, group)
         out = []
@@ -335,7 +338,7 @@
 
 def middle_kernel(
     got_ref, t_ref, e_ref, rinv_ref, mb_ref, lab_ref, rs_ref, m_ref, par_ref, who_ref,
-    t_out, pay, tfine, grid, flux, arms, acc, edge,
+    t_out, pay, tfine, grid, flux, acc, edge,
 ):
     misc = got_ref[pl.ds(OWN, 128, stride=LATER), :]
     t = fine_update(got_ref, misc, t_ref, e_ref, rinv_ref, lab_ref, rs_ref, par_ref, tfine, grid)
@@ -345,11 +348,11 @@
 
     def gather(group, carry):
         flux_rows = rows_of(flux, group)
+        arms = []
         for q in range(8):
-            at = slice(q * 128, (q + 1) * 128)
-            for k, part in enumerate(halves(flux_rows[q : q + 1])):
-                arms[k * LABELS : (k + 1) * LABELS, at] = who_ref[group, :, at] * part
-        acc[...] += dot(arms[...], e_ref[group, 0:128], NT)
+            mine = who_ref[group * 8 + q]
+            arms.append(jnp.concatenate([mine * part for part in halves(flux_rows[q : q + 1])], axis=0))
+        acc[...] += dot(jnp.concatenate(arms, axis=1), together(e_ref, group, 128), NT)
         return carry
 
     lax.fori_loop(0, GROUPS, gather, 0, unroll=UNROLL)
@@ -402,29 +405,28 @@
     states = lax.all_to_all(state.T.reshape(DEV, 1, ROWS), ("gx", "gy"), 0, 0, tiled=True).reshape(DEV, ROWS)
     table, mb, rinv, lab, rs, m, sums, edges, count, cols, sw, who = call(
         prep_kernel,
-        [((GROUPS, 256, WIDE), bf16), cells, cells, ((LABELS, 128), jnp.int32), ((SLOTS, LABELS), bf16),
+        [((ROWS, 256, 128), bf16), cells, cells, ((LABELS, 128), jnp.int32), ((SLOTS, LABELS), bf16),
          ((SLOTS, SLOTS), bf16), ((SLOTS, 256), f32), square, cells, ((SPEC, SPEC, ETA), f32), ((SPEC, ETA), f32),
-         ((GROUPS, LABELS, WIDE), bf16)],
-        [square, square, cells, cells, cells, ((4 * LABELS, WIDE), bf16),
-         ((4 * LABELS, 128), f32), ((GROUPS, 256, WIDE), bf16), square, pltpu.SemaphoreType.DMA((GROUPS,))],
+         ((ROWS, LABELS, 128), bf16)],
+        [square, square, cells, cells, cells, ((4 * LABELS, 128), f32), ((ROWS, 256, 128), bf16), square, pltpu.SemaphoreType.DMA((GROUPS,))],
         dev, *from_hbm(t0, av, var, mass, bare, par, bp, partners.T, ri, chem, sw), scalars=1, streamed=(0,),
     )
     (sent,) = call(first_pack_kernel, [((DEV * FIRST, 128), f32)], [], states, m, sums, edges)
     got = exchange(sent)
     state, own_weight, sent = call(
-        first_advance_kernel, [((ROWS, ETA), f32), ((8, 128), f32), pay], [],
+        first_advance_kernel, [((ROWS, ETA), f32), ((8, 128), f32), pay], [cells],
         got, *from_hbm(state), count, cols, sw,
     )
     got = exchange(sent)
     grid = ((6, 32, 128), f32)
     t1, sent = call(
         middle_kernel, [cells, pay],
-        [cells, grid, cells, ((2 * LABELS, WIDE), bf16), ((2 * LABELS, 128), f32), square],
+        [cells, grid, cells, ((2 * LABELS, 128), f32), square],
         got, t0, table, rinv, mb, lab, rs, m, par, who,
     )
     got = exchange(sent)
     state, sent = call(
-        later_advance_kernel, [((ROWS, ETA), f32), pay], [],
+        later_advance_kernel, [((ROWS, ETA), f32), pay], [cells],
         got, state, own_weight, count, cols, sw, results=(0,),
     )
     got = exchange(sent)

time: 102 us -> 101 us (level)
  Pallas kernels: 16.3 us -> 14.7 us
  blocking collectives: 69.2 us -> 67.9 us
  waiting for transfers between devices: 2.85 us -> 4.1 us
    pallas_call x6, Pallas kernels: 16.3 us -> 14.7 us  [call(): pl.pallas_call(kernel, out_shape=[pltpu.HBM(*o) if i in away else pltpu.V...]
    all_to_all x4, blocking collectives: 69.2 us -> 67.9 us  [exchange(): lax.all_to_all(sent, ('gx', 'gy'), 0, 0, tiled=True).reshape(array.shape)]
    all_to_all x1, waiting for transfers between devices: 2.85 us -> 4.1 us  [shards(): lax.all_to_all(state.T.reshape(DEV, 1, ROWS), ('gx', 'gy'), 0, 0, tiled=T...]
  transfers between devices with their start and end apart: 1 -> 1, of which waited for: 1 -> 1; matrix products, arithmetic and copies ran while one was open for 0% -> 0% of each run, Pallas kernels for 7% -> 5%
where the time goes in v5:
time: 101 us; the launch traced here: 100 us
  blocking collectives  67.9 us (67%)
  Pallas kernels  14.7 us (15%)
  starting transfers between devices  11.5 us (11%)
  waiting for transfers between devices  4.1 us (4%)
  local copies, waits for them, and re-layouts  1.5 us (1%)
    all_to_all x4, blocking collectives, exchange(): lax.all_to_all(sent, ('gx', 'gy'), 0, 0, tiled=True).reshape(array.shape)  67.9 us
    pallas_call x6, Pallas kernels, call(): pl.pallas_call(kernel, out_shape=[pltpu.HBM(*o) if i in away else pltpu.V...  14.7 us
    all_to_all x1, starting transfers between devices, shards(): lax.all_to_all(state.T.reshape(DEV, 1, ROWS), ('gx', 'gy'), 0, 0, tiled=T...  11.5 us
    all_to_all x1, waiting for transfers between devices, shards(): lax.all_to_all(state.T.reshape(DEV, 1, ROWS), ('gx', 'gy'), 0, 0, tiled=T...  4.1 us
  transfers between devices with their start and end apart: 1, of which 1 were waited for; matrix products, arithmetic and copies ran while one was open for 0% of the time, Pallas kernels for 5%

profile of v5, /device:TPU:1, one launch (start us, length us, event | category | flops | bytes accessed | tf_op | source)
XLA Modules:
  0.0 100.4 jit_solution(12386923354149565309)
XLA Ops:
  0.6 0.0 copy-start.1
  0.6 0.0 copy-start.2
  0.7 1.5 %copy.15 = f32[128,1,64]{2,1,0:T(1,128)} copy(f32[128,1,64]{0,2,1:T(8,128)} %bitcast.41) | data formatting | bytes 65536 | tf_op jit(solution)/shard_map/reshape | solution.py:405
  2.1 11.5 %all-to-all-start = ((f32[128,1,64]{2,1,0:T(1,128)}), f32[128,1,64]{2,1,0:T(1,128)S(1)}, u32[]{:S(2)}, u32[]{:S(2)}) async-start(f32[128,1,64]{2,1,0:T(1,128)} %copy.15), calls=%async_computation | async-start | bytes 131072 | tf_op jit(solution)/shard_map/all_to_all | solution.py:405
  13.6 5.5 %shard_map.131 = (bf16[64,256,128]{2,1,0:T(8,128)(2,1)}, f32[64,128]{1,0:T(8,128)S(1)}, f32[64,128]{1,0:T(8,128)S(1)}, s32[48,128]{1,0:T(8,128)S(1)}, bf16[512,4...) custom-call(s32[1]{0:T(128)} %bitcast.4.dev_ref, ...), custom_call_target="tpu_custom_call" | custom-call | tf_op jit(solution)/shard_map/pallas_call | solution.py:375
  19.1 4.1 %all-to-all-done = f32[128,1,64]{2,1,0:T(1,128)S(1)} async-done(((f32[128,1,64]{2,1,0:T(1,128)}), f32[128,1,64]{2,1,0:T(1,128)S(1)}, u32[]{:S(2)}, u32[]{:S(2)}) %all-to-all-start) | async-done | bytes 32800 | tf_op jit(solution)/shard_map/all_to_all | solution.py:405
  23.2 0.0 copy-start
  23.2 0.5 shard_map.132
  23.8 19.8 %all_to_all.25 = f32[128,1,1152]{2,1,0:T(1,128)S(1)} all-to-all(f32[128,1,1152]{2,1,0:T(1,128)S(1)} %bitcast.27), channel_id=1, replica_groups=mesh['gx'=16,'gy'=8] {'gx','gy'}, dimensions={0} | all-to-all | bytes 1179648 | tf_op jit(solution)/shard_map/all_to_all | solution.py:388
  43.6 2.3 %shard_map.133 = (f32[64,128]{1,0:T(8,128)S(1)}, f32[8,128]{1,0:T(8,128)S(1)}, f32[640,128]{1,0:T(8,128)S(1)}) custom-call(f32[1152,128]{1,0:T(8,128)S(1)} %bitcast.28, f32[64,128]{1,0:T(8,128)} %bitcast.42, f32[64,128]{1,0:T(8,128)S(1)} %get-tuple-element.24.count_ref, f32[16,16,128]{2,1,0:T(8,128)S(1)} %get-tuple-element.25.cols, ...), custom_call_target="tpu_custom_call" | custom-call | tf_op jit(solution)/shard_map/pallas_call | solution.py:375
  45.9 16.2 %all_to_all.26 = f32[128,1,640]{2,1,0:T(1,128)S(1)} all-to-all(f32[128,1,640]{2,1,0:T(1,128)S(1)} %bitcast.34), channel_id=1, replica_groups=mesh['gx'=16,'gy'=8] {'gx','gy'}, dimensions={0} | all-to-all | bytes 655360 | tf_op jit(solution)/shard_map/all_to_all | solution.py:388
  62.0 0.0 copy-done.1
  62.1 0.0 copy-done.2
  62.1 0.0 copy-done
  62.1 2.6 %shard_map.134 = (f32[64,128]{1,0:T(8,128)S(1)}, f32[640,128]{1,0:T(8,128)S(1)}) custom-call(f32[640,128]{1,0:T(8,128)S(1)} %bitcast.29, f32[64,128]{1,0:T(8,128)S(1)} %bitcast.40, bf16[64,256,128]{2,1,0:T(8,128)(2,1)S(1)} %copy-done, f32[64,128]{1,0:T(8,128)S(1)} %get-tuple-element.29.rinv_ref, f32[64,128]{1,0:T(8,128)S(1)} %get-tuple-element.30.mb_ref, ...), custom_call_target="tpu_custom_call" | custom-call | tf_op jit(solution)/shard_map/pallas_call | solution.py:375
  64.7 16.0 %all_to_all.27 = f32[128,1,640]{2,1,0:T(1,128)S(1)} all-to-all(f32[128,1,640]{2,1,0:T(1,128)S(1)} %bitcast.33), channel_id=1, replica_groups=mesh['gx'=16,'gy'=8] {'gx','gy'}, dimensions={0} | all-to-all | bytes 655360 | tf_op jit(solution)/shard_map/all_to_all | solution.py:388
  80.7 2.1 %shard_map.135 = (f32[64,128]{1,0:T(8,128)}, f32[640,128]{1,0:T(8,128)S(1)}) custom-call(f32[640,128]{1,0:T(8,128)S(1)} %bitcast.31, f32[64,128]{1,0:T(8,128)S(1)} %get-tuple-element.35.state_ref, f32[8,128]{1,0:T(8,128)S(1)} %get-tuple-element.36.mass_ref, f32[64,128]{1,0:T(8,128)S(1)} %get-tuple-element.24.count_ref, ...), custom_call_target="tpu_custom_call" | custom-call | tf_op jit(solution)/shard_map/pallas_call | solution.py:375
  82.7 16.0 %all_to_all.28 = f32[128,1,640]{2,1,0:T(1,128)S(1)} all-to-all(f32[128,1,640]{2,1,0:T(1,128)S(1)} %bitcast.32), channel_id=1, replica_groups=mesh['gx'=16,'gy'=8] {'gx','gy'}, dimensions={0} | all-to-all | bytes 655360 | tf_op jit(solution)/shard_map/all_to_all | solution.py:388
  98.7 1.7 %shard_map.136 = f32[64,128]{1,0:T(8,128)} custom-call(f32[640,128]{1,0:T(8,128)S(1)} %bitcast.30, f32[64,128]{1,0:T(8,128)S(1)} %get-tuple-element.39.t_ref, bf16[64,256,128]{2,1,0:T(8,128)(2,1)S(1)} %copy-done, f32[64,128]{1,0:T(8,128)S(1)} %get-tuple-element.29.rinv_ref, s32[48,128]{1,0:T(8,128)S(1)} %get-tuple-element.31.lab_ref, ...), custom_call_target="tpu_custom_call" | custom-call | tf_op jit(solution)/shard_map/pallas_call | solution.py:375
Async XLA Ops:
  0.6 61.4 %copy-start.1 = (s32[4,16,128]{2,1,0:T(8,128)S(1)}, s32[4,16,128]{2,1,0:T(8,128)}, u32[]{:S(2)}) copy-start(s32[4,16,128]{2,1,0:T(8,128)} %param.17) | copy-start | bytes 98308
  0.6 61.4 %copy-start.2 = (f32[4,16,128]{2,1,0:T(8,128)S(1)}, f32[4,16,128]{2,1,0:T(8,128)}, u32[]{:S(2)}) copy-start(f32[4,16,128]{2,1,0:T(8,128)} %param.12) | copy-start | bytes 98308
  2.1 21.1 %all-to-all-start = ((f32[128,1,64]{2,1,0:T(1,128)}), f32[128,1,64]{2,1,0:T(1,128)S(1)}, u32[]{:S(2)}, u32[]{:S(2)}) async-start(f32[128,1,64]{2,1,0:T(1,128)} %copy.15), calls=%async_computation | async-start | bytes 131072 | tf_op jit(solution)/shard_map/all_to_all | solution.py:405
  23.2 38.8 %copy-start = (bf16[64,256,128]{2,1,0:T(8,128)(2,1)S(1)}, bf16[64,256,128]{2,1,0:T(8,128)(2,1)}, u32[]{:S(2)}) copy-start(bf16[64,256,128]{2,1,0:T(8,128)(2,1)} %get-tuple-element.28.e_ref) | copy-start | bytes 12582916

commit v6 on v5

--- a/solution.py
+++ b/solution.py
@@ -207,6 +207,14 @@
     return edge[...].T
 
 
+def load_kernel(*refs):
+    half = (len(refs) - 1) // 2
+    for source, target in zip(refs[:half], refs[half:]):
+        target[...] = source[...]
+    state = refs[0][...]
+    refs[-1][...] = jnp.concatenate([state, state], axis=0).T[:, :ROWS]
+
+
 def first_pack_kernel(got_ref, m_ref, sums_ref, edge_ref, out_ref):
     misc = neighbour_sums(jnp.concatenate([got_ref[...], jnp.zeros((128, 128 - ROWS), f32)], axis=1), m_ref[...]) + edge_ref[...]
     for t in range(OWN):
@@ -364,7 +372,10 @@
     pay[pl.ds(OWN, 128, stride=LATER), :] = out
 
 
-def final_kernel(got_ref, t_ref, e_ref, rinv_ref, lab_ref, rs_ref, par_ref, t_out, tfine, grid):
+def final_kernel(
+    got_ref, t_ref, e_ref, rinv_ref, lab_ref, rs_ref, par_ref, state_ref, t_out, state_out, tfine, grid
+):
+    state_out[...] = state_ref[...]
     misc = got_ref[pl.ds(OWN, 128, stride=LATER), :]
     t_out[...] = fine_update(got_ref, misc, t_ref, e_ref, rinv_ref, lab_ref, rs_ref, par_ref, tfine, grid)
 
@@ -402,20 +413,25 @@
     square = ((128, 128), f32)
     pay = ((DEV * LATER, 128), f32)
 
-    states = lax.all_to_all(state.T.reshape(DEV, 1, ROWS), ("gx", "gy"), 0, 0, tiled=True).reshape(DEV, ROWS)
+    inputs = from_hbm(state, t0, av, var, mass, bare, par, bp, partners.T, ri, chem, sw)
+    *inputs, turned = call(
+        load_kernel, [(a.shape, a.dtype) for a in inputs] + [((ETA, ROWS), f32)], [], *inputs, results=(len(inputs),)
+    )
+    states = lax.all_to_all(turned.reshape(DEV, 1, ROWS), ("gx", "gy"), 0, 0, tiled=True).reshape(DEV, ROWS)
+    state, t0, par = inputs[0], inputs[1], inputs[6]
     table, mb, rinv, lab, rs, m, sums, edges, count, cols, sw, who = call(
         prep_kernel,
         [((ROWS, 256, 128), bf16), cells, cells, ((LABELS, 128), jnp.int32), ((SLOTS, LABELS), bf16),
          ((SLOTS, SLOTS), bf16), ((SLOTS, 256), f32), square, cells, ((SPEC, SPEC, ETA), f32), ((SPEC, ETA), f32),
          ((ROWS, LABELS, 128), bf16)],
         [square, square, cells, cells, cells, ((4 * LABELS, 128), f32), ((ROWS, 256, 128), bf16), square, pltpu.SemaphoreType.DMA((GROUPS,))],
-        dev, *from_hbm(t0, av, var, mass, bare, par, bp, partners.T, ri, chem, sw), scalars=1, streamed=(0,),
+        dev, *inputs[1:], scalars=1, streamed=(0,),
     )
     (sent,) = call(first_pack_kernel, [((DEV * FIRST, 128), f32)], [], states, m, sums, edges)
     got = exchange(sent)
     state, own_weight, sent = call(
         first_advance_kernel, [((ROWS, ETA), f32), ((8, 128), f32), pay], [cells],
-        got, *from_hbm(state), count, cols, sw,
+        got, state, count, cols, sw,
     )
     got = exchange(sent)
     grid = ((6, 32, 128), f32)
@@ -427,10 +443,12 @@
     got = exchange(sent)
     state, sent = call(
         later_advance_kernel, [((ROWS, ETA), f32), pay], [cells],
-        got, state, own_weight, count, cols, sw, results=(0,),
+        got, state, own_weight, count, cols, sw,
     )
     got = exchange(sent)
-    (t2,) = call(final_kernel, [cells], [cells, grid], got, t1, table, rinv, lab, rs, par, results=(0,))
+    t2, state = call(
+        final_kernel, [cells, cells], [cells, grid], got, t1, table, rinv, lab, rs, par, state, results=(0, 1)
+    )
     return state.reshape(species.shape), t2.reshape(thermal.shape)
 
 

time: 101 us -> 98.6 us (0.976)
  local copies, waits for them, and re-layouts: 1.5 us -> 0.01 us
    reshape x1 -> x0, local copies, waits for them, and re-layouts: 1.48 us -> none  [shards(): state.T.reshape(DEV, 1, ROWS)]
    pallas_call x6 -> x7, Pallas kernels: 14.7 us -> 14.1 us  [call(): pl.pallas_call(kernel, out_shape=[pltpu.HBM(*o) if i in away else pltpu.V...]
where the time goes in v6:
time: 98.6 us; the launch traced here: 98.3 us
  blocking collectives  67 us (68%)
  Pallas kernels  14.1 us (14%)
  starting transfers between devices  11.5 us (12%)
  waiting for transfers between devices  5 us (5%)
    all_to_all x4, blocking collectives, exchange(): lax.all_to_all(sent, ('gx', 'gy'), 0, 0, tiled=True).reshape(array.shape)  67 us
    pallas_call x7, Pallas kernels, call(): pl.pallas_call(kernel, out_shape=[pltpu.HBM(*o) if i in away else pltpu.V...  14.1 us
    all_to_all x1, starting transfers between devices, shards(): lax.all_to_all(turned.reshape(DEV, 1, ROWS), ('gx', 'gy'), 0, 0, tiled=True)  11.5 us
    all_to_all x1, waiting for transfers between devices, shards(): lax.all_to_all(turned.reshape(DEV, 1, ROWS), ('gx', 'gy'), 0, 0, tiled=True)  5 us
  transfers between devices with their start and end apart: 1, of which 1 were waited for; matrix products, arithmetic and copies ran while one was open for 0% of the time, Pallas kernels for 5%

profile of v6, /device:TPU:1, one launch (start us, length us, event | category | flops | bytes accessed | tf_op | source)
XLA Modules:
  0.0 98.3 jit_solution(3033094717517959839)
XLA Ops:
  0.6 1.6 %shard_map.131 = (f32[64,128]{1,0:T(8,128)S(1)}, f32[64,128]{1,0:T(8,128)S(1)}, f32[64,128]{1,0:T(8,128)S(1)}, f32[64,128]{1,0:T(8,128)S(1)}, f32[64,128]{1,0:T(...) custom-call(f32[64,128]{1,0:T(8,128)} %bitcast.36, ...), custom_call_target="tpu_custom_call" | custom-call | tf_op jit(solution)/shard_map/pallas_call | solution.py:386
  2.3 11.5 %all-to-all-start = ((f32[128,1,64]{2,1,0:T(1,128)}), f32[128,1,64]{2,1,0:T(1,128)S(1)}, u32[]{:S(2)}, u32[]{:S(2)}) async-start(f32[128,1,64]{2,1,0:T(1,128)} %bitcast.35), calls=%async_computation | async-start | bytes 131072 | tf_op jit(solution)/shard_map/all_to_all | solution.py:420
  13.8 4.6 %shard_map.132 = (bf16[64,256,128]{2,1,0:T(8,128)(2,1)}, f32[64,128]{1,0:T(8,128)S(1)}, f32[64,128]{1,0:T(8,128)S(1)}, s32[48,128]{1,0:T(8,128)S(1)}, bf16[512,4...) custom-call(s32[1]{0:T(128)} %bitcast.14.dev_ref, ...), custom_call_target="tpu_custom_call" | custom-call | tf_op jit(solution)/shard_map/pallas_call | solution.py:386
  18.4 5.0 %all-to-all-done = f32[128,1,64]{2,1,0:T(1,128)S(1)} async-done(((f32[128,1,64]{2,1,0:T(1,128)}), f32[128,1,64]{2,1,0:T(1,128)S(1)}, u32[]{:S(2)}, u32[]{:S(2)}) %all-to-all-start) | async-done | bytes 32800 | tf_op jit(solution)/shard_map/all_to_all | solution.py:420
  23.4 0.0 copy-start
  23.4 0.5 shard_map.133
  23.9 18.9 %all_to_all.25 = f32[128,1,1152]{2,1,0:T(1,128)S(1)} all-to-all(f32[128,1,1152]{2,1,0:T(1,128)S(1)} %bitcast.26), channel_id=1, replica_groups=mesh['gx'=16,'gy'=8] {'gx','gy'}, dimensions={0} | all-to-all | bytes 1179648 | tf_op jit(solution)/shard_map/all_to_all | solution.py:399
  42.8 1.6 %shard_map.134 = (f32[64,128]{1,0:T(8,128)S(1)}, f32[8,128]{1,0:T(8,128)S(1)}, f32[640,128]{1,0:T(8,128)S(1)}) custom-call(f32[1152,128]{1,0:T(8,128)S(1)} %bitcast.27, f32[64,128]{1,0:T(8,128)S(1)} %get-tuple-element.51.state_ref, f32[64,128]{1,0:T(8,128)S(1)} %get-tuple-element.52.count_ref, f32[16,16,128]{2,1,0:T(8,128)S(1)} %get-tuple-element.53.cols, ...), custom_call_target="tpu_custom_call" | custom-call | tf_op jit(solution)/shard_map/pallas_call | solution.py:386
  44.4 16.2 %all_to_all.26 = f32[128,1,640]{2,1,0:T(1,128)S(1)} all-to-all(f32[128,1,640]{2,1,0:T(1,128)S(1)} %bitcast.33), channel_id=1, replica_groups=mesh['gx'=16,'gy'=8] {'gx','gy'}, dimensions={0} | all-to-all | bytes 655360 | tf_op jit(solution)/shard_map/all_to_all | solution.py:399
  60.5 0.0 copy-done
  60.5 2.6 %shard_map.135 = (f32[64,128]{1,0:T(8,128)S(1)}, f32[640,128]{1,0:T(8,128)S(1)}) custom-call(f32[640,128]{1,0:T(8,128)S(1)} %bitcast.29, f32[64,128]{1,0:T(8,128)S(1)} %get-tuple-element.37.t_ref, bf16[64,256,128]{2,1,0:T(8,128)(2,1)S(1)} %copy-done, f32[64,128]{1,0:T(8,128)S(1)} %get-tuple-element.57.rinv_ref, f32[64,128]{1,0:T(8,128)S(1)} %get-tuple-element.58.mb_ref, ...), custom_call_target="tpu_custom_call" | custom-call | tf_op jit(solution)/shard_map/pallas_call | solution.py:386
  63.1 16.0 %all_to_all.27 = f32[128,1,640]{2,1,0:T(1,128)S(1)} all-to-all(f32[128,1,640]{2,1,0:T(1,128)S(1)} %bitcast.32), channel_id=1, replica_groups=mesh['gx'=16,'gy'=8] {'gx','gy'}, dimensions={0} | all-to-all | bytes 655360 | tf_op jit(solution)/shard_map/all_to_all | solution.py:399
  79.1 1.5 %shard_map.136 = (f32[64,128]{1,0:T(8,128)S(1)}, f32[640,128]{1,0:T(8,128)S(1)}) custom-call(f32[640,128]{1,0:T(8,128)S(1)} %bitcast.30, f32[64,128]{1,0:T(8,128)S(1)} %get-tuple-element.63.state_ref, f32[8,128]{1,0:T(8,128)S(1)} %get-tuple-element.64.mass_ref, f32[64,128]{1,0:T(8,128)S(1)} %get-tuple-element.52.count_ref, ...), custom_call_target="tpu_custom_call" | custom-call | tf_op jit(solution)/shard_map/pallas_call | solution.py:386
  80.7 16.0 %all_to_all.28 = f32[128,1,640]{2,1,0:T(1,128)S(1)} all-to-all(f32[128,1,640]{2,1,0:T(1,128)S(1)} %bitcast.31), channel_id=1, replica_groups=mesh['gx'=16,'gy'=8] {'gx','gy'}, dimensions={0} | all-to-all | bytes 655360 | tf_op jit(solution)/shard_map/all_to_all | solution.py:399
  96.6 1.6 %shard_map.137 = (f32[64,128]{1,0:T(8,128)}, f32[64,128]{1,0:T(8,128)}) custom-call(f32[640,128]{1,0:T(8,128)S(1)} %bitcast.28, f32[64,128]{1,0:T(8,128)S(1)} %get-tuple-element.66.t_ref, bf16[64,256,128]{2,1,0:T(8,128)(2,1)S(1)} %copy-done, f32[64,128]{1,0:T(8,128)S(1)} %get-tuple-element.57.rinv_ref, s32[48,128]{1,0:T(8,128)S(1)} %get-tuple-element.59.lab_ref, ...), custom_call_target="tpu_custom_call" | custom-call | tf_op jit(solution)/shard_map/pallas_call | solution.py:386
Async XLA Ops:
  2.3 21.1 %all-to-all-start = ((f32[128,1,64]{2,1,0:T(1,128)}), f32[128,1,64]{2,1,0:T(1,128)S(1)}, u32[]{:S(2)}, u32[]{:S(2)}) async-start(f32[128,1,64]{2,1,0:T(1,128)} %bitcast.35), calls=%async_computation | async-start | bytes 131072 | tf_op jit(solution)/shard_map/all_to_all | solution.py:420
  23.4 37.2 %copy-start = (bf16[64,256,128]{2,1,0:T(8,128)(2,1)S(1)}, bf16[64,256,128]{2,1,0:T(8,128)(2,1)}, u32[]{:S(2)}) copy-start(bf16[64,256,128]{2,1,0:T(8,128)(2,1)} %get-tuple-element.56.e_ref) | copy-start | bytes 12582916

commit v7 on v6

--- a/solution.py
+++ b/solution.py
@@ -76,8 +76,8 @@
 
 def prep_kernel(
     dev_ref, t_ref, av_ref, var_ref, mass_ref, bare_ref, par_ref, bp_ref, fp_ref, ri_ref, c_ref, sw_ref,
-    e_out, mb_ref, rinv_ref, lab_ref, rs_ref, m_ref, sums_ref, edge_ref, count_ref, cols, weight_ref, who_ref,
-    le, l1e, a1, b1, chi, acc, e_ref, edge, sems,
+    e_out, mb_ref, rinv_ref, lab_ref, rs_ref, m_ref, sums_ref, edge_ref, count_ref, cols, weight_ref, who_ref, rst_ref,
+    le, l1e, a1, b1, chi, over, acc, e_ref, edge, sems,
 ):
     edge_ref[...] = edges_by_z(t_ref, edge)
     for s in range(SPEC):
@@ -92,54 +92,68 @@
     count = jnp.sum(jnp.where(own, ri_ref[...] + 1, 0).astype(f32), axis=1, keepdims=True)
     count_ref[...] = jnp.broadcast_to(count, (ROWS, ETA))
 
-    named = jnp.zeros((32, 16), f32)
-    for group in range(GROUPS):
-        rows = par_ref[group * 8 : (group + 1) * 8, :]
-        tall, short = rows >> 4, rows & 15
-        tall = jnp.concatenate([hot(tall[q : q + 1] == iota((32, 128), 0)) for q in range(8)], axis=1)
-        short = jnp.concatenate([hot(short[q : q + 1] == iota((16, 128), 0)) for q in range(8)], axis=1)
-        named = named + dot(tall, short, NT)
-    named = hot(named > 0.5)
-    within = dot(named, hot(iota((16, 16), 0) < iota((16, 16), 1)), NN)
-    ahead = dot(hot(iota((32, 32), 1) < iota((32, 32), 0)), named, NN).astype(bf16)
-    ahead = dot(ahead, jnp.ones((16, 16), bf16), NN)
-    order = jnp.where(named > 0, within + ahead + 1.0, 0.0).astype(bf16)
-    spread = dot(hot(iota((SLOTS, 32), 0) >> 4 == iota((SLOTS, 32), 1)), order, NN)
-    spread = jnp.where(iota((SLOTS, 16), 0) & 15 == iota((SLOTS, 16), 1), spread, 0.0).astype(bf16)
-    order = dot(spread, jnp.ones((16, 128), bf16), NN)
-    sel = hot(order == (iota((SLOTS, 128), 1) + 1).astype(f32))
-    cell = iota((SLOTS, 128), 0) + 1
-    label = dot(
-        sel,
-        jnp.concatenate([(cell >> 4).astype(f32).astype(bf16), (cell & 15).astype(f32).astype(bf16)], axis=1),
-        TN,
-    )
-    lab = ((label[:, :128] * 16.0 + label[:, 128:]).astype(jnp.int32) - 1)[:LABELS]
-    lab_ref[...] = lab
-
-    bp = bp_ref[...]
-    device = iota((128, SLOTS), 0).astype(f32).astype(bf16)
-    pt = jnp.concatenate(
-        [
-            marked(jnp.where(bp & 3 == t, bp >> 2, -1).astype(f32).astype(bf16) == device)
-            for t in range(OWN)
-        ],
-        axis=0,
-    )
-    rs = dot(pt, sel, NN).astype(bf16)[:, :LABELS]
-    rs_ref[...] = rs
-    other = iota((256, SLOTS), 0).astype(f32).astype(bf16)
-    near = fp_ref[...]
-    adjacent = []
-    for half in range(2):
-        part = near - 256 * half
-        part = jnp.where((part >= 0) & (part < 256), part, -1).astype(f32)
-        total = jnp.zeros((256, SLOTS), bf16)
-        for j in range(6):
-            total = total + marked(part[j : j + 1].astype(bf16) == other)
-        adjacent.append(total)
-    half = dot(pt, jnp.concatenate(adjacent, axis=0), NT).astype(bf16)
-    m_ref[...] = dot(half, pt, NT).astype(bf16)
+    made = {}
+
+    def label_steps():
+        named = jnp.zeros((32, 16), f32)
+        for group in range(GROUPS):
+            rows = par_ref[group * 8 : (group + 1) * 8, :]
+            tall, short = rows >> 4, rows & 15
+            tall = jnp.concatenate([hot(tall[q : q + 1] == iota((32, 128), 0)) for q in range(8)], axis=1)
+            short = jnp.concatenate([hot(short[q : q + 1] == iota((16, 128), 0)) for q in range(8)], axis=1)
+            named = named + dot(tall, short, NT)
+        named = hot(named > 0.5)
+        yield
+        within = dot(named, hot(iota((16, 16), 0) < iota((16, 16), 1)), NN)
+        ahead = dot(hot(iota((32, 32), 1) < iota((32, 32), 0)), named, NN).astype(bf16)
+        yield
+        ahead = dot(ahead, jnp.ones((16, 16), bf16), NN)
+        order = jnp.where(named > 0, within + ahead + 1.0, 0.0).astype(bf16)
+        yield
+        spread = dot(hot(iota((SLOTS, 32), 0) >> 4 == iota((SLOTS, 32), 1)), order, NN)
+        spread = jnp.where(iota((SLOTS, 16), 0) & 15 == iota((SLOTS, 16), 1), spread, 0.0).astype(bf16)
+        yield
+        order = dot(spread, jnp.ones((16, 128), bf16), NN)
+        sel = hot(order == (iota((SLOTS, 128), 1) + 1).astype(f32))
+        cell = iota((SLOTS, 128), 0) + 1
+        yield
+        label = dot(
+            sel,
+            jnp.concatenate([(cell >> 4).astype(f32).astype(bf16), (cell & 15).astype(f32).astype(bf16)], axis=1),
+            TN,
+        )
+        lab = ((label[:, :128] * 16.0 + label[:, 128:]).astype(jnp.int32) - 1)[:LABELS]
+        lab_ref[...] = lab
+        made['lab'] = lab
+
+        yield
+        bp = bp_ref[...]
+        device = iota((128, SLOTS), 0).astype(f32).astype(bf16)
+        pt = jnp.concatenate(
+            [
+                marked(jnp.where(bp & 3 == t, bp >> 2, -1).astype(f32).astype(bf16) == device)
+                for t in range(OWN)
+            ],
+            axis=0,
+        )
+        rs = dot(pt, sel, NN)
+        made['rs'] = rs.astype(bf16)[:, :LABELS]
+        rst_ref[...] = rs.T[:LABELS].astype(bf16)
+        rs_ref[...] = made['rs']
+        yield
+        other = iota((256, SLOTS), 0).astype(f32).astype(bf16)
+        near = fp_ref[...]
+        adjacent = []
+        for half in range(2):
+            part = near - 256 * half
+            part = jnp.where((part >= 0) & (part < 256), part, -1).astype(f32)
+            total = jnp.zeros((256, SLOTS), bf16)
+            for j in range(6):
+                total = total + marked(part[j : j + 1].astype(bf16) == other)
+            adjacent.append(total)
+        half = dot(pt, jnp.concatenate(adjacent, axis=0), NT).astype(bf16)
+        m_ref[...] = dot(half, pt, NT).astype(bf16)
+        yield
 
     point = (iota((ETA, 128), 0).astype(f32) + 0.5) / ETA
     le[...] = jnp.log(point) * LOG2E
@@ -148,33 +162,39 @@
     a1[...] = av_ref[...] * shape_sum - 1.0
     b1[...] = (1.0 - av_ref[...]) * shape_sum - 1.0
     chi[...] = bare_ref[...] * (1.0 + 0.5 * jnp.tanh(t_ref[...]))
-    acc[...] = jnp.zeros_like(acc)
-
-    def tables(group, carry):
-        a_rows, b_rows = rows_of(a1, group), rows_of(b1, group)
-        chi_rows, mass_rows, par_rows = rows_of(chi, group), rows_of(mass_ref, group), rows_of(par_ref, group)
-        inverse, mass_over, arms = [], [], []
+
+    steps = label_steps()
+    for group in range(GROUPS):
+        next(steps, None)
+        a_rows, b_rows, mass_rows = rows_of(a1, group), rows_of(b1, group), rows_of(mass_ref, group)
+        inverse = []
         for q in range(8):
             logits = a_rows[q : q + 1] * le[...] + b_rows[q : q + 1] * l1e[...]
             table = jnp.exp2(logits - jnp.max(logits, axis=0, keepdims=True))
-            r = 1.0 / jnp.sum(table, axis=0, keepdims=True)
+            inverse.append(1.0 / jnp.sum(table, axis=0, keepdims=True))
             high, low = halves(table)
             e_ref[group * 8 + q, 0:128, :] = high
             e_ref[group * 8 + q, 128:256, :] = low
-            w = mass_rows[q : q + 1] * r
-            n = w * chi_rows[q : q + 1]
-            inverse.append(r)
-            mass_over.append(w)
+        pltpu.make_async_copy(e_ref.at[pl.ds(group * 8, 8)], e_out.at[pl.ds(group * 8, 8)], sems.at[group]).start()
+        inverse = jnp.concatenate(inverse, axis=0)
+        put_rows(rinv_ref, group, [inverse])
+        put_rows(over, group, [mass_rows * inverse])
+        put_rows(mb_ref, group, [mass_rows * inverse * rows_of(bare_ref, group)])
+    for _ in steps:
+        pass
+    lab, rs = made["lab"], made["rs"]
+    total = jnp.zeros((4 * LABELS, 128), f32)
+    for group in range(GROUPS):
+        w_rows, par_rows = rows_of(over, group), rows_of(par_ref, group)
+        n_rows = w_rows * rows_of(chi, group)
+        arms = []
+        for q in range(8):
             mine = hot(lab == par_rows[q : q + 1])
             who_ref[group * 8 + q] = mine
-            arms.append(jnp.concatenate([mine * part for part in (*halves(w), *halves(n))], axis=0))
-        put_rows(rinv_ref, group, inverse)
-        put_rows(mb_ref, group, [jnp.concatenate(mass_over, axis=0) * rows_of(bare_ref, group)])
-        pltpu.make_async_copy(e_ref.at[pl.ds(group * 8, 8)], e_out.at[pl.ds(group * 8, 8)], sems.at[group]).start()
-        acc[...] += dot(jnp.concatenate(arms, axis=1), together(e_ref, group, 128), NT)
-        return carry
-
-    lax.fori_loop(0, GROUPS, tables, 0, unroll=UNROLL)
+            parts = (*halves(w_rows[q : q + 1]), *halves(n_rows[q : q + 1]))
+            arms.append(jnp.concatenate([mine * part for part in parts], axis=0))
+        total = total + dot(jnp.concatenate(arms, axis=1), together(e_ref, group, 128), NT)
+    acc[...] = total
     both = acc[...]
     w48 = both[0:48] + both[48:96]
     n48 = both[96:144] + both[144:192]
@@ -306,9 +326,9 @@
     advance(state_ref, misc, cchi, count_ref, cols, weight_ref, speed_ref, (state_out, pay), True)
 
 
-def fine_update(got_ref, misc, t_ref, e_ref, rinv_ref, lab_ref, rs_ref, par_ref, tfine, grid):
+def fine_update(got_ref, misc, t_ref, e_ref, rinv_ref, lab_ref, rst_ref, par_ref, tfine, grid):
     theta = jnp.concatenate([got_ref[pl.ds(t, 128, stride=LATER), :] for t in range(OWN)], axis=0)
-    picked = dot(rs_ref[...], jnp.concatenate(halves(theta), axis=1), TN).astype(bf16)
+    picked = dot(rst_ref[...], jnp.concatenate(halves(theta), axis=1), NN).astype(bf16)
     high, low = picked[:, :128], picked[:, 128:]
     rows = jnp.concatenate(
         [jnp.concatenate([high, high], axis=1), jnp.concatenate([low, low], axis=1)], axis=0
@@ -345,12 +365,14 @@
 
 
 def middle_kernel(
-    got_ref, t_ref, e_ref, rinv_ref, mb_ref, lab_ref, rs_ref, m_ref, par_ref, who_ref,
+    got_ref, t_ref, e_ref, rinv_ref, mb_ref, lab_ref, rs_ref, rst_ref, m_ref, par_ref, who_ref,
     t_out, pay, tfine, grid, flux, acc, edge,
 ):
     misc = got_ref[pl.ds(OWN, 128, stride=LATER), :]
-    t = fine_update(got_ref, misc, t_ref, e_ref, rinv_ref, lab_ref, rs_ref, par_ref, tfine, grid)
+    near = neighbour_sums(misc, m_ref[...])
+    t = fine_update(got_ref, misc, t_ref, e_ref, rinv_ref, lab_ref, rst_ref, par_ref, tfine, grid)
     t_out[...] = t
+    pay[pl.ds(OWN, 128, stride=LATER), :] = near + edges_by_z(t_out, edge)
     flux[...] = mb_ref[...] * (1.0 + 0.5 * jnp.tanh(t))
     acc[...] = jnp.zeros_like(acc)
 
@@ -368,16 +390,14 @@
     sums = to_slots(rs_ref[...], both[0:48] + both[48:96])
     for k in range(OWN):
         pay[pl.ds(k, 128, stride=LATER), :] = sums[k * 128 : (k + 1) * 128]
-    out = neighbour_sums(misc, m_ref[...]) + edges_by_z(t_out, edge)
-    pay[pl.ds(OWN, 128, stride=LATER), :] = out
 
 
 def final_kernel(
-    got_ref, t_ref, e_ref, rinv_ref, lab_ref, rs_ref, par_ref, state_ref, t_out, state_out, tfine, grid
+    got_ref, t_ref, e_ref, rinv_ref, lab_ref, rst_ref, par_ref, state_ref, t_out, state_out, tfine, grid
 ):
     state_out[...] = state_ref[...]
     misc = got_ref[pl.ds(OWN, 128, stride=LATER), :]
-    t_out[...] = fine_update(got_ref, misc, t_ref, e_ref, rinv_ref, lab_ref, rs_ref, par_ref, tfine, grid)
+    t_out[...] = fine_update(got_ref, misc, t_ref, e_ref, rinv_ref, lab_ref, rst_ref, par_ref, tfine, grid)
 
 
 def call(kernel, outs, scratch, *operands, scalars=0, results=(), streamed=()):
@@ -419,12 +439,12 @@
     )
     states = lax.all_to_all(turned.reshape(DEV, 1, ROWS), ("gx", "gy"), 0, 0, tiled=True).reshape(DEV, ROWS)
     state, t0, par = inputs[0], inputs[1], inputs[6]
-    table, mb, rinv, lab, rs, m, sums, edges, count, cols, sw, who = call(
+    table, mb, rinv, lab, rs, m, sums, edges, count, cols, sw, who, rst = call(
         prep_kernel,
         [((ROWS, 256, 128), bf16), cells, cells, ((LABELS, 128), jnp.int32), ((SLOTS, LABELS), bf16),
          ((SLOTS, SLOTS), bf16), ((SLOTS, 256), f32), square, cells, ((SPEC, SPEC, ETA), f32), ((SPEC, ETA), f32),
-         ((ROWS, LABELS, 128), bf16)],
-        [square, square, cells, cells, cells, ((4 * LABELS, 128), f32), ((ROWS, 256, 128), bf16), square, pltpu.SemaphoreType.DMA((GROUPS,))],
+         ((ROWS, LABELS, 128), bf16), ((LABELS, SLOTS), bf16)],
+        [square, square, cells, cells, cells, cells, ((4 * LABELS, 128), f32), ((ROWS, 256, 128), bf16), square, pltpu.SemaphoreType.DMA((GROUPS,))],
         dev, *inputs[1:], scalars=1, streamed=(0,),
     )
     (sent,) = call(first_pack_kernel, [((DEV * FIRST, 128), f32)], [], states, m, sums, edges)
@@ -438,7 +458,7 @@
     t1, sent = call(
         middle_kernel, [cells, pay],
         [cells, grid, cells, ((2 * LABELS, 128), f32), square],
-        got, t0, table, rinv, mb, lab, rs, m, par, who,
+        got, t0, table, rinv, mb, lab, rs, rst, m, par, who,
     )
     got = exchange(sent)
     state, sent = call(
@@ -447,7 +467,7 @@
     )
     got = exchange(sent)
     t2, state = call(
-        final_kernel, [cells, cells], [cells, grid], got, t1, table, rinv, lab, rs, par, state, results=(0, 1)
+        final_kernel, [cells, cells], [cells, grid], got, t1, table, rinv, lab, rst, par, state, results=(0, 1)
     )
     return state.reshape(species.shape), t2.reshape(thermal.shape)
 

time: 98.6 us -> 98.1 us (level)
  no operation moved by 1% of the time
where the time goes in v7:
time: 98.1 us; the launch traced here: 97.9 us
  blocking collectives  66.9 us (68%)
  Pallas kernels  13.7 us (14%)
  starting transfers between devices  11.5 us (12%)
  waiting for transfers between devices  5.15 us (5%)
    all_to_all x4, blocking collectives, exchange(): lax.all_to_all(sent, ('gx', 'gy'), 0, 0, tiled=True).reshape(array.shape)  66.9 us
    pallas_call x7, Pallas kernels, call(): pl.pallas_call(kernel, out_shape=[pltpu.HBM(*o) if i in away else pltpu.V...  13.7 us
    all_to_all x1, starting transfers between devices, shards(): lax.all_to_all(turned.reshape(DEV, 1, ROWS), ('gx', 'gy'), 0, 0, tiled=True)  11.5 us
    all_to_all x1, waiting for transfers between devices, shards(): lax.all_to_all(turned.reshape(DEV, 1, ROWS), ('gx', 'gy'), 0, 0, tiled=True)  5.15 us
  transfers between devices with their start and end apart: 1, of which 1 were waited for; matrix products, arithmetic and copies ran while one was open for 0% of the time, Pallas kernels for 5%

profile of v7, /device:TPU:1, one launch (start us, length us, event | category | flops | bytes accessed | tf_op | source)
XLA Modules:
  0.0 97.9 jit_solution(7251369836080899443)
XLA Ops:
  0.6 1.6 %shard_map.131 = (f32[64,128]{1,0:T(8,128)S(1)}, f32[64,128]{1,0:T(8,128)S(1)}, f32[64,128]{1,0:T(8,128)S(1)}, f32[64,128]{1,0:T(8,128)S(1)}, f32[64,128]{1,0:T(...) custom-call(f32[64,128]{1,0:T(8,128)} %bitcast.36, ...), custom_call_target="tpu_custom_call" | custom-call | tf_op jit(solution)/shard_map/pallas_call | solution.py:406
  2.3 11.5 %all-to-all-start = ((f32[128,1,64]{2,1,0:T(1,128)}), f32[128,1,64]{2,1,0:T(1,128)S(1)}, u32[]{:S(2)}, u32[]{:S(2)}) async-start(f32[128,1,64]{2,1,0:T(1,128)} %bitcast.35), calls=%async_computation | async-start | bytes 131072 | tf_op jit(solution)/shard_map/all_to_all | solution.py:440
  13.8 4.4 %shard_map.132 = (bf16[64,256,128]{2,1,0:T(8,128)(2,1)}, f32[64,128]{1,0:T(8,128)S(1)}, f32[64,128]{1,0:T(8,128)S(1)}, s32[48,128]{1,0:T(8,128)S(1)}, bf16[512,4...) custom-call(s32[1]{0:T(128)} %bitcast.14.dev_ref, ...), custom_call_target="tpu_custom_call" | custom-call | tf_op jit(solution)/shard_map/pallas_call | solution.py:406
  18.2 5.1 %all-to-all-done = f32[128,1,64]{2,1,0:T(1,128)S(1)} async-done(((f32[128,1,64]{2,1,0:T(1,128)}), f32[128,1,64]{2,1,0:T(1,128)S(1)}, u32[]{:S(2)}, u32[]{:S(2)}) %all-to-all-start) | async-done | bytes 32800 | tf_op jit(solution)/shard_map/all_to_all | solution.py:440
  23.4 0.0 copy-start
  23.4 0.5 shard_map.133
  23.9 18.8 %all_to_all.25 = f32[128,1,1152]{2,1,0:T(1,128)S(1)} all-to-all(f32[128,1,1152]{2,1,0:T(1,128)S(1)} %bitcast.26), channel_id=1, replica_groups=mesh['gx'=16,'gy'=8] {'gx','gy'}, dimensions={0} | all-to-all | bytes 1179648 | tf_op jit(solution)/shard_map/all_to_all | solution.py:419
  42.6 1.6 %shard_map.134 = (f32[64,128]{1,0:T(8,128)S(1)}, f32[8,128]{1,0:T(8,128)S(1)}, f32[640,128]{1,0:T(8,128)S(1)}) custom-call(f32[1152,128]{1,0:T(8,128)S(1)} %bitcast.27, f32[64,128]{1,0:T(8,128)S(1)} %get-tuple-element.52.state_ref, f32[64,128]{1,0:T(8,128)S(1)} %get-tuple-element.53.count_ref, f32[16,16,128]{2,1,0:T(8,128)S(1)} %get-tuple-element.54.cols, ...), custom_call_target="tpu_custom_call" | custom-call | tf_op jit(solution)/shard_map/pallas_call | solution.py:406
  44.2 16.2 %all_to_all.26 = f32[128,1,640]{2,1,0:T(1,128)S(1)} all-to-all(f32[128,1,640]{2,1,0:T(1,128)S(1)} %bitcast.33), channel_id=1, replica_groups=mesh['gx'=16,'gy'=8] {'gx','gy'}, dimensions={0} | all-to-all | bytes 655360 | tf_op jit(solution)/shard_map/all_to_all | solution.py:419
  60.4 0.0 copy-done
  60.4 2.3 %shard_map.135 = (f32[64,128]{1,0:T(8,128)S(1)}, f32[640,128]{1,0:T(8,128)S(1)}) custom-call(f32[640,128]{1,0:T(8,128)S(1)} %bitcast.29, f32[64,128]{1,0:T(8,128)S(1)} %get-tuple-element.38.t_ref, bf16[64,256,128]{2,1,0:T(8,128)(2,1)S(1)} %copy-done, f32[64,128]{1,0:T(8,128)S(1)} %get-tuple-element.58.rinv_ref, f32[64,128]{1,0:T(8,128)S(1)} %get-tuple-element.59.mb_ref, ...), custom_call_target="tpu_custom_call" | custom-call | tf_op jit(solution)/shard_map/pallas_call | solution.py:406
  62.7 16.0 %all_to_all.27 = f32[128,1,640]{2,1,0:T(1,128)S(1)} all-to-all(f32[128,1,640]{2,1,0:T(1,128)S(1)} %bitcast.31), channel_id=1, replica_groups=mesh['gx'=16,'gy'=8] {'gx','gy'}, dimensions={0} | all-to-all | bytes 655360 | tf_op jit(solution)/shard_map/all_to_all | solution.py:419
  78.7 1.5 %shard_map.136 = (f32[64,128]{1,0:T(8,128)S(1)}, f32[640,128]{1,0:T(8,128)S(1)}) custom-call(f32[640,128]{1,0:T(8,128)S(1)} %bitcast.30, f32[64,128]{1,0:T(8,128)S(1)} %get-tuple-element.65.state_ref, f32[8,128]{1,0:T(8,128)S(1)} %get-tuple-element.66.mass_ref, f32[64,128]{1,0:T(8,128)S(1)} %get-tuple-element.53.count_ref, ...), custom_call_target="tpu_custom_call" | custom-call | tf_op jit(solution)/shard_map/pallas_call | solution.py:406
  80.2 16.0 %all_to_all.28 = f32[128,1,640]{2,1,0:T(1,128)S(1)} all-to-all(f32[128,1,640]{2,1,0:T(1,128)S(1)} %bitcast.32), channel_id=1, replica_groups=mesh['gx'=16,'gy'=8] {'gx','gy'}, dimensions={0} | all-to-all | bytes 655360 | tf_op jit(solution)/shard_map/all_to_all | solution.py:419
  96.2 1.6 %shard_map.137 = (f32[64,128]{1,0:T(8,128)}, f32[64,128]{1,0:T(8,128)}) custom-call(f32[640,128]{1,0:T(8,128)S(1)} %bitcast.28, f32[64,128]{1,0:T(8,128)S(1)} %get-tuple-element.68.t_ref, bf16[64,256,128]{2,1,0:T(8,128)(2,1)S(1)} %copy-done, f32[64,128]{1,0:T(8,128)S(1)} %get-tuple-element.58.rinv_ref, s32[48,128]{1,0:T(8,128)S(1)} %get-tuple-element.60.lab_ref, ...), custom_call_target="tpu_custom_call" | custom-call | tf_op jit(solution)/shard_map/pallas_call | solution.py:406
Async XLA Ops:
  2.3 21.1 %all-to-all-start = ((f32[128,1,64]{2,1,0:T(1,128)}), f32[128,1,64]{2,1,0:T(1,128)S(1)}, u32[]{:S(2)}, u32[]{:S(2)}) async-start(f32[128,1,64]{2,1,0:T(1,128)} %bitcast.35), calls=%async_computation | async-start | bytes 131072 | tf_op jit(solution)/shard_map/all_to_all | solution.py:440
  23.4 37.0 %copy-start = (bf16[64,256,128]{2,1,0:T(8,128)(2,1)S(1)}, bf16[64,256,128]{2,1,0:T(8,128)(2,1)}, u32[]{:S(2)}) copy-start(bf16[64,256,128]{2,1,0:T(8,128)(2,1)} %get-tuple-element.57.e_ref) | copy-start | bytes 12582916

commit v8 on v7

--- a/solution.py
+++ b/solution.py
@@ -18,7 +18,7 @@
 FIRST = 9
 LATER = 5
 UNROLL = 8
-SUBROLL = 4
+SUBROLL = 16
 LOG2E = 1.4426950408889634
 
 coupling = 0.05

time: 98.1 us -> 97.7 us (level)
  no operation moved by 1% of the time
where the time goes in v8:
time: 97.7 us; the launch traced here: 97.5 us
  blocking collectives  66.9 us (68%)
  Pallas kernels  13.3 us (14%)
  starting transfers between devices  11.5 us (12%)
  waiting for transfers between devices  5.15 us (5%)
    all_to_all x4, blocking collectives, exchange(): lax.all_to_all(sent, ('gx', 'gy'), 0, 0, tiled=True).reshape(array.shape)  66.9 us
    pallas_call x7, Pallas kernels, call(): pl.pallas_call(kernel, out_shape=[pltpu.HBM(*o) if i in away else pltpu.V...  13.3 us
    all_to_all x1, starting transfers between devices, shards(): lax.all_to_all(turned.reshape(DEV, 1, ROWS), ('gx', 'gy'), 0, 0, tiled=True)  11.5 us
    all_to_all x1, waiting for transfers between devices, shards(): lax.all_to_all(turned.reshape(DEV, 1, ROWS), ('gx', 'gy'), 0, 0, tiled=True)  5.15 us
  transfers between devices with their start and end apart: 1, of which 1 were waited for; matrix products, arithmetic and copies ran while one was open for 0% of the time, Pallas kernels for 5%

profile of v8, /device:TPU:1, one launch (start us, length us, event | category | flops | bytes accessed | tf_op | source)
XLA Modules:
  0.0 97.5 jit_solution(11252847561029597557)
XLA Ops:
  0.6 1.6 %shard_map.131 = (f32[64,128]{1,0:T(8,128)S(1)}, f32[64,128]{1,0:T(8,128)S(1)}, f32[64,128]{1,0:T(8,128)S(1)}, f32[64,128]{1,0:T(8,128)S(1)}, f32[64,128]{1,0:T(...) custom-call(f32[64,128]{1,0:T(8,128)} %bitcast.36, ...), custom_call_target="tpu_custom_call" | custom-call | tf_op jit(solution)/shard_map/pallas_call | solution.py:406
  2.3 11.5 %all-to-all-start = ((f32[128,1,64]{2,1,0:T(1,128)}), f32[128,1,64]{2,1,0:T(1,128)S(1)}, u32[]{:S(2)}, u32[]{:S(2)}) async-start(f32[128,1,64]{2,1,0:T(1,128)} %bitcast.35), calls=%async_computation | async-start | bytes 131072 | tf_op jit(solution)/shard_map/all_to_all | solution.py:440
  13.8 4.4 %shard_map.132 = (bf16[64,256,128]{2,1,0:T(8,128)(2,1)}, f32[64,128]{1,0:T(8,128)S(1)}, f32[64,128]{1,0:T(8,128)S(1)}, s32[48,128]{1,0:T(8,128)S(1)}, bf16[512,4...) custom-call(s32[1]{0:T(128)} %bitcast.14.dev_ref, ...), custom_call_target="tpu_custom_call" | custom-call | tf_op jit(solution)/shard_map/pallas_call | solution.py:406
  18.2 5.1 %all-to-all-done = f32[128,1,64]{2,1,0:T(1,128)S(1)} async-done(((f32[128,1,64]{2,1,0:T(1,128)}), f32[128,1,64]{2,1,0:T(1,128)S(1)}, u32[]{:S(2)}, u32[]{:S(2)}) %all-to-all-start) | async-done | bytes 32800 | tf_op jit(solution)/shard_map/all_to_all | solution.py:440
  23.4 0.0 copy-start
  23.4 0.5 shard_map.133
  23.9 18.8 %all_to_all.25 = f32[128,1,1152]{2,1,0:T(1,128)S(1)} all-to-all(f32[128,1,1152]{2,1,0:T(1,128)S(1)} %bitcast.26), channel_id=1, replica_groups=mesh['gx'=16,'gy'=8] {'gx','gy'}, dimensions={0} | all-to-all | bytes 1179648 | tf_op jit(solution)/shard_map/all_to_all | solution.py:419
  42.6 1.4 %shard_map.134 = (f32[64,128]{1,0:T(8,128)S(1)}, f32[8,128]{1,0:T(8,128)S(1)}, f32[640,128]{1,0:T(8,128)S(1)}) custom-call(f32[1152,128]{1,0:T(8,128)S(1)} %bitcast.27, f32[64,128]{1,0:T(8,128)S(1)} %get-tuple-element.52.state_ref, f32[64,128]{1,0:T(8,128)S(1)} %get-tuple-element.53.count_ref, f32[16,16,128]{2,1,0:T(8,128)S(1)} %get-tuple-element.54.cols, ...), custom_call_target="tpu_custom_call" | custom-call | tf_op jit(solution)/shard_map/pallas_call | solution.py:406
  44.0 16.2 %all_to_all.26 = f32[128,1,640]{2,1,0:T(1,128)S(1)} all-to-all(f32[128,1,640]{2,1,0:T(1,128)S(1)} %bitcast.33), channel_id=1, replica_groups=mesh['gx'=16,'gy'=8] {'gx','gy'}, dimensions={0} | all-to-all | bytes 655360 | tf_op jit(solution)/shard_map/all_to_all | solution.py:419
  60.2 0.0 copy-done
  60.2 2.3 %shard_map.135 = (f32[64,128]{1,0:T(8,128)S(1)}, f32[640,128]{1,0:T(8,128)S(1)}) custom-call(f32[640,128]{1,0:T(8,128)S(1)} %bitcast.29, f32[64,128]{1,0:T(8,128)S(1)} %get-tuple-element.38.t_ref, bf16[64,256,128]{2,1,0:T(8,128)(2,1)S(1)} %copy-done, f32[64,128]{1,0:T(8,128)S(1)} %get-tuple-element.58.rinv_ref, f32[64,128]{1,0:T(8,128)S(1)} %get-tuple-element.59.mb_ref, ...), custom_call_target="tpu_custom_call" | custom-call | tf_op jit(solution)/shard_map/pallas_call | solution.py:406
  62.5 16.0 %all_to_all.27 = f32[128,1,640]{2,1,0:T(1,128)S(1)} all-to-all(f32[128,1,640]{2,1,0:T(1,128)S(1)} %bitcast.31), channel_id=1, replica_groups=mesh['gx'=16,'gy'=8] {'gx','gy'}, dimensions={0} | all-to-all | bytes 655360 | tf_op jit(solution)/shard_map/all_to_all | solution.py:419
  78.5 1.3 %shard_map.136 = (f32[64,128]{1,0:T(8,128)S(1)}, f32[640,128]{1,0:T(8,128)S(1)}) custom-call(f32[640,128]{1,0:T(8,128)S(1)} %bitcast.30, f32[64,128]{1,0:T(8,128)S(1)} %get-tuple-element.65.state_ref, f32[8,128]{1,0:T(8,128)S(1)} %get-tuple-element.66.mass_ref, f32[64,128]{1,0:T(8,128)S(1)} %get-tuple-element.53.count_ref, ...), custom_call_target="tpu_custom_call" | custom-call | tf_op jit(solution)/shard_map/pallas_call | solution.py:406
  79.9 16.0 %all_to_all.28 = f32[128,1,640]{2,1,0:T(1,128)S(1)} all-to-all(f32[128,1,640]{2,1,0:T(1,128)S(1)} %bitcast.32), channel_id=1, replica_groups=mesh['gx'=16,'gy'=8] {'gx','gy'}, dimensions={0} | all-to-all | bytes 655360 | tf_op jit(solution)/shard_map/all_to_all | solution.py:419
  95.8 1.6 %shard_map.137 = (f32[64,128]{1,0:T(8,128)}, f32[64,128]{1,0:T(8,128)}) custom-call(f32[640,128]{1,0:T(8,128)S(1)} %bitcast.28, f32[64,128]{1,0:T(8,128)S(1)} %get-tuple-element.68.t_ref, bf16[64,256,128]{2,1,0:T(8,128)(2,1)S(1)} %copy-done, f32[64,128]{1,0:T(8,128)S(1)} %get-tuple-element.58.rinv_ref, s32[48,128]{1,0:T(8,128)S(1)} %get-tuple-element.60.lab_ref, ...), custom_call_target="tpu_custom_call" | custom-call | tf_op jit(solution)/shard_map/pallas_call | solution.py:406
Async XLA Ops:
  2.3 21.1 %all-to-all-start = ((f32[128,1,64]{2,1,0:T(1,128)}), f32[128,1,64]{2,1,0:T(1,128)S(1)}, u32[]{:S(2)}, u32[]{:S(2)}) async-start(f32[128,1,64]{2,1,0:T(1,128)} %bitcast.35), calls=%async_computation | async-start | bytes 131072 | tf_op jit(solution)/shard_map/all_to_all | solution.py:440
  23.4 36.8 %copy-start = (bf16[64,256,128]{2,1,0:T(8,128)(2,1)S(1)}, bf16[64,256,128]{2,1,0:T(8,128)(2,1)}, u32[]{:S(2)}) copy-start(bf16[64,256,128]{2,1,0:T(8,128)(2,1)} %get-tuple-element.57.e_ref) | copy-start | bytes 12582916
